TPU v7x, 32 devices: a whole 2x2x4 slice. The times are simulated.
32 devices in a mesh: rows: 4 (over x, core), tp: 8 (over z, y).
Axes of the slice: x: 2, y: 2, z: 4, core: 2. Of those that a mesh axis runs over, the one named last changes fastest.
Arguments:
- tokens: bfloat16 [8192, 1024], P('rows'), may hold values from -6 to 6
- time_embed: bfloat16 [8, 1024], P('rows'), may hold values from -3 to 3
- segment_ids: int32 [8, 1024], P('rows'), may hold values from 0 to 5, never falling along the last dimension, each value on 1 to 512 neighbouring positions
- cotangent: bfloat16 [8192, 1024], P('rows'), may hold values from -6 to 6
- input_weight: float32 [1024, 3072], P('rows', 'tp'), may hold values from -0.1875 to 0.1875
- input_moment: float32 [1024, 3072], P('rows', 'tp'), may hold values from -0.00018310547 to 0.00018310547
- input_square: float32 [1024, 3072], P('rows', 'tp'), may hold values from 1.9888103e-11 to 1.2728386e-09
- output_weight: float32 [1024, 1024], P('rows', 'tp'), may hold values from -1 to 1
- output_moment: float32 [1024, 1024], P('rows', 'tp'), may hold values from -0.00018310547 to 0.00018310547
- output_square: float32 [1024, 1024], P('rows', 'tp'), may hold values from 1.9888103e-11 to 1.2728386e-09
- upward_weight: float32 [1024, 4096], P('rows', 'tp'), may hold values from -0.1875 to 0.1875
- upward_moment: float32 [1024, 4096], P('rows', 'tp'), may hold values from -0.00018310547 to 0.00018310547
- upward_square: float32 [1024, 4096], P('rows', 'tp'), may hold values from 1.9888103e-11 to 1.2728386e-09
- downward_weight: float32 [1024, 4096], P('rows', 'tp'), may hold values from -0.09375 to 0.09375
- downward_moment: float32 [1024, 4096], P('rows', 'tp'), may hold values from -0.00018310547 to 0.00018310547
- downward_square: float32 [1024, 4096], P('rows', 'tp'), may hold values from 1.9888103e-11 to 1.2728386e-09
- head_bias: float32 [128, 16], P('rows', 'tp'), may hold values from -1.75 to 1.75
- head_moment: float32 [128, 16], P('rows', 'tp'), may hold values from -0.00018310547 to 0.00018310547
- head_square: float32 [128, 16], P('rows', 'tp'), may hold values from 1.9888103e-11 to 1.2728386e-09
- hidden_bias: float32 [128, 32], P('rows', 'tp'), may hold values from -1.75 to 1.75
- hidden_moment: float32 [128, 32], P('rows', 'tp'), may hold values from -0.00018310547 to 0.00018310547
- hidden_square: float32 [128, 32], P('rows', 'tp'), may hold values from 1.9888103e-11 to 1.2728386e-09
- norm_gains: float32 [1024, 2], P('rows'), may hold values from 0.5 to 1.5
- gains_moment: float32 [1024, 2], P('rows'), may hold values from -0.00018310547 to 0.00018310547
- gains_square: float32 [1024, 2], P('rows'), may hold values from 1.9888103e-11 to 1.2728386e-09
- branch_biases: float32 [1024, 4], P('rows'), may hold values from -1.75 to 1.75
- biases_moment: float32 [1024, 4], P('rows'), may hold values from -0.00018310547 to 0.00018310547
- biases_square: float32 [1024, 4], P('rows'), may hold values from 1.9888103e-11 to 1.2728386e-09
Outputs:
- block_output: bfloat16 [8192, 1024], P('rows')
- input_grad: float32 [8192, 1024], P('rows')
- grad_norm: float32 [1], replicated
- input_weight_new: float32 [1024, 3072], P('rows', 'tp')
- input_moment_new: float32 [1024, 3072], P('rows', 'tp')
- input_square_new: float32 [1024, 3072], P('rows', 'tp')
- output_weight_new: float32 [1024, 1024], P('rows', 'tp')
- output_moment_new: float32 [1024, 1024], P('rows', 'tp')
- output_square_new: float32 [1024, 1024], P('rows', 'tp')
- upward_weight_new: float32 [1024, 4096], P('rows', 'tp')
- upward_moment_new: float32 [1024, 4096], P('rows', 'tp')
- upward_square_new: float32 [1024, 4096], P('rows', 'tp')
- downward_weight_new: float32 [1024, 4096], P('rows', 'tp')
- downward_moment_new: float32 [1024, 4096], P('rows', 'tp')
- downward_square_new: float32 [1024, 4096], P('rows', 'tp')
- head_bias_new: float32 [128, 16], P('rows', 'tp')
- head_moment_new: float32 [128, 16], P('rows', 'tp')
- head_square_new: float32 [128, 16], P('rows', 'tp')
- hidden_bias_new: float32 [128, 32], P('rows', 'tp')
- hidden_moment_new: float32 [128, 32], P('rows', 'tp')
- hidden_square_new: float32 [128, 32], P('rows', 'tp')
- norm_gains_new: float32 [1024, 2], P('rows')
- gains_moment_new: float32 [1024, 2], P('rows')
- gains_square_new: float32 [1024, 2], P('rows')
- branch_biases_new: float32 [1024, 4], P('rows')
- biases_moment_new: float32 [1024, 4], P('rows')
- biases_square_new: float32 [1024, 4], P('rows')
Inputs may be any that keep to these rules, and one draw needn't show every extreme that they name: `segment_ids`: in each sequence the numbers never fall, and each document holds at most 512 tokens.
All inputs are finite; a program needn't handle non-finite values.
Results may differ from a plain program's by a relative error of at most 0.01.
The roundings to bfloat16 on the way count: a program that leaves them out, or rounds other values in their place, can miss the bound.
Values may be sent and summed in bfloat16 or wider, within the bound.
A program may use at most 192 MiB of HBM per device.

v0:
```python
from functools import reduce

import jax
import jax.numpy as jnp
from jax import lax
from jax.sharding import PartitionSpec as P

HD = 64
STEP = 10


NORM_EPS = 1e-05
BETA_ONE = 0.9
BETA_TWO = 0.999
ADAM_EPS = 1e-08
CLIP = 1.0
RATES = (0.1, 0.4, 0.1, 0.05, 0.5, 0.5, 0.5, 0.5)
DECAYS = (0.01, 0.01, 0.01, 0.01, 0.0, 0.0, 0.0, 0.0)
ROW_PAIR = (((1,), (1,)), ((), ()))
COL_PAIR = (((0,), (0,)), ((), ()))


def norm_stats(summed):
    average = jnp.mean(summed, axis=-1, keepdims=True)
    centered = summed - average
    inverse = lax.rsqrt(jnp.mean(centered * centered, axis=-1, keepdims=True) + NORM_EPS)
    return (centered * inverse, inverse)


def norm_back(grad_normed, normed, inverse):
    first_mean = jnp.mean(grad_normed, axis=-1, keepdims=True)
    second_mean = jnp.mean(grad_normed * normed, axis=-1, keepdims=True)
    return inverse * (grad_normed - first_mean - normed * second_mean)


def gelu_value(inputs):
    return 0.5 * inputs * (1.0 + jax.scipy.special.erf(inputs * 0.7071067811865476))


def gelu_slope(inputs):
    cumulative = 0.5 * (1.0 + jax.scipy.special.erf(inputs * 0.7071067811865476))
    return cumulative + inputs * jnp.exp(-0.5 * inputs * inputs) * 0.3989422804014327


def masked_scores(queries, key_rows, segments):
    scores = jnp.einsum(
        "qhd,khd->hqk", queries, key_rows, preferred_element_type=jnp.float32
    ) * HD ** (-0.5)
    matching = segments[:, None] == segments[None, :]
    return jnp.where(matching[None], scores, -1e30)


def attend_forward(pieces):
    queries, key_rows, values, segments = pieces
    scores = masked_scores(queries, key_rows, segments)
    highest = jnp.max(scores, axis=-1, keepdims=True)
    exponent = jnp.exp(scores - highest)
    totals = jnp.sum(exponent, axis=-1, keepdims=True)
    probability = (exponent / totals).astype(jnp.bfloat16)
    context = jnp.einsum("hqk,khd->qhd", probability, values, preferred_element_type=jnp.float32)
    return (context, (highest + jnp.log(totals))[..., 0])


def attend_back(pieces):
    queries, key_rows, values, segments, log_total, grad_context = pieces
    scores = masked_scores(queries, key_rows, segments)
    probability = jnp.exp(scores - log_total[..., None])
    grad_prob = jnp.einsum("qhd,khd->hqk", grad_context, values, preferred_element_type=jnp.float32)
    weighted = jnp.sum(probability * grad_prob, axis=-1, keepdims=True)
    grad_score = (probability * (grad_prob - weighted)).astype(jnp.bfloat16)
    grad_query = jnp.einsum(
        "hqk,khd->qhd", grad_score, key_rows, preferred_element_type=jnp.float32
    ) * HD ** (-0.5)
    grad_key = jnp.einsum(
        "hqk,qhd->khd", grad_score, queries, preferred_element_type=jnp.float32
    ) * HD ** (-0.5)
    grad_value = jnp.einsum(
        "hqk,qhd->khd",
        probability.astype(jnp.bfloat16),
        grad_context,
        preferred_element_type=jnp.float32,
    )
    return jnp.stack([grad_query, grad_key, grad_value], axis=2)


def adam_update(weight, moment, square, clipped, rate, decay):
    moment = BETA_ONE * moment + (1.0 - BETA_ONE) * clipped
    square = BETA_TWO * square + (1.0 - BETA_TWO) * clipped * clipped
    corrected = (
        moment / (1.0 - BETA_ONE**STEP) / (jnp.sqrt(square / (1.0 - BETA_TWO**STEP)) + ADAM_EPS)
    )
    return (weight - rate * (corrected + decay * weight), moment, square)


def add_squares(running, member):
    return running + jnp.sum(member * member)


def on_device(
    tokens,
    time_embed,
    segment_ids,
    cotangent,
    input_weight,
    input_moment,
    input_square,
    output_weight,
    output_moment,
    output_square,
    upward_weight,
    upward_moment,
    upward_square,
    downward_weight,
    downward_moment,
    downward_square,
    head_bias,
    head_moment,
    head_square,
    hidden_bias,
    hidden_moment,
    hidden_square,
    norm_gains,
    gains_moment,
    gains_square,
    branch_biases,
    biases_moment,
    biases_square,
):
    masters = (
        input_weight,
        output_weight,
        upward_weight,
        downward_weight,
        head_bias,
        hidden_bias,
        norm_gains,
        branch_biases,
    )
    moments = (
        input_moment,
        output_moment,
        upward_moment,
        downward_moment,
        head_moment,
        hidden_moment,
        gains_moment,
        biases_moment,
    )
    squares = (
        input_square,
        output_square,
        upward_square,
        downward_square,
        head_square,
        hidden_square,
        gains_square,
        biases_square,
    )
    (
        weights_in,
        weights_out,
        weights_up,
        weights_down,
        head_shift,
        unit_shift,
        gains_low,
        shifts_low,
    ) = (
        lax.all_gather(input_weight.astype(jnp.bfloat16), "rows", axis=0, tiled=True),
        lax.all_gather(output_weight.astype(jnp.bfloat16), "rows", axis=0, tiled=True),
        lax.all_gather(upward_weight.astype(jnp.bfloat16), "rows", axis=0, tiled=True),
        lax.all_gather(downward_weight.astype(jnp.bfloat16), "rows", axis=0, tiled=True),
        lax.all_gather(head_bias.astype(jnp.bfloat16), "rows", axis=0, tiled=True),
        lax.all_gather(hidden_bias.astype(jnp.bfloat16), "rows", axis=0, tiled=True),
        lax.all_gather(norm_gains.astype(jnp.bfloat16), "rows", axis=0, tiled=True),
        lax.all_gather(branch_biases.astype(jnp.bfloat16), "rows", axis=0, tiled=True),
    )
    seq_count, length = segment_ids.shape
    width = tokens.shape[1]
    num_heads = head_shift.shape[1]
    head_size = head_shift.shape[0] // 2
    tok_rows = seq_count * length
    gains = gains_low.astype(jnp.float32)
    shifts = shifts_low.astype(jnp.float32)
    embedded = (
        tokens.astype(jnp.float32).reshape(seq_count, length, width)
        + time_embed.astype(jnp.float32)[:, None, :]
    ).reshape(tok_rows, width)
    embedded_low = embedded.astype(jnp.bfloat16)
    head_float = head_shift.astype(jnp.float32)
    offset = jnp.stack(
        [
            head_float[:head_size].T,
            jnp.zeros((num_heads, head_size), jnp.float32),
            head_float[head_size:].T,
        ],
        axis=1,
    )
    projected = jnp.dot(embedded_low, weights_in, preferred_element_type=jnp.float32).reshape(
        tok_rows, num_heads, 3, head_size
    )
    projected = (
        (projected + offset)
        .astype(jnp.bfloat16)
        .reshape(seq_count, length, num_heads, 3, head_size)
    )
    queries = projected[:, :, :, 0]
    key_rows = projected[:, :, :, 1]
    values = projected[:, :, :, 2]
    context, log_total = lax.map(attend_forward, (queries, key_rows, values, segment_ids))
    context_low = context.reshape(tok_rows, num_heads * head_size).astype(jnp.bfloat16)
    mixed_part = lax.dot_general(
        context_low, weights_out, ROW_PAIR, preferred_element_type=jnp.float32
    )
    mixed = lax.psum(mixed_part, "tp")
    normed_one, inverse_one = norm_stats(embedded + mixed + shifts[:, 0])
    hidden = normed_one * gains[:, 0] + shifts[:, 1]
    hidden_low = hidden.astype(jnp.bfloat16)
    unit_offset = unit_shift.astype(jnp.float32).T.reshape(-1)
    pre_act = jnp.dot(hidden_low, weights_up, preferred_element_type=jnp.float32) + unit_offset
    expanded_low = gelu_value(pre_act).astype(jnp.bfloat16)
    reduced_part = lax.dot_general(
        expanded_low, weights_down, ROW_PAIR, preferred_element_type=jnp.float32
    )
    reduced = lax.psum(reduced_part, "tp")
    normed_two, inverse_two = norm_stats(hidden + reduced + shifts[:, 2])
    block_output = (normed_two * gains[:, 1] + shifts[:, 3]).astype(jnp.bfloat16)
    upstream = cotangent.astype(jnp.float32)
    gain_two = jnp.sum(upstream * normed_two, axis=0)
    shift_three = jnp.sum(upstream, axis=0)
    grad_pre_two = norm_back(upstream * gains[:, 1], normed_two, inverse_two)
    shift_two = jnp.sum(grad_pre_two, axis=0)
    grad_pre_two_low = grad_pre_two.astype(jnp.bfloat16)
    grad_down = lax.dot_general(
        grad_pre_two_low, expanded_low, COL_PAIR, preferred_element_type=jnp.float32
    )
    grad_act = jnp.dot(grad_pre_two_low, weights_down, preferred_element_type=jnp.float32)
    grad_pre_act = (grad_act * gelu_slope(pre_act)).astype(jnp.bfloat16)
    unit_sums = jnp.sum(grad_pre_act, axis=0, dtype=jnp.float32)
    grad_unit = unit_sums.reshape(-1, 2 * head_size).T
    grad_up = lax.dot_general(
        hidden_low, grad_pre_act, COL_PAIR, preferred_element_type=jnp.float32
    )
    back_part = lax.dot_general(
        grad_pre_act, weights_up, ROW_PAIR, preferred_element_type=jnp.float32
    )
    grad_hidden = lax.psum(back_part, "tp") + grad_pre_two
    gain_one = jnp.sum(grad_hidden * normed_one, axis=0)
    shift_one = jnp.sum(grad_hidden, axis=0)
    grad_pre_one = norm_back(grad_hidden * gains[:, 0], normed_one, inverse_one)
    shift_zero = jnp.sum(grad_pre_one, axis=0)
    grad_pre_one_low = grad_pre_one.astype(jnp.bfloat16)
    grad_out = lax.dot_general(
        grad_pre_one_low, context_low, COL_PAIR, preferred_element_type=jnp.float32
    )
    grad_context = jnp.dot(
        grad_pre_one_low, weights_out, preferred_element_type=jnp.float32
    ).astype(jnp.bfloat16)
    grad_context = grad_context.reshape(seq_count, length, num_heads, head_size)
    grad_projected = lax.map(
        attend_back, (queries, key_rows, values, segment_ids, log_total, grad_context)
    )
    grad_projected = grad_projected.reshape(tok_rows, num_heads * 3 * head_size).astype(
        jnp.bfloat16
    )
    head_sums = jnp.sum(grad_projected, axis=0, dtype=jnp.float32).reshape(num_heads, 3, head_size)
    grad_head = jnp.concatenate([head_sums[:, 0].T, head_sums[:, 2].T], axis=0)
    grad_in = lax.dot_general(
        embedded_low, grad_projected, COL_PAIR, preferred_element_type=jnp.float32
    )
    input_part = lax.dot_general(
        grad_projected, weights_in, ROW_PAIR, preferred_element_type=jnp.float32
    )
    input_grad = lax.psum(input_part, "tp") + grad_pre_one
    grad_gains = jnp.stack([gain_one, gain_two], axis=1)
    grad_shifts = jnp.stack([shift_zero, shift_one, shift_two, shift_three], axis=1)
    sent_in, sent_out, sent_up, sent_down, sent_head, sent_unit, sent_gains, sent_shifts = (
        lax.psum_scatter(grad_in, "rows", scatter_dimension=0, tiled=True),
        lax.psum_scatter(grad_out, "rows", scatter_dimension=0, tiled=True),
        lax.psum_scatter(grad_up, "rows", scatter_dimension=0, tiled=True),
        lax.psum_scatter(grad_down, "rows", scatter_dimension=0, tiled=True),
        lax.psum_scatter(grad_head, "rows", scatter_dimension=0, tiled=True),
        lax.psum_scatter(grad_unit, "rows", scatter_dimension=0, tiled=True),
        lax.psum_scatter(grad_gains, "rows", scatter_dimension=0, tiled=True),
        lax.psum_scatter(grad_shifts, "rows", scatter_dimension=0, tiled=True),
    )
    gradients = (
        sent_in,
        sent_out,
        sent_up,
        sent_down,
        sent_head,
        sent_unit,
        sent_gains,
        sent_shifts,
    )
    split_part = reduce(
        add_squares,
        (sent_in, sent_out, sent_up, sent_down, sent_head, sent_unit),
        jnp.zeros((), jnp.float32),
    )
    copied_part = (
        jnp.sum(sent_gains * sent_gains) + jnp.sum(sent_shifts * sent_shifts)
    ) / lax.axis_size("tp")
    grad_norm = jnp.sqrt(lax.psum(split_part + copied_part, ("rows", "tp")))
    factor = CLIP / jnp.maximum(grad_norm, CLIP)
    updated = [
        adam_update(
            masters[position],
            moments[position],
            squares[position],
            gradients[position] * factor,
            RATES[position],
            DECAYS[position],
        )
        for position in range(8)
    ]
    return (
        block_output,
        input_grad,
        grad_norm.reshape(1),
        updated[0][0],
        updated[0][1],
        updated[0][2],
        updated[1][0],
        updated[1][1],
        updated[1][2],
        updated[2][0],
        updated[2][1],
        updated[2][2],
        updated[3][0],
        updated[3][1],
        updated[3][2],
        updated[4][0],
        updated[4][1],
        updated[4][2],
        updated[5][0],
        updated[5][1],
        updated[5][2],
        updated[6][0],
        updated[6][1],
        updated[6][2],
        updated[7][0],
        updated[7][1],
        updated[7][2],
    )


def solution(mesh):
    in_specs = (
        P("rows", None),
        P("rows", None),
        P("rows", None),
        P("rows", None),
        P("rows", "tp"),
        P("rows", "tp"),
        P("rows", "tp"),
        P("rows", "tp"),
        P("rows", "tp"),
        P("rows", "tp"),
        P("rows", "tp"),
        P("rows", "tp"),
        P("rows", "tp"),
        P("rows", "tp"),
        P("rows", "tp"),
        P("rows", "tp"),
        P("rows", "tp"),
        P("rows", "tp"),
        P("rows", "tp"),
        P("rows", "tp"),
        P("rows", "tp"),
        P("rows", "tp"),
        P("rows", None),
        P("rows", None),
        P("rows", None),
        P("rows", None),
        P("rows", None),
        P("rows", None),
    )
    out_specs = (
        P("rows", None),
        P("rows", None),
        P(),
        P("rows", "tp"),
        P("rows", "tp"),
        P("rows", "tp"),
        P("rows", "tp"),
        P("rows", "tp"),
        P("rows", "tp"),
        P("rows", "tp"),
        P("rows", "tp"),
        P("rows", "tp"),
        P("rows", "tp"),
        P("rows", "tp"),
        P("rows", "tp"),
        P("rows", "tp"),
        P("rows", "tp"),
        P("rows", "tp"),
        P("rows", "tp"),
        P("rows", "tp"),
        P("rows", "tp"),
        P("rows", None),
        P("rows", None),
        P("rows", None),
        P("rows", None),
        P("rows", None),
        P("rows", None),
    )
    return jax.shard_map(
        on_device, mesh=mesh, in_specs=in_specs, out_specs=out_specs, check_vma=False
    )
```

profile of v0, /device:TPU:1, one launch (start us, length us, event | category | flops | bytes accessed | tf_op | source)
XLA Modules:
  0.0 1300.6 jit_solution(2111556763713260341)
XLA Ops:
  8.8 5.8 all-gather
  16.6 6.3 all_gather.26
  23.9 8.7 all_gather.24
  32.9 3.3 fusion.56
  36.2 2.0 copy-done.10
  38.2 3.0 add_convert_fusion.1
  41.2 2.9 reshape.215
  45.6 14.9 %while.22 = (s32[]{:T(128)}, bf16[2,1024,2,64]{1,3,2,0:T(8,128)(2,1)S(1)}, f32[2,2,1024]{2,1,0:T(2,128)S(1)}, bf16[2,1024,2,64]{1,3,2,0:T(8,128)(2,1)S(1)}, s32[...) while((s32[]{:T(128)}, ...), condition=%wide.region_3.4_spmd, body=%wide.region_0.3_spmd.sunk | while | flops 563083264 | bytes 30750820 | solution.py:210
  46.3 1.9 fusion.144
  48.2 2.0 fusion.145
  50.2 2.8 fusion.146
  53.7 1.9 fusion.144
  55.6 2.0 fusion.145
  57.6 2.8 fusion.146
  62.0 4.7 fusion.99
  68.9 5.1 all_gather.28
  73.9 5.1 all-gather.1
  79.1 5.4 all_gather.27
  84.5 253.0 %all-reduce.5.cloned.1.call-done = f32[2048,1024]{1,0:T(8,128)} async-done(((f32[2048,1024]{1,0:T(8,128)}), f32[2048,1024]{1,0:T(8,128)}) %all-reduce.5.cloned.1.call-update) | async-done | bytes 8388624 | tf_op jit(solution)/shard_map/psum | solution.py:215
  337.5 6.1 fusion.94
  344.7 2.1 copy-done
  346.8 2.8 fusion.57
  349.5 8.0 multiply_convert_fusion.1
  357.5 7.6 fusion.100
  365.4 269.0 %all-reduce.7.cloned.1.call-done = f32[2048,1024]{1,0:T(8,128)} async-done(((f32[2048,1024]{1,0:T(8,128)}), f32[2048,1024]{1,0:T(8,128)}) %all-reduce.7.cloned.1.call-update) | async-done | bytes 8388624 | tf_op jit(solution)/shard_map/psum | solution.py:225
  634.4 7.2 fusion.93
  643.8 4.3 fusion.55
  648.1 4.7 fusion.91
  652.8 4.0 convert_reduce_fusion.1
  658.1 5.9 fusion.101
  664.9 7.7 fusion.71
  672.7 6.6 fusion.104
  679.4 253.9 %all-reduce.9.cloned.1.call-done = f32[2048,1024]{1,0:T(8,128)} async-done(((f32[2048,1024]{1,0:T(8,128)}), f32[2048,1024]{1,0:T(8,128)}) %all-reduce.9.cloned.1.call-update) | async-done | bytes 8388624 | tf_op jit(solution)/shard_map/psum | solution.py:247
  933.3 10.8 multiply_reduce_fusion.1
  944.1 5.4 fusion.90
  949.5 3.2 copy-done.1
  955.2 27.6 %while.23 = (s32[]{:T(128)}, bf16[2,1024,2,3,64]{1,4,2,3,0:T(8,128)(2,1)}, bf16[2,1024,2,64]{1,3,2,0:T(8,128)(2,1)S(1)}, s32[2,1024]{1,0:T(2,128)S(1)}, bf16[2,1...) while((s32[]{:T(128)}, ...), condition=%wide.region_17.18_spmd, body=%wide.region_15.17_spmd.sunk | while | flops 1377564672 | bytes 83957928 | solution.py:260
  957.4 2.5 fusion.156
  959.9 3.0 multiply_reduce_fusion.15
  962.9 2.7 multiply_convert_fusion.3
  966.5 1.4 fusion.157
  971.1 2.5 fusion.156
  973.6 3.0 multiply_reduce_fusion.15
  976.6 2.7 multiply_convert_fusion.3
  982.8 1.7 convert_reduce_fusion.2
  987.7 5.5 fusion.68
  993.7 3.0 copy.98
  997.2 5.8 fusion.103
  1003.0 5.8 fusion.102
  1010.5 1.8 multiply_reduce_fusion.6
  1012.3 1.9 multiply_reduce_fusion.7
  1015.6 13.1 %reduce-scatter.29.cloned.1.call-done = f32[256,2]{1,0:T(8,128)} async-done(((f32[1024,2]{1,0:T(8,128)}), f32[256,2]{1,0:T(8,128)}) %reduce-scatter.29.cloned.1.call-update) | async-done | bytes 2064
  1030.2 23.0 %reduce-scatter.31.cloned.1.call-done = f32[256,4]{1,0:T(8,128)} async-done(((f32[1024,4]{1,0:T(8,128)}), f32[256,4]{1,0:T(8,128)}) %reduce-scatter.31.cloned.1.call-update) | async-done | bytes 4112
  1056.1 21.7 %reduce-scatter.19.cloned.1.call-done = f32[256,128]{1,0:T(8,128)} async-done(((f32[1024,128]{1,0:T(8,128)}), f32[256,128]{1,0:T(8,128)}) %reduce-scatter.19.cloned.1.call-update) | async-done | bytes 131088 | tf_op jit(solution)/shard_map/reduce_scatter | solution.py:279
  1077.8 1.5 multiply_reduce_fusion.9
  1079.3 29.0 %reduce-scatter.17.cloned.1.call-done = f32[256,384]{1,0:T(8,128)} async-done(((f32[1024,384]{1,0:T(8,128)}), f32[256,384]{1,0:T(8,128)}) %reduce-scatter.17.cloned.1.call-update) | async-done | bytes 393232 | tf_op jit(solution)/shard_map/reduce_scatter | solution.py:278
  1108.3 1.7 multiply_reduce_fusion.8
  1113.9 41.2 %psum.39 = f32[]{:T(128)} all-reduce(f32[]{:T(128)S(6)} %add.324), channel_id=1, replica_groups=mesh['rows'=4,'tp'=8] {'rows','tp'}, use_global_device_ids=true, to_apply=%region_43.44 | all-reduce | flops 1 | bytes 8 | tf_op jit(solution)/shard_map/psum | solution.py:305
  1161.1 1.8 multiply_subtract_fusion.3
  1163.0 2.3 multiply_subtract_fusion.2
  1165.3 2.5 multiply_subtract_fusion
  1167.8 2.6 multiply_subtract_fusion.1
  1170.4 109.7 %all-reduce.11.cloned.1.call-done = f32[2048,1024]{1,0:T(8,128)} async-done(((f32[2048,1024]{1,0:T(8,128)}), f32[2048,1024]{1,0:T(8,128)}) %all-reduce.11.cloned.1.call-update) | async-done | bytes 8388624 | tf_op jit(solution)/shard_map/psum | solution.py:274
  1280.0 12.1 add.317
  (184 shorter events, 43.9 us)
Async XLA Ops:
  8.0 329.4 %all-reduce.5.cloned.1.call-start = ((), (), s32[]{:S(2)}) async-start(), calls=%async_computation.8 | async-start | bytes 16777216 | tf_op jit(solution)/shard_map/psum | solution.py:215
  32.6 8.6 copy-start.4
  36.2 2.0 copy-start.10
  41.2 4.4 copy-start.22
  61.1 0.8 copy-start.6
  61.9 4.8 copy-start.13
  61.9 6.1 copy-start.11
  66.6 2.2 copy-start.28
  66.6 2.2 copy-start.27
  66.6 2.2 copy-start.25
  66.7 282.9 %all-gather.5.cloned.1.call-start = ((), (), s32[]{:S(2)}) async-start(), calls=%async_computation.9 | async-start | bytes 1310720 | tf_op jit(solution)/shard_map/all_gather | solution.py:171
  67.5 290.1 %all-gather.7.cloned.1.call-start = ((), (), s32[]{:S(2)}) async-start(), calls=%async_computation.10 | async-start | bytes 1310720 | tf_op jit(solution)/shard_map/all_gather | solution.py:172
  68.8 565.7 %all-reduce.7.cloned.1.call-start = ((), (), s32[]{:S(2)}) async-start(), calls=%async_computation.11 | async-start | bytes 16777216 | tf_op jit(solution)/shard_map/psum | solution.py:225
  343.5 3.2 copy-start
  365.2 568.1 %all-reduce.9.cloned.1.call-start = ((), (), s32[]{:S(2)}) async-start(), calls=%async_computation.12 | async-start | bytes 16777216 | tf_op jit(solution)/shard_map/psum | solution.py:247
  641.6 2.2 copy-start.3
  648.1 4.7 copy-start.31
  648.1 4.7 copy-start.32
  652.8 4.1 copy-start.2
  652.8 5.4 copy-start.30
  656.8 1.3 copy-start.16
  664.1 344.9 %reduce-scatter.27.cloned.1.call-start = ((), (), s32[]{:S(2)}) async-start(), calls=%async_computation.19 | async-start | bytes 81920
  664.9 345.6 %reduce-scatter.23.cloned.1.call-start = ((), (), s32[]{:S(2)}) async-start(), calls=%async_computation.17 | async-start | bytes 2621440 | tf_op jit(solution)/shard_map/reduce_scatter | solution.py:281
  672.6 339.7 %reduce-scatter.21.cloned.1.call-start = ((), (), s32[]{:S(2)}) async-start(), calls=%async_computation.16 | async-start | bytes 2621440 | tf_op jit(solution)/shard_map/reduce_scatter | solution.py:280
  679.3 334.8 %reduce-scatter.25.cloned.1.call-start = ((), (), s32[]{:S(2)}) async-start(), calls=%async_computation.18 | async-start | bytes 81920
  949.5 3.2 copy-start.1
  955.2 30.3 %copy-start.23 = (f32[1024]{0:T(1024)S(1)}, f32[1024]{0:T(1024)}, u32[]{:S(2)}) copy-start(f32[1024]{0:T(1024)} %get-tuple-element.136) | copy-start | bytes 12292
  955.2 31.4 %copy-start.24 = (f32[1024]{0:T(1024)S(1)}, f32[1024]{0:T(1024)}, u32[]{:S(2)}) copy-start(f32[1024]{0:T(1024)} %get-tuple-element.141) | copy-start | bytes 12292
  955.2 32.5 %copy-start.7 = (bf16[16,8,2,1024]{3,1,2,0:T(8,128)(2,1)S(1)}, bf16[16,8,2,1024]{3,1,2,0:T(8,128)(2,1)}, u32[]{:S(2)}) copy-start(bf16[16,8,2,1024]{3,1,2,0:T(8,128)(2,1)} %copy-done.6) | copy-start | bytes 1572868
  965.6 2.3 copy-start.8
  968.0 1.1 copy-start.9
  979.3 2.3 copy-start.8
  981.7 1.1 copy-start.9
  985.4 43.2 %reduce-scatter.29.cloned.1.call-start = ((), (), s32[]{:S(2)}) async-start(), calls=%async_computation.20 | async-start | bytes 655360
  986.5 66.7 %reduce-scatter.31.cloned.1.call-start = ((), (), s32[]{:S(2)}) async-start(), calls=%async_computation.21 | async-start | bytes 655360
  987.7 90.1 %reduce-scatter.19.cloned.1.call-start = ((), (), s32[]{:S(2)}) async-start(), calls=%async_computation.15 | async-start | bytes 655360 | tf_op jit(solution)/shard_map/reduce_scatter | solution.py:279
  993.2 115.1 %reduce-scatter.17.cloned.1.call-start = ((), (), s32[]{:S(2)}) async-start(), calls=%async_computation.14 | async-start | bytes 1966080 | tf_op jit(solution)/shard_map/reduce_scatter | solution.py:278
  996.7 6.3 copy-start.5
  1003.0 277.1 %all-reduce.11.cloned.1.call-start = ((), (), s32[]{:S(2)}) async-start(), calls=%async_computation.13 | async-start | bytes 16777216 | tf_op jit(solution)/shard_map/psum | solution.py:274
  1008.8 151.0 %copy-start.26 = (f32[256,4]{0,1:T(4,128)S(1)}, f32[256,4]{0,1:T(4,128)}, u32[]{:S(2)}) copy-start(f32[256,4]{0,1:T(4,128)} %param.57) | copy-start | bytes 12292
  1008.8 152.3 %copy-start.18 = (f32[256,128]{1,0:T(8,128)S(1)}, f32[256,128]{1,0:T(8,128)}, u32[]{:S(2)}) copy-start(f32[256,128]{1,0:T(8,128)} %param.39) | copy-start | bytes 393220
  1008.8 154.1 %copy-start.17 = (f32[256,384]{1,0:T(8,128)S(1)}, f32[256,384]{1,0:T(8,128)}, u32[]{:S(2)}) copy-start(f32[256,384]{1,0:T(8,128)} %param.36) | copy-start | bytes 1179652
  1008.8 154.1 %copy-start.21 = (f32[256,384]{1,0:T(8,128)S(1)}, f32[256,384]{1,0:T(8,128)}, u32[]{:S(2)}) copy-start(f32[256,384]{1,0:T(8,128)} %param.37) | copy-start | bytes 1179652
  1008.8 156.4 %copy-start.12 = (f32[256,512]{1,0:T(8,128)S(1)}, f32[256,512]{1,0:T(8,128)}, u32[]{:S(2)}) copy-start(f32[256,512]{1,0:T(8,128)} %param.45) | copy-start | bytes 1572868
  1008.9 156.4 %copy-start.19 = (f32[256,512]{1,0:T(8,128)S(1)}, f32[256,512]{1,0:T(8,128)}, u32[]{:S(2)}) copy-start(f32[256,512]{1,0:T(8,128)} %param.46) | copy-start | bytes 1572868
  1008.9 156.4 %copy-start.20 = (f32[256,512]{1,0:T(8,128)S(1)}, f32[256,512]{1,0:T(8,128)}, u32[]{:S(2)}) copy-start(f32[256,512]{1,0:T(8,128)} %param.47) | copy-start | bytes 1572868
  1008.9 158.9 %copy-start.14 = (f32[256,512]{1,0:T(8,128)S(1)}, f32[256,512]{1,0:T(8,128)}, u32[]{:S(2)}) copy-start(f32[256,512]{1,0:T(8,128)} %param.42) | copy-start | bytes 1572868
  1012.3 155.5 %copy-start.15 = (f32[256,512]{1,0:T(8,128)S(1)}, f32[256,512]{1,0:T(8,128)}, u32[]{:S(2)}) copy-start(f32[256,512]{1,0:T(8,128)} %reduce-scatter.21.cloned.1.call-done) | copy-start | bytes 1572868
  1015.0 15.3 %copy-start.29 = (f32[32,2]{0,1:T(2,128)}, f32[32,2]{0,1:T(2,128)S(1)}, u32[]{:S(2)}) copy-start(f32[32,2]{0,1:T(2,128)S(1)} %copy.107) | copy-start | bytes 772
Sparse Core Ops, SparseCore 0:
  66.8 270.6 all-reduce.4
  365.3 269.0 all-reduce.6
  664.2 269.0 all-reduce.8
  1009.0 270.9 all-reduce.10
Sparse Core Ops, SparseCore 1:
  69.3 17.8 all-gather.4
  89.1 16.5 all-gather.6
  667.5 18.5 reduce-scatter.26
  688.6 31.2 reduce-scatter.22
  722.4 31.2 reduce-scatter.20
  985.5 18.2 reduce-scatter.24
  1006.7 21.9 reduce-scatter.28
  1031.6 21.6 reduce-scatter.30
  1056.1 21.6 reduce-scatter.18
  1080.3 27.9 reduce-scatter.16
where the time goes:
time: 1310 us; the launch traced here: 1300 us
  waiting for transfers between devices  973 us (74%)
  other arithmetic  102 us (8%)
  matrix products  93.4 us (7%)
  blocking collectives  77.5 us (6%)
  local copies, waits for them, and re-layouts  30.3 us (2%)
  between operations  23.2 us (2%)
    psum x1, waiting for transfers between devices, on_device(): reduced = lax.psum(reduced_part, 'tp')  269 us
    psum x1, waiting for transfers between devices, on_device(): grad_hidden = lax.psum(back_part, 'tp') + grad_pre_two  254 us
    psum x1, waiting for transfers between devices, on_device(): mixed = lax.psum(mixed_part, 'tp')  253 us
    psum x1, waiting for transfers between devices, on_device(): input_grad = lax.psum(input_part, 'tp') + grad_pre_one  110 us
    psum x1, blocking collectives, on_device(): grad_norm = jnp.sqrt(lax.psum(split_part + copied_part, ('rows', 'tp')))  41.2 us
    unnamed x18, waiting for transfers between devices  36.3 us
    reduce_scatter x1, waiting for transfers between devices, on_device(): lax.psum_scatter(grad_in, 'rows', scatter_dimension=0, tiled=True)  29 us
  transfers between devices with their start and end apart: 14, of which 8 were waited for; matrix products, arithmetic and copies ran while one was open for 10% of the time, Pallas kernels for 0%

commit v1 on v0

--- a/solution.py
+++ b/solution.py
@@ -1,8 +1,11 @@
-from functools import reduce
+from functools import partial, reduce
 
 import jax
 import jax.numpy as jnp
 from jax import lax
+from jax.experimental import pallas as pl
+from jax.experimental.pallas import tpu as pltpu
+from jax.sharding import Mesh
 from jax.sharding import PartitionSpec as P
 
 HD = 64
@@ -346,66 +349,479 @@
     )
 
 
+def flip(value, axis):
+    return lax.ppermute(value, axis, [(0, 1), (1, 0)])
+
+
+def turn(value, amount, count):
+    return lax.ppermute(value, "z", [(i, (i + amount) % count) for i in range(count)])
+
+
+def swap_halves(value, swapped):
+    half = value.shape[-1] // 2
+    return jnp.where(
+        swapped, jnp.concatenate([value[..., half:], value[..., :half]], axis=-1), value
+    )
+
+
+def in_order(first, mine, other):
+    return jnp.where(
+        first, jnp.concatenate([mine, other], axis=0), jnp.concatenate([other, mine], axis=0)
+    )
+
+
+def attend_kernel(length, head_size, block, emb_ref, weight_ref, bias_ref, col_ref, row_ref, proj_ref, ctx_ref):
+    width = 3 * head_size
+    proj = jnp.dot(emb_ref[...], weight_ref[0], preferred_element_type=jnp.float32)
+    proj_ref[0] = (proj[:, :width] + bias_ref[0, 0:1, :width]).astype(jnp.bfloat16)
+    keys = proj_ref[0, :, head_size : 2 * head_size]
+    values = proj_ref[0, :, 2 * head_size : width]
+
+    def one_block(at, carry):
+        rows = pl.ds(pl.multiple_of(at * block, block), block)
+        queries = proj_ref[0, rows, 0:head_size] * jnp.bfloat16(head_size**-0.5)
+        scores = lax.dot_general(queries, keys, ROW_PAIR, preferred_element_type=jnp.float32)
+        scores = jnp.where(col_ref[rows, :] == row_ref[...], scores, -1e30)
+        highest = jnp.max(scores, axis=1, keepdims=True)
+        exponent = jnp.exp(scores - highest)
+        totals = jnp.sum(exponent, axis=1, keepdims=True)
+        probability = (exponent * (1.0 / totals)).astype(jnp.bfloat16)
+        ctx = jnp.dot(probability, values, preferred_element_type=jnp.float32)
+        ctx_ref[0, rows, :] = ctx.astype(jnp.bfloat16)
+        return carry
+
+    lax.fori_loop(0, length // block, one_block, 0)
+
+
+def attend_back_kernel(length, head_size, block, proj_ref, grad_ref, col_ref, row_ref, out_ref, key_sum, value_sum):
+    width = 3 * head_size
+    keys = proj_ref[0, :, head_size : 2 * head_size]
+    values = proj_ref[0, :, 2 * head_size : width]
+    key_sum[...] = jnp.zeros_like(key_sum)
+    value_sum[...] = jnp.zeros_like(value_sum)
+    scale = head_size**-0.5
+
+    def one_block(at, carry):
+        rows = pl.ds(pl.multiple_of(at * block, block), block)
+        queries = proj_ref[0, rows, 0:head_size] * jnp.bfloat16(scale)
+        grads = grad_ref[0, rows, :]
+        scores = lax.dot_general(keys, queries, ROW_PAIR, preferred_element_type=jnp.float32)
+        scores = jnp.where(col_ref[...] == row_ref[0:1, rows], scores, -1e30)
+        highest = jnp.max(scores, axis=0, keepdims=True)
+        exponent = jnp.exp(scores - highest)
+        probability = exponent * (1.0 / jnp.sum(exponent, axis=0, keepdims=True))
+        grad_prob = lax.dot_general(values, grads, ROW_PAIR, preferred_element_type=jnp.float32)
+        weighted = jnp.sum(probability * grad_prob, axis=0, keepdims=True)
+        grad_score = (probability * (grad_prob - weighted)).astype(jnp.bfloat16)
+        value_sum[...] += jnp.dot(
+            probability.astype(jnp.bfloat16), grads, preferred_element_type=jnp.float32
+        )
+        key_sum[...] += jnp.dot(grad_score, queries, preferred_element_type=jnp.float32)
+        grad_query = lax.dot_general(grad_score, keys, COL_PAIR, preferred_element_type=jnp.float32)
+        out_ref[0, rows, 0:head_size] = (grad_query * scale).astype(jnp.bfloat16)
+        return carry
+
+    lax.fori_loop(0, length // block, one_block, 0)
+    out_ref[0, :, head_size : 2 * head_size] = key_sum[...].astype(jnp.bfloat16)
+    out_ref[0, :, 2 * head_size : width] = value_sum[...].astype(jnp.bfloat16)
+
+
+def attend_all(emb_low, weights, biases, segments, head_size):
+    heads, depth, packed = weights.shape
+    length = emb_low.shape[0]
+    whole = lambda shape: pl.BlockSpec(shape, lambda h: (0, 0))
+    each = lambda shape: pl.BlockSpec((1,) + shape, lambda h: (h, 0, 0))
+    return pl.pallas_call(
+        partial(attend_kernel, length, head_size, 256),
+        grid=(heads,),
+        in_specs=[
+            whole((length, depth)),
+            each((depth, packed)),
+            each((8, packed)),
+            whole((length, 1)),
+            whole((1, length)),
+        ],
+        out_specs=[each((length, 3 * head_size)), each((length, head_size))],
+        out_shape=[
+            jax.ShapeDtypeStruct((heads, length, 3 * head_size), jnp.bfloat16),
+            jax.ShapeDtypeStruct((heads, length, head_size), jnp.bfloat16),
+        ],
+        compiler_params=pltpu.CompilerParams(vmem_limit_bytes=48 << 20),
+        cost_estimate=pl.CostEstimate(
+            flops=2 * heads * length * (depth * packed + 2 * length * 128),
+            bytes_accessed=8 << 20,
+            transcendentals=heads * length * length,
+        ),
+        name="attend_all",
+    )(emb_low, weights, biases, segments[:, None], segments[None, :])
+
+
+def attend_all_back(proj, grad_ctx, segments, head_size):
+    heads, length, width = proj.shape
+    whole = lambda shape: pl.BlockSpec(shape, lambda h: (0, 0))
+    each = lambda shape: pl.BlockSpec((1,) + shape, lambda h: (h, 0, 0))
+    return pl.pallas_call(
+        partial(attend_back_kernel, length, head_size, 256),
+        grid=(heads,),
+        in_specs=[
+            each((length, width)),
+            each((length, head_size)),
+            whole((length, 1)),
+            whole((1, length)),
+        ],
+        out_specs=each((length, width)),
+        out_shape=jax.ShapeDtypeStruct((heads, length, width), jnp.bfloat16),
+        scratch_shapes=[
+            pltpu.VMEM((length, head_size), jnp.float32),
+            pltpu.VMEM((length, head_size), jnp.float32),
+        ],
+        compiler_params=pltpu.CompilerParams(vmem_limit_bytes=48 << 20),
+        cost_estimate=pl.CostEstimate(
+            flops=2 * heads * length * length * 128 * 5,
+            bytes_accessed=8 << 20,
+            transcendentals=heads * length * length,
+        ),
+        name="attend_all_back",
+    )(proj, grad_ctx, segments[:, None], segments[None, :])
+
+
+def spread_tokens(own):
+    near = flip(own, "y")
+    pair = jnp.concatenate([own, near], axis=0)
+    return jnp.concatenate([pair, flip(pair, "core")], axis=0)
+
+
+def sum_tokens(left, right, pairing):
+    half = left.shape[0] // 2
+    far = lax.dot_general(left[half:], right, pairing, preferred_element_type=jnp.float32)
+    came = flip(far.astype(jnp.bfloat16), "core")
+    near = lax.dot_general(left[:half], right, pairing, preferred_element_type=jnp.float32)
+    near = near + came.astype(jnp.float32)
+    quarter = half // 2
+    return near[:quarter] + flip(near[quarter:].astype(jnp.bfloat16), "y").astype(jnp.float32)
+
+
+def spread_output(own, zs, dtype):
+    count = 4
+    at_z, at_y = lax.axis_index("z"), lax.axis_index("y")
+    quarter, width = own.shape
+    result = jnp.zeros((2 * count * quarter, width), dtype)
+    for step in range(count):
+        pairs = []
+        for core in range(2):
+            for place in range(count):
+                index = core * 2 + place % 2
+                target = (place // 2) * count + (index + step) % count
+                pairs.append((core * count + place, target))
+        came = lax.ppermute(own, ("core", "z"), pairs)
+        crossed = flip(came, "y")
+        index = (at_z - step) % count
+        start = (index % 2) * count + (index // 2) * 2
+        result = lax.dynamic_update_slice(
+            result, came.astype(dtype), ((start + at_y) * quarter, 0)
+        )
+        result = lax.dynamic_update_slice(
+            result, crossed.astype(dtype), ((start + 1 - at_y) * quarter, 0)
+        )
+    return result
+
+
+def sum_scalar(value):
+    value = jnp.broadcast_to(value, (8, 128))
+    for axis in ("core", "y", "x"):
+        value = value + flip(value, axis)
+    value = value + lax.ppermute(value, "z", [(0, 1), (1, 0), (2, 3), (3, 2)])
+    value = value + lax.ppermute(value, "z", [(0, 3), (3, 0), (1, 2), (2, 1)])
+    return value[0, 0]
+
+
+def on_grid(*arguments):
+    tokens, time_embed, segment_ids, cotangent = arguments[:4]
+    masters, moments, squares = arguments[4::3], arguments[5::3], arguments[6::3]
+    input_weight, output_weight, upward_weight, downward_weight = masters[:4]
+    head_bias, hidden_bias, norm_gains, branch_biases = masters[4:]
+    at_x, at_core = lax.axis_index("x"), lax.axis_index("core")
+    at_z, at_y = lax.axis_index("z"), lax.axis_index("y")
+    first_core, first_x = at_core == 0, at_x == 0
+    swapped = at_x == 1
+    low = jnp.bfloat16
+    f32 = jnp.float32
+    length = segment_ids.shape[1]
+    head_size = head_bias.shape[0] * 4 // 2
+    zs = 4
+    place = at_core * 2 + at_y
+    quarter = length // 4
+
+    rows = input_weight.shape[0]
+    wide = upward_weight.shape[1] // 2
+    packed = 4 * head_size
+    small_rows = head_bias.shape[0]
+
+    def head_piece(half):
+        body = jnp.concatenate(
+            [
+                input_weight[:, half * 3 * head_size : (half + 1) * 3 * head_size],
+                output_weight[:, half * head_size : (half + 1) * head_size],
+            ],
+            axis=1,
+        )
+        shifts = jnp.concatenate(
+            [head_bias[:, half : half + 1], hidden_bias[:, 2 * half : 2 * half + 2]], axis=1
+        ).T
+        shifts = jnp.pad(shifts, ((0, 0), (0, packed - small_rows)))
+        vectors = jnp.concatenate([norm_gains, branch_biases], axis=1).T
+        vectors = jnp.pad(vectors, ((0, 7), (0, packed - rows)))
+        return jnp.concatenate([body, shifts, vectors], axis=0).astype(low)
+
+    def column_piece(weight):
+        return lambda half: weight[:, half * wide : (half + 1) * wide].astype(low)
+
+    def pair_cores(piece):
+        zero, one = piece(0), piece(1)
+        mine = jnp.where(first_core, zero, one)
+        other = flip(jnp.where(first_core, one, zero), "core")
+        return mine, other
+
+    def spread(block):
+        came = [block] + [turn(block, step, zs) for step in range(1, zs)]
+        return came, [flip(member, "x") for member in came]
+
+    mine, other = pair_cores(head_piece)
+    head_block = jnp.concatenate(
+        [in_order(first_core, mine[:rows], other[:rows]), in_order(first_core, mine[rows:], other[rows:])],
+        axis=0,
+    )
+    head_own, head_far = spread(head_block)
+    up_own, up_far = spread(in_order(first_core, *pair_cores(column_piece(upward_weight))))
+    down_own, down_far = spread(in_order(first_core, *pair_cores(column_piece(downward_weight))))
+
+    seat = ("core", "z")
+    holds = at_core == at_z // 2
+    lend = [((i // 2) * zs + i, (1 - i // 2) * zs + i) for i in range(zs)]
+
+    def borrow(kept, sent):
+        return jnp.where(holds, kept, lax.ppermute(sent, seat, lend))
+
+    local = at_z % 2
+    own_tokens = lax.dynamic_slice_in_dim(tokens, local * length, length, 0)
+    own_tokens = borrow(own_tokens, own_tokens)
+    own_time = lax.dynamic_slice_in_dim(time_embed, local, 1, 0)
+    own_time = borrow(own_time, own_time)
+    own_ids = lax.dynamic_slice_in_dim(segment_ids, local, 1, 0)
+    own_ids = borrow(own_ids, own_ids)[0]
+
+    def at_quarter(which):
+        return lax.dynamic_slice_in_dim(cotangent, local * length + which * quarter, quarter, 0)
+
+    upstream = borrow(at_quarter(place), at_quarter(place ^ 2))
+    upstream = swap_halves(upstream, swapped).astype(f32)
+
+    def relative(values):
+        return jnp.concatenate(
+            [lax.dynamic_slice_in_dim(values, (place ^ turnover) * quarter, quarter, 0) for turnover in range(4)],
+            axis=0,
+        )
+
+    embedded_all = swap_halves(
+        relative(own_tokens).astype(f32) + own_time.astype(f32), swapped
+    )
+    embedded = embedded_all[:quarter]
+    embedded_low = embedded_all.astype(low)
+    segments = relative(own_ids)
+
+    span = 2 * rows
+    small_own = [member[span:] for member in head_own]
+    small_far = [member[span:] for member in head_far]
+    weights_head = jnp.stack(
+        [jnp.concatenate([a[:span], b[:span]], axis=0) for a, b in zip(head_own, head_far)]
+    )
+    vectors = [
+        jnp.concatenate([member[3:9], member[19:25]], axis=1).astype(f32)
+        for member in (small_own[0], small_far[0])
+    ]
+    vectors = jnp.concatenate(vectors, axis=1)
+    gains, shifts = vectors[0:2], vectors[2:6]
+
+    def shift_rows(member):
+        return jnp.concatenate([member[0:3, :small_rows], member[16:19, :small_rows]], axis=1)
+
+    biases, unit_offset = [], []
+    for a, b in zip(small_own, small_far):
+        near, distant = shift_rows(a).astype(f32), shift_rows(b).astype(f32)
+        lower = jnp.where(first_x, near, distant)
+        upper = jnp.where(first_x, distant, near)
+        biases.append(
+            jnp.concatenate(
+                [lower[0], jnp.zeros((head_size,), f32), upper[0], jnp.zeros((head_size,), f32)]
+            )
+        )
+        unit_offset.append(jnp.concatenate([lower[1:], upper[1:]], axis=1).reshape(-1))
+    biases = jnp.broadcast_to(jnp.stack(biases)[:, None, :], (zs, 8, packed))
+    unit_offset = jnp.concatenate(unit_offset)
+
+    projected, context = attend_all(embedded_low, weights_head, biases, segments, head_size)
+    context_low = jnp.concatenate([context[i] for i in range(zs)], axis=1)
+    weights_in = jnp.concatenate([weights_head[i, :, : 3 * head_size] for i in range(zs)], axis=1)
+    weights_out = jnp.concatenate([weights_head[i, :, 3 * head_size :] for i in range(zs)], axis=1)
+    mixed = sum_tokens(context_low, weights_out, ROW_PAIR)
+    normed_one, inverse_one = norm_stats(embedded + mixed + shifts[0])
+    hidden = normed_one * gains[0] + shifts[1]
+    hidden_low = spread_tokens(hidden.astype(low))
+
+    def joined(own, far):
+        return jnp.concatenate(
+            [jnp.concatenate(own, axis=1), jnp.concatenate(far, axis=1)], axis=0
+        )
+
+    weights_up, weights_down = joined(up_own, up_far), joined(down_own, down_far)
+    pre_act = jnp.dot(hidden_low, weights_up, preferred_element_type=f32) + unit_offset
+    expanded_low = gelu_value(pre_act).astype(low)
+    reduced = sum_tokens(expanded_low, weights_down, ROW_PAIR)
+    normed_two, inverse_two = norm_stats(hidden + reduced + shifts[2])
+    out = swap_halves((normed_two * gains[1] + shifts[3]).astype(low), swapped)
+    block_output = spread_output(out, zs, low)
+
+    gain_two = jnp.sum(upstream * normed_two, axis=0)
+    shift_three = jnp.sum(upstream, axis=0)
+    grad_pre_two = norm_back(upstream * gains[1], normed_two, inverse_two)
+    shift_two = jnp.sum(grad_pre_two, axis=0)
+    grad_two_low = spread_tokens(grad_pre_two.astype(low))
+    grad_down = lax.dot_general(grad_two_low, expanded_low, COL_PAIR, preferred_element_type=f32)
+    grad_act = jnp.dot(grad_two_low, weights_down, preferred_element_type=f32)
+    grad_pre_act = (grad_act * gelu_slope(pre_act)).astype(low)
+    unit_sums = jnp.sum(grad_pre_act, axis=0, dtype=f32)
+    back = sum_tokens(grad_pre_act, weights_up, ROW_PAIR)
+    grad_up = lax.dot_general(hidden_low, grad_pre_act, COL_PAIR, preferred_element_type=f32)
+    grad_hidden = back + grad_pre_two
+    gain_one = jnp.sum(grad_hidden * normed_one, axis=0)
+    shift_one = jnp.sum(grad_hidden, axis=0)
+    grad_pre_one = norm_back(grad_hidden * gains[0], normed_one, inverse_one)
+    shift_zero = jnp.sum(grad_pre_one, axis=0)
+    grad_one_low = spread_tokens(grad_pre_one.astype(low))
+    grad_context = jnp.dot(grad_one_low, weights_out, preferred_element_type=f32).astype(low)
+    grad_context = jnp.stack(
+        [grad_context[:, i * head_size : (i + 1) * head_size] for i in range(zs)]
+    )
+    grad_out = lax.dot_general(grad_one_low, context_low, COL_PAIR, preferred_element_type=f32)
+    grad_heads = attend_all_back(projected, grad_context, segments, head_size)
+    grad_projected = jnp.concatenate([grad_heads[i] for i in range(zs)], axis=1)
+    input_part = sum_tokens(grad_projected, weights_in, ROW_PAIR)
+    input_grad = swap_halves((input_part + grad_pre_one).astype(low), swapped)
+    input_grad = spread_output(input_grad, zs, f32)
+    grad_in = lax.dot_general(embedded_low, grad_projected, COL_PAIR, preferred_element_type=f32)
+    head_sums = jnp.sum(grad_projected, axis=0, dtype=f32).reshape(zs, 3, head_size)
+
+    def collect(own, far):
+        near = [
+            (a + flip(b.astype(low), "x").astype(f32)) for a, b in zip(own, far)
+        ]
+        total = near[0]
+        for step in range(1, zs):
+            total = total + turn(near[step].astype(low), -step, zs).astype(f32)
+        return total
+
+    def return_cores(block):
+        half = block.shape[0] // 2
+        mine = jnp.where(first_core, block[:half], block[half:])
+        sent = jnp.where(first_core, block[half:], block[:half])
+        came = flip(sent.astype(low), "core").astype(f32)
+        return jnp.where(first_core, mine, came), jnp.where(first_core, came, mine)
+
+    def split_blocks(grad):
+        parts = [grad[:, i * wide : (i + 1) * wide] for i in range(zs)]
+        return [p[:span] for p in parts], [p[span:] for p in parts]
+
+    total_down = collect(*split_blocks(grad_down))
+    total_up = collect(*split_blocks(grad_up))
+    head_near, head_distant = [], []
+    units = unit_sums.reshape(zs, 2, 2, 2 * small_rows)
+    for i in range(zs):
+        whole = jnp.concatenate(
+            [
+                grad_in[:, i * 3 * head_size : (i + 1) * 3 * head_size],
+                grad_out[:, i * head_size : (i + 1) * head_size],
+            ],
+            axis=1,
+        )
+        lower = jnp.concatenate([head_sums[i, 0][None], units[i, :, 0]], axis=0)
+        upper = jnp.concatenate([head_sums[i, 2][None], units[i, :, 1]], axis=0)
+        kept = jnp.where(first_x, lower, upper)
+        sent = jnp.where(first_x, upper, lower)
+        pad = ((0, 13), (0, packed - 2 * small_rows))
+        head_near.append(jnp.concatenate([whole[:span], jnp.pad(kept, pad)], axis=0))
+        head_distant.append(jnp.concatenate([whole[span:], jnp.pad(sent, pad)], axis=0))
+    total_head = collect(head_near, head_distant)
+    small_total = total_head[span : span + 3]
+    small_total = jnp.concatenate(
+        [small_total[:, :small_rows], small_total[:, small_rows : 2 * small_rows]], axis=0
+    )
+    tail = jnp.pad(small_total, ((0, 0), (0, packed - small_rows)))
+    head_zero, head_one = return_cores(
+        jnp.concatenate(
+            [
+                total_head[:rows],
+                jnp.pad(tail[:3], ((0, 13), (0, 0))),
+                total_head[rows:span],
+                jnp.pad(tail[3:], ((0, 13), (0, 0))),
+            ],
+            axis=0,
+        )
+    )
+    up_zero, up_one = return_cores(total_up)
+    down_zero, down_one = return_cores(total_down)
+    in_size = 3 * head_size
+    sent_in = jnp.concatenate([head_zero[:rows, :in_size], head_one[:rows, :in_size]], axis=1)
+    sent_out = jnp.concatenate([head_zero[:rows, in_size:], head_one[:rows, in_size:]], axis=1)
+    sent_up = jnp.concatenate([up_zero, up_one], axis=1)
+    sent_down = jnp.concatenate([down_zero, down_one], axis=1)
+    tails = [member[rows : rows + 3, :small_rows].T for member in (head_zero, head_one)]
+    sent_head = jnp.concatenate([tails[0][:, :1], tails[1][:, :1]], axis=1)
+    sent_unit = jnp.concatenate([tails[0][:, 1:], tails[1][:, 1:]], axis=1)
+
+    feature = jnp.stack([gain_one, gain_two, shift_zero, shift_one, shift_two, shift_three])
+    feature = jnp.pad(feature, ((0, 2), (0, 0)))
+    for axis in ("core", "y"):
+        feature = feature + flip(feature, axis)
+    feature = feature + lax.ppermute(feature, "z", [(0, 1), (1, 0), (2, 3), (3, 2)])
+    feature = feature + lax.ppermute(feature, "z", [(0, 3), (3, 0), (1, 2), (2, 1)])
+    feature = feature[:, :span] + flip(feature[:, span:], "x")
+    feature = jnp.where(first_core, feature[:, :rows], feature[:, rows:])
+    sent_gains, sent_shifts = feature[0:2].T, feature[2:6].T
+
+    gradients = (sent_in, sent_out, sent_up, sent_down, sent_head, sent_unit, sent_gains, sent_shifts)
+    split_part = reduce(add_squares, gradients[:6], jnp.zeros((), f32))
+    copied_part = reduce(add_squares, gradients[6:], jnp.zeros((), f32)) / (
+        lax.axis_size("z") * lax.axis_size("y")
+    )
+    grad_norm = jnp.sqrt(sum_scalar(split_part + copied_part))
+    factor = CLIP / jnp.maximum(grad_norm, CLIP)
+    results = [block_output, input_grad, grad_norm.reshape(1)]
+    for position in range(8):
+        results += adam_update(
+            masters[position],
+            moments[position],
+            squares[position],
+            gradients[position] * factor,
+            RATES[position],
+            DECAYS[position],
+        )
+    return tuple(results)
+
+
 def solution(mesh):
-    in_specs = (
-        P("rows", None),
-        P("rows", None),
-        P("rows", None),
-        P("rows", None),
-        P("rows", "tp"),
-        P("rows", "tp"),
-        P("rows", "tp"),
-        P("rows", "tp"),
-        P("rows", "tp"),
-        P("rows", "tp"),
-        P("rows", "tp"),
-        P("rows", "tp"),
-        P("rows", "tp"),
-        P("rows", "tp"),
-        P("rows", "tp"),
-        P("rows", "tp"),
-        P("rows", "tp"),
-        P("rows", "tp"),
-        P("rows", "tp"),
-        P("rows", "tp"),
-        P("rows", "tp"),
-        P("rows", "tp"),
-        P("rows", None),
-        P("rows", None),
-        P("rows", None),
-        P("rows", None),
-        P("rows", None),
-        P("rows", None),
-    )
-    out_specs = (
-        P("rows", None),
-        P("rows", None),
-        P(),
-        P("rows", "tp"),
-        P("rows", "tp"),
-        P("rows", "tp"),
-        P("rows", "tp"),
-        P("rows", "tp"),
-        P("rows", "tp"),
-        P("rows", "tp"),
-        P("rows", "tp"),
-        P("rows", "tp"),
-        P("rows", "tp"),
-        P("rows", "tp"),
-        P("rows", "tp"),
-        P("rows", "tp"),
-        P("rows", "tp"),
-        P("rows", "tp"),
-        P("rows", "tp"),
-        P("rows", "tp"),
-        P("rows", "tp"),
-        P("rows", None),
-        P("rows", None),
-        P("rows", None),
-        P("rows", None),
-        P("rows", None),
-        P("rows", None),
-    )
+    plain = mesh.shape["rows"] != 4 or mesh.shape["tp"] != 8
+    if plain:
+        rows, tp = "rows", "tp"
+        grid, work = mesh, on_device
+    else:
+        rows, tp = ("x", "core"), ("z", "y")
+        grid = Mesh(mesh.devices.reshape(2, 2, 4, 2), ("x", "core", "z", "y"))
+        work = on_grid
+    narrow, split = P(rows, None), P(rows, tp)
     return jax.shard_map(
-        on_device, mesh=mesh, in_specs=in_specs, out_specs=out_specs, check_vma=False
-    )
+        work,
+        mesh=grid,
+        in_specs=(narrow,) * 4 + (split,) * 18 + (narrow,) * 6,
+        out_specs=(narrow, narrow, P()) + (split,) * 18 + (narrow,) * 6,
+        check_vma=False,
+    )

time: 1310 us -> 640 us (0.49)
  the two profiles are of different devices: /device:TPU:1 before, /device:TPU:9 now
where the time goes in v1:
time: 640 us; the launch traced here: 630 us
  waiting for transfers between devices  313 us (49%)
  starting transfers between devices  112 us (18%)
  matrix products  61.3 us (10%)
  other arithmetic  48.3 us (8%)
  Pallas kernels  43.8 us (7%)
  local copies, waits for them, and re-layouts  40.5 us (6%)
  between operations  10.6 us (2%)
    ppermute x58, waiting for transfers between devices, flip(): return lax.ppermute(value, axis, [(0, 1), (1, 0)])  166 us
    ppermute x18, waiting for transfers between devices, turn(): lax.ppermute(value, 'z', [(i, (i + amount) % count) for i in range(count)])  85.5 us
    ppermute x8, waiting for transfers between devices, spread_output(): came = lax.ppermute(own, ('core', 'z'), pairs)  54.4 us
    ppermute x58, starting transfers between devices, flip(): return lax.ppermute(value, axis, [(0, 1), (1, 0)])  44.4 us
    ppermute x8, starting transfers between devices, spread_output(): came = lax.ppermute(own, ('core', 'z'), pairs)  33.9 us
    dot_general x4, matrix products, sum_tokens(): lax.dot_general(left[half:], right, pairing, preferred_element_type=jnp.f...  30.1 us
    pallas_call x1, Pallas kernels, attend_all_back(): pl.pallas_call(partial(attend_back_kernel, length, head_size, 256), grid=...  25.5 us
    ppermute x18, starting transfers between devices, turn(): lax.ppermute(value, 'z', [(i, (i + amount) % count) for i in range(count)])  20.1 us
  transfers between devices with their start and end apart: 92, of which 50 were waited for; matrix products, arithmetic and copies ran while one was open for 14% of the time, Pallas kernels for 4%

profile of v1, /device:TPU:9, one launch (start us, length us, event | category | flops | bytes accessed | tf_op | source)
XLA Modules:
  0.0 630.2 jit_solution(10366949578950608847)
XLA Ops:
  5.8 3.1 constant_dynamic-slice_fusion.11
  12.9 2.4 collective-permute-done.1
  21.2 3.1 collective-permute-done.3
  25.9 19.2 %collective-permute-done.8 = bf16[544,256]{1,0:T(8,128)(2,1)S(1)} collective-permute-done((bf16[544,256]{1,0:T(8,128)(2,1)S(1)}, bf16[544,256]{1,0:T(8,128)(2,1)S(1)}, u32[]{:S(2)}, u32[]{:S(2)}) %collective-permute-start.8) | collective-permute-done | bytes 278560 | tf_op jit(solution)/shard_map/ppermute | solution.py:357
  47.0 11.8 %collective-permute-done.7 = bf16[544,256]{1,0:T(8,128)(2,1)S(1)} collective-permute-done((bf16[544,256]{1,0:T(8,128)(2,1)S(1)}, bf16[544,256]{1,0:T(8,128)(2,1)S(1)}, u32[]{:S(2)}, u32[]{:S(2)}) %collective-permute-start.7) | collective-permute-done | bytes 278560 | tf_op jit(solution)/shard_map/ppermute | solution.py:353
  63.0 2.5 broadcast_select_fusion
  66.8 4.1 fusion.133
  71.0 18.3 %attend_all.1 = (bf16[4,1024,192]{2,1,0:T(8,128)(2,1)S(1)}, bf16[4,1024,64]{2,1,0:T(8,128)(2,1)S(1)}) custom-call(bf16[1024,1024]{1,0:T(8,128)(2,1)S(1)} %get-tuple-element.75.emb_ref, bf16[4,1024,256]{2,1,0:T(8,128)(2,1)} %pad_maximum_fusion.weight_ref, f32[4,8,256]{2,1,0:T(8,128)S(1)} %broadcast_in_dim.13.bias_ref, s32[1024,1]{1,0:T(8,128)S(1)} %copy.74.col_ref, ...), custom_call_target="tpu_custom_call" | custom-call | flops 4294967296 | bytes 8388608 | tf_op jit(solution)/shard_map/attend_all/pallas_call | solution.py:434
  90.5 2.6 collective-permute-done.11
  95.3 12.0 %collective-permute-done.12 = bf16[256,1024]{1,0:T(8,128)(2,1)S(1)} collective-permute-done((bf16[256,1024]{1,0:T(8,128)(2,1)S(1)}, bf16[256,1024]{1,0:T(8,128)(2,1)S(1)}, u32[]{:S(2)}, u32[]{:S(2)}) %collective-permute-start.12) | collective-permute-done | bytes 524320 | tf_op jit(solution)/shard_map/ppermute | solution.py:353
  112.2 8.5 %collective-permute-done.13 = bf16[256,1024]{1,0:T(8,128)(2,1)S(1)} collective-permute-done((bf16[256,1024]{1,0:T(8,128)(2,1)S(1)}, bf16[256,1024]{1,0:T(8,128)(2,1)S(1)}, u32[]{:S(2)}, u32[]{:S(2)}) %collective-permute-start.13) | collective-permute-done | bytes 524320 | tf_op jit(solution)/shard_map/ppermute | solution.py:353
  125.6 8.9 %collective-permute-done.17 = bf16[512,256]{1,0:T(8,128)(2,1)S(1)} collective-permute-done((bf16[512,256]{1,0:T(8,128)(2,1)S(1)}, bf16[512,256]{1,0:T(8,128)(2,1)S(1)}, u32[]{:S(2)}, u32[]{:S(2)}) %collective-permute-start.17) | collective-permute-done | bytes 262176 | tf_op jit(solution)/shard_map/ppermute | solution.py:357
  134.4 3.1 collective-permute-start.25
  139.7 11.6 %collective-permute-done.24 = bf16[512,256]{1,0:T(8,128)(2,1)S(1)} collective-permute-done((bf16[512,256]{1,0:T(8,128)(2,1)S(1)}, bf16[512,256]{1,0:T(8,128)(2,1)S(1)}, u32[]{:S(2)}, u32[]{:S(2)}) %collective-permute-start.24) | collective-permute-done | bytes 262176 | tf_op jit(solution)/shard_map/ppermute | solution.py:357
  151.6 5.4 collective-permute-done.25
  160.1 3.5 collective-permute-done.22
  163.8 4.6 multiply_convert_fusion
  169.2 5.6 collective-permute-done.28
  174.8 5.6 collective-permute-done.29
  180.4 5.6 collective-permute-done.30
  186.1 13.3 %convolution_convert_fusion.2 = bf16[512,1024]{1,0:T(8,128)(2,1)} fusion(bf16[1024,1024]{1,0:T(8,128)(2,1)S(1)} %get-tuple-element.208, bf16[512,256]{1,0:T(8,128)(2,1)S(1)} %collective-permute-done.30, bf16[512,256]{1,0:T(8,128)(2,1)S(1)} %collective-permute-done.29, bf16[512,256]{1,0:T(8,128)(2,1)S(1)} %collective-permute-done.28, ...), kind=kOutput, calls=%fused_computation.31 | convolution fusion | flops 1091043328 | bytes 4194304 | tf_op jit(solution)/shard_map/dot_general | solution.py:496
  204.7 3.5 convert_add_fusion.3
  212.1 10.2 %collective-permute-done.32 = bf16[256,1024]{1,0:T(8,128)(2,1)} collective-permute-done((bf16[256,1024]{1,0:T(8,128)(2,1)}, bf16[256,1024]{1,0:T(8,128)(2,1)}, u32[]{:S(2)}, u32[]{:S(2)}) %collective-permute-start.32) | collective-permute-done | bytes 524320 | tf_op jit(solution)/shard_map/ppermute | solution.py:353
  227.3 7.5 %collective-permute-start.33 = (bf16[256,1024]{1,0:T(8,128)(2,1)}, bf16[256,1024]{1,0:T(8,128)(2,1)S(1)}, u32[]{:S(2)}, u32[]{:S(2)}) collective-permute-start(bf16[256,1024]{1,0:T(8,128)(2,1)} %maximum_select_fusion.1), channel_id=1, source_target_pairs={{0,0},{2,2},{4,8},{6,10},{8,4},{10,6},{12,12},{14,14},{1,1},{3,3},... | collective-permute-start | bytes 1572872 | tf_op jit(solution)/shard_map/ppermute | solution.py:516
  236.9 3.7 collective-permute-start.43
  241.4 16.3 %collective-permute-done.33 = bf16[256,1024]{1,0:T(8,128)(2,1)S(1)} collective-permute-done((bf16[256,1024]{1,0:T(8,128)(2,1)}, bf16[256,1024]{1,0:T(8,128)(2,1)S(1)}, u32[]{:S(2)}, u32[]{:S(2)}) %collective-permute-start.33) | collective-permute-done | bytes 524320 | tf_op jit(solution)/shard_map/ppermute | solution.py:516
  260.9 2.7 broadcast_in_dim.12
  264.4 6.0 collective-permute-done.34
  272.0 4.9 collective-permute-done.36
  277.9 3.5 convert_reduce_fusion
  281.5 13.6 %convolution_convert_fusion.1 = bf16[512,1024]{1,0:T(8,128)(2,1)} fusion(bf16[1024,1024]{1,0:T(8,128)(2,1)S(1)} %get-tuple-element.211, bf16[512,256]{1,0:T(8,128)(2,1)S(1)} %copy-done.98, bf16[512,256]{1,0:T(8,128)(2,1)S(1)} %copy-done.95, bf16[512,256]{1,0:T(8,128)(2,1)S(1)} %copy-done.92, bf16[512,256]{1,0:T(8,128)(2,1)S(1)} %copy-done.89, ...), kind=kOutput, calls=%fused_computation.30 | convolution fusion | flops 1091043328 | bytes 4194304 | tf_op jit(solution)/shard_map/dot_general | solution.py:496
  295.2 4.5 fusion.161
  303.8 4.7 fusion.160
  308.9 2.7 convert_add_fusion.2
  314.2 5.4 collective-permute-done.79
  321.1 9.7 %collective-permute-done.67 = bf16[512,256]{1,0:T(8,128)(2,1)S(1)} collective-permute-done((bf16[512,256]{1,0:T(8,128)(2,1)S(1)}, bf16[512,256]{1,0:T(8,128)(2,1)S(1)}, u32[]{:S(2)}, u32[]{:S(2)}) %collective-permute-start.67) | collective-permute-done | bytes 262176 | tf_op jit(solution)/shard_map/ppermute | solution.py:353
  331.1 5.4 collective-permute-done.69
  336.4 5.6 collective-permute-done.71
  346.8 2.4 collective-permute-start.70
  349.1 6.1 collective-permute-done.78
  356.9 14.0 %collective-permute-done.80 = bf16[512,256]{1,0:T(8,128)(2,1)S(1)} collective-permute-done((bf16[512,256]{1,0:T(8,128)(2,1)S(1)}, bf16[512,256]{1,0:T(8,128)(2,1)S(1)}, u32[]{:S(2)}, u32[]{:S(2)}) %collective-permute-start.80) | collective-permute-done | bytes 262176 | tf_op jit(solution)/shard_map/ppermute | solution.py:357
  372.4 2.2 collective-permute-start.37
  374.6 14.8 %collective-permute-start.39 = (bf16[256,1024]{1,0:T(8,128)(2,1)}, bf16[256,1024]{1,0:T(8,128)(2,1)}, u32[]{:S(2)}, u32[]{:S(2)}) collective-permute-start(bf16[256,1024]{1,0:T(8,128)(2,1)} %maximum_select_fusion.1), channel_id=1, source_target_pairs={{0,6},{2,0},{4,14},{6,8},{8,2},{10,4},{12,10},{14,12},{1,7},{3,1},... | collective-permute-start | bytes 1572872 | tf_op jit(solution)/shard_map/ppermute | solution.py:516
  390.8 2.6 collective-permute-done.72
  400.9 6.0 collective-permute-start.84
  408.7 2.7 collective-permute-done.85
  421.2 25.5 %attend_all_back.1 = bf16[4,1024,192]{2,1,0:T(8,128)(2,1)S(1)} custom-call(bf16[4,1024,192]{2,1,0:T(8,128)(2,1)S(1)} %copy-done.1, bf16[4,1024,64]{2,1,0:T(8,128)(2,1)S(1)} %pad_maximum_fusion.9.grad_ref, s32[1024,1]{1,0:T(8,128)S(1)} %copy.74.col_ref, s32[1,1024]{1,0:T(1,128)S(1)} %bitcast.152), custom_call_target="tpu_custom_call" | custom-call | flops 5368709120 | bytes 8388608 | tf_op jit(solution)/shard_map/attend_all_back/pallas_call | solution.py:463
  458.4 8.7 %collective-permute-done.59 = bf16[528,256]{1,0:T(8,128)(2,1)S(1)} collective-permute-done((bf16[528,256]{1,0:T(8,128)(2,1)S(1)}, bf16[528,256]{1,0:T(8,128)(2,1)S(1)}, u32[]{:S(2)}, u32[]{:S(2)}) %collective-permute-start.59) | collective-permute-done | bytes 270368 | tf_op jit(solution)/shard_map/ppermute | solution.py:353
  467.6 5.3 collective-permute-done.61
  472.9 2.2 collective-permute-start.60
  475.2 3.5 collective-permute-done.63
  480.1 2.3 collective-permute-start.64
  484.1 10.3 %collective-permute-done.62 = bf16[528,256]{1,0:T(8,128)(2,1)S(1)} collective-permute-done((bf16[528,256]{1,0:T(8,128)(2,1)S(1)}, bf16[528,256]{1,0:T(8,128)(2,1)S(1)}, u32[]{:S(2)}, u32[]{:S(2)}) %collective-permute-start.62) | collective-permute-done | bytes 270368 | tf_op jit(solution)/shard_map/ppermute | solution.py:357
  494.4 5.8 collective-permute-done.64
  514.6 2.5 convolution_convert_fusion
  520.4 2.9 collective-permute-start.90
  534.7 8.4 %collective-permute-done.49 = bf16[256,1024]{1,0:T(8,128)(2,1)S(1)} collective-permute-done((bf16[256,1024]{1,0:T(8,128)(2,1)S(1)}, bf16[256,1024]{1,0:T(8,128)(2,1)S(1)}, u32[]{:S(2)}, u32[]{:S(2)}) %collective-permute-start.49) | collective-permute-done | bytes 524320 | tf_op jit(solution)/shard_map/ppermute | solution.py:353
  543.6 7.6 %collective-permute-start.50 = (bf16[256,1024]{1,0:T(8,128)(2,1)S(1)}, bf16[256,1024]{1,0:T(8,128)(2,1)S(1)}, u32[]{:S(2)}, u32[]{:S(2)}) collective-permute-start(bf16[256,1024]{1,0:T(8,128)(2,1)S(1)} %maximum_select_fusion.3), channel_id=1, source_target_pairs={{0,0},{2,2},{4,8},{6,10},{8,4},{10,6},{12,12},{14,14},{1,1},{3,3},... | collective-permute-start | bytes 1572872 | tf_op jit(solution)/shard_map/ppermute | solution.py:516
  555.1 28.2 %collective-permute-done.50 = bf16[256,1024]{1,0:T(8,128)(2,1)S(1)} collective-permute-done((bf16[256,1024]{1,0:T(8,128)(2,1)S(1)}, bf16[256,1024]{1,0:T(8,128)(2,1)S(1)}, u32[]{:S(2)}, u32[]{:S(2)}) %collective-permute-start.50) | collective-permute-done | bytes 524320 | tf_op jit(solution)/shard_map/ppermute | solution.py:516
  585.0 9.9 %collective-permute-done.52 = bf16[256,1024]{1,0:T(8,128)(2,1)S(1)} collective-permute-done((bf16[256,1024]{1,0:T(8,128)(2,1)S(1)}, bf16[256,1024]{1,0:T(8,128)(2,1)S(1)}, u32[]{:S(2)}, u32[]{:S(2)}) %collective-permute-start.52) | collective-permute-done | bytes 524320 | tf_op jit(solution)/shard_map/ppermute | solution.py:516
  598.0 8.7 %collective-permute-done.53 = bf16[256,1024]{1,0:T(8,128)(2,1)S(1)} collective-permute-done((bf16[256,1024]{1,0:T(8,128)(2,1)S(1)}, bf16[256,1024]{1,0:T(8,128)(2,1)S(1)}, u32[]{:S(2)}, u32[]{:S(2)}) %collective-permute-start.53) | collective-permute-done | bytes 524320 | tf_op jit(solution)/shard_map/ppermute | solution.py:353
  606.9 11.0 %collective-permute-done.55 = bf16[256,1024]{1,0:T(8,128)(2,1)S(1)} collective-permute-done((bf16[256,1024]{1,0:T(8,128)(2,1)S(1)}, bf16[256,1024]{1,0:T(8,128)(2,1)S(1)}, u32[]{:S(2)}, u32[]{:S(2)}) %collective-permute-start.55) | collective-permute-done | bytes 524320 | tf_op jit(solution)/shard_map/ppermute | solution.py:353
  618.1 7.2 %collective-permute-done.57 = bf16[256,1024]{1,0:T(8,128)(2,1)S(1)} collective-permute-done((bf16[256,1024]{1,0:T(8,128)(2,1)S(1)}, bf16[256,1024]{1,0:T(8,128)(2,1)S(1)}, u32[]{:S(2)}, u32[]{:S(2)}) %collective-permute-start.57) | collective-permute-done | bytes 524320 | tf_op jit(solution)/shard_map/ppermute | solution.py:353
  625.5 3.4 copy-done.8
  (620 shorter events, 151.0 us)
Async XLA Ops:
  8.9 52.5 %collective-permute-start = (bf16[1024,1024]{1,0:T(8,128)(2,1)}, bf16[1024,1024]{1,0:T(8,128)(2,1)}, u32[]{:S(2)}, u32[]{:S(2)}) collective-permute-start(bf16[1024,1024]{1,0:T(8,128)(2,1)} %constant_dynamic-slice_fusion.11), channel_id=1, source_target_pairs={{0,8},{2,10},{12,4},{14,6},{1,9},{3,11},{13,5},{15,7},{16,24},{18,... | collective-permute-start | bytes 6291464 | tf_op jit(solution)/shard_map/ppermute | solution.py:603
  18.7 26.3 %collective-permute-start.6 = (bf16[544,256]{1,0:T(8,128)(2,1)S(1)}, bf16[544,256]{1,0:T(8,128)(2,1)S(1)}, u32[]{:S(2)}, u32[]{:S(2)}) collective-permute-start(bf16[544,256]{1,0:T(8,128)(2,1)S(1)} %pad_maximum_fusion.25), channel_id=1, source_target_pairs={{0,4},{2,6},{4,0},{6,2},{1,5},{3,7},{5,1},{7,3},{8,12},{10,14},{12... | collective-permute-start | bytes 835592 | tf_op jit(solution)/shard_map/ppermute | solution.py:357
  20.0 25.1 %collective-permute-start.8 = (bf16[544,256]{1,0:T(8,128)(2,1)S(1)}, bf16[544,256]{1,0:T(8,128)(2,1)S(1)}, u32[]{:S(2)}, u32[]{:S(2)}) collective-permute-start(bf16[544,256]{1,0:T(8,128)(2,1)S(1)} %pad_maximum_fusion.25), channel_id=1, source_target_pairs={{0,6},{2,0},{4,2},{6,4},{1,7},{3,1},{5,3},{7,5},{8,14},{10,8},{12,... | collective-permute-start | bytes 835592 | tf_op jit(solution)/shard_map/ppermute | solution.py:357
  25.5 21.3 %collective-permute-start.5 = (bf16[544,256]{1,0:T(8,128)(2,1)S(1)}, bf16[544,256]{1,0:T(8,128)(2,1)S(1)}, u32[]{:S(2)}, u32[]{:S(2)}) collective-permute-start(bf16[544,256]{1,0:T(8,128)(2,1)S(1)} %collective-permute-done.4), channel_id=1, source_target_pairs={{0,16},{16,0},{1,17},{17,1},{2,18},{18,2},{3,19},{19,3},{4,20},{20... | collective-permute-start | bytes 835592 | tf_op jit(solution)/shard_map/ppermute | solution.py:353
  45.1 13.8 %collective-permute-start.9 = (bf16[544,256]{1,0:T(8,128)(2,1)S(1)}, bf16[544,256]{1,0:T(8,128)(2,1)S(1)}, u32[]{:S(2)}, u32[]{:S(2)}) collective-permute-start(bf16[544,256]{1,0:T(8,128)(2,1)S(1)} %collective-permute-done.8), channel_id=1, source_target_pairs={{0,16},{16,0},{1,17},{17,1},{2,18},{18,2},{3,19},{19,3},{4,20},{20... | collective-permute-start | bytes 835592 | tf_op jit(solution)/shard_map/ppermute | solution.py:353
  45.1 13.6 %collective-permute-start.7 = (bf16[544,256]{1,0:T(8,128)(2,1)S(1)}, bf16[544,256]{1,0:T(8,128)(2,1)S(1)}, u32[]{:S(2)}, u32[]{:S(2)}) collective-permute-start(bf16[544,256]{1,0:T(8,128)(2,1)S(1)} %collective-permute-done.6), channel_id=1, source_target_pairs={{0,16},{16,0},{1,17},{17,1},{2,18},{18,2},{3,19},{19,3},{4,20},{20... | collective-permute-start | bytes 835592 | tf_op jit(solution)/shard_map/ppermute | solution.py:353
  93.9 13.4 %collective-permute-start.12 = (bf16[256,1024]{1,0:T(8,128)(2,1)S(1)}, bf16[256,1024]{1,0:T(8,128)(2,1)S(1)}, u32[]{:S(2)}, u32[]{:S(2)}) collective-permute-start(bf16[256,1024]{1,0:T(8,128)(2,1)S(1)} %slice.1175), channel_id=1, source_target_pairs={{0,1},{1,0},{2,3},{3,2},{4,5},{5,4},{6,7},{7,6},{8,9},{9,8},{10,11... | collective-permute-start | bytes 1572872 | tf_op jit(solution)/shard_map/ppermute | solution.py:353
  108.1 12.6 %collective-permute-start.13 = (bf16[256,1024]{1,0:T(8,128)(2,1)S(1)}, bf16[256,1024]{1,0:T(8,128)(2,1)S(1)}, u32[]{:S(2)}, u32[]{:S(2)}) collective-permute-start(bf16[256,1024]{1,0:T(8,128)(2,1)S(1)} %fusion.24), channel_id=1, source_target_pairs={{0,1},{1,0},{2,3},{3,2},{4,5},{5,4},{6,7},{7,6},{8,9},{9,8},{10,11... | collective-permute-start | bytes 1572872 | tf_op jit(solution)/shard_map/ppermute | solution.py:353
  112.0 13.4 %collective-permute-start.16 = (bf16[512,256]{1,0:T(8,128)(2,1)S(1)}, bf16[512,256]{1,0:T(8,128)(2,1)S(1)}, u32[]{:S(2)}, u32[]{:S(2)}) collective-permute-start(bf16[512,256]{1,0:T(8,128)(2,1)S(1)} %maximum_select_fusion.5), channel_id=1, source_target_pairs={{0,2},{2,4},{4,6},{6,0},{1,3},{3,5},{5,7},{7,1},{8,10},{10,12},{12... | collective-permute-start | bytes 786440 | tf_op jit(solution)/shard_map/ppermute | solution.py:357
  112.2 22.2 %collective-permute-start.17 = (bf16[512,256]{1,0:T(8,128)(2,1)S(1)}, bf16[512,256]{1,0:T(8,128)(2,1)S(1)}, u32[]{:S(2)}, u32[]{:S(2)}) collective-permute-start(bf16[512,256]{1,0:T(8,128)(2,1)S(1)} %maximum_select_fusion.5), channel_id=1, source_target_pairs={{0,4},{2,6},{4,0},{6,2},{1,5},{3,7},{5,1},{7,3},{8,12},{10,14},{12... | collective-permute-start | bytes 786440 | tf_op jit(solution)/shard_map/ppermute | solution.py:357
  120.8 43.0 %collective-permute-start.14 = (bf16[512,1024]{1,0:T(8,128)(2,1)S(1)}, bf16[512,1024]{1,0:T(8,128)(2,1)S(1)}, u32[]{:S(2)}, u32[]{:S(2)}) collective-permute-start(bf16[512,1024]{1,0:T(8,128)(2,1)S(1)} %pad_maximum_fusion.6), channel_id=1, source_target_pairs={{0,8},{8,0},{1,9},{9,1},{2,10},{10,2},{3,11},{11,3},{4,12},{12,4},... | collective-permute-start | bytes 3145736 | tf_op jit(solution)/shard_map/ppermute | solution.py:353
  122.8 15.5 %collective-permute-start.18 = (bf16[512,256]{1,0:T(8,128)(2,1)S(1)}, bf16[512,256]{1,0:T(8,128)(2,1)S(1)}, u32[]{:S(2)}, u32[]{:S(2)}) collective-permute-start(bf16[512,256]{1,0:T(8,128)(2,1)S(1)} %maximum_select_fusion.5), channel_id=1, source_target_pairs={{0,6},{2,0},{4,2},{6,4},{1,7},{3,1},{5,3},{7,5},{8,14},{10,8},{12,... | collective-permute-start | bytes 786440 | tf_op jit(solution)/shard_map/ppermute | solution.py:357
  125.2 14.3 %collective-permute-start.19 = (bf16[512,256]{1,0:T(8,128)(2,1)S(1)}, bf16[512,256]{1,0:T(8,128)(2,1)S(1)}, u32[]{:S(2)}, u32[]{:S(2)}) collective-permute-start(bf16[512,256]{1,0:T(8,128)(2,1)S(1)} %maximum_select_fusion.5), channel_id=1, source_target_pairs={{0,16},{16,0},{1,17},{17,1},{2,18},{18,2},{3,19},{19,3},{4,20},{20... | collective-permute-start | bytes 786440 | tf_op jit(solution)/shard_map/ppermute | solution.py:353
  125.4 25.9 %collective-permute-start.24 = (bf16[512,256]{1,0:T(8,128)(2,1)S(1)}, bf16[512,256]{1,0:T(8,128)(2,1)S(1)}, u32[]{:S(2)}, u32[]{:S(2)}) collective-permute-start(bf16[512,256]{1,0:T(8,128)(2,1)S(1)} %maximum_select_fusion.6), channel_id=1, source_target_pairs={{0,2},{2,4},{4,6},{6,0},{1,3},{3,5},{5,7},{7,1},{8,10},{10,12},{12... | collective-permute-start | bytes 786440 | tf_op jit(solution)/shard_map/ppermute | solution.py:357
  134.4 22.5 %collective-permute-start.25 = (bf16[512,256]{1,0:T(8,128)(2,1)S(1)}, bf16[512,256]{1,0:T(8,128)(2,1)S(1)}, u32[]{:S(2)}, u32[]{:S(2)}) collective-permute-start(bf16[512,256]{1,0:T(8,128)(2,1)S(1)} %maximum_select_fusion.6), channel_id=1, source_target_pairs={{0,4},{2,6},{4,0},{6,2},{1,5},{3,7},{5,1},{7,3},{8,12},{10,14},{12... | collective-permute-start | bytes 786440 | tf_op jit(solution)/shard_map/ppermute | solution.py:357
  138.3 19.1 %collective-permute-start.26 = (bf16[512,256]{1,0:T(8,128)(2,1)S(1)}, bf16[512,256]{1,0:T(8,128)(2,1)S(1)}, u32[]{:S(2)}, u32[]{:S(2)}) collective-permute-start(bf16[512,256]{1,0:T(8,128)(2,1)S(1)} %maximum_select_fusion.6), channel_id=1, source_target_pairs={{0,6},{2,0},{4,2},{6,4},{1,7},{3,1},{5,3},{7,5},{8,14},{10,8},{12,... | collective-permute-start | bytes 786440 | tf_op jit(solution)/shard_map/ppermute | solution.py:357
  139.4 19.2 %collective-permute-start.20 = (bf16[512,256]{1,0:T(8,128)(2,1)S(1)}, bf16[512,256]{1,0:T(8,128)(2,1)S(1)}, u32[]{:S(2)}, u32[]{:S(2)}) collective-permute-start(bf16[512,256]{1,0:T(8,128)(2,1)S(1)} %collective-permute-done.16), channel_id=1, source_target_pairs={{0,16},{16,0},{1,17},{17,1},{2,18},{18,2},{3,19},{19,3},{4,20},{20... | collective-permute-start | bytes 786440 | tf_op jit(solution)/shard_map/ppermute | solution.py:353
  157.4 11.8 %collective-permute-start.27 = (bf16[512,256]{1,0:T(8,128)(2,1)S(1)}, bf16[512,256]{1,0:T(8,128)(2,1)S(1)}, u32[]{:S(2)}, u32[]{:S(2)}) collective-permute-start(bf16[512,256]{1,0:T(8,128)(2,1)S(1)} %maximum_select_fusion.6), channel_id=1, source_target_pairs={{0,16},{16,0},{1,17},{17,1},{2,18},{18,2},{3,19},{19,3},{4,20},{20... | collective-permute-start | bytes 786440 | tf_op jit(solution)/shard_map/ppermute | solution.py:353
  158.6 16.2 %collective-permute-start.28 = (bf16[512,256]{1,0:T(8,128)(2,1)S(1)}, bf16[512,256]{1,0:T(8,128)(2,1)S(1)}, u32[]{:S(2)}, u32[]{:S(2)}) collective-permute-start(bf16[512,256]{1,0:T(8,128)(2,1)S(1)} %collective-permute-done.24), channel_id=1, source_target_pairs={{0,16},{16,0},{1,17},{17,1},{2,18},{18,2},{3,19},{19,3},{4,20},{20... | collective-permute-start | bytes 786440 | tf_op jit(solution)/shard_map/ppermute | solution.py:353
  158.9 21.5 %collective-permute-start.29 = (bf16[512,256]{1,0:T(8,128)(2,1)S(1)}, bf16[512,256]{1,0:T(8,128)(2,1)S(1)}, u32[]{:S(2)}, u32[]{:S(2)}) collective-permute-start(bf16[512,256]{1,0:T(8,128)(2,1)S(1)} %collective-permute-done.25), channel_id=1, source_target_pairs={{0,16},{16,0},{1,17},{17,1},{2,18},{18,2},{3,19},{19,3},{4,20},{20... | collective-permute-start | bytes 786440 | tf_op jit(solution)/shard_map/ppermute | solution.py:353
  163.6 22.5 %collective-permute-start.30 = (bf16[512,256]{1,0:T(8,128)(2,1)S(1)}, bf16[512,256]{1,0:T(8,128)(2,1)S(1)}, u32[]{:S(2)}, u32[]{:S(2)}) collective-permute-start(bf16[512,256]{1,0:T(8,128)(2,1)S(1)} %collective-permute-done.26), channel_id=1, source_target_pairs={{0,16},{16,0},{1,17},{17,1},{2,18},{18,2},{3,19},{19,3},{4,20},{20... | collective-permute-start | bytes 786440 | tf_op jit(solution)/shard_map/ppermute | solution.py:353
  210.4 11.9 %collective-permute-start.32 = (bf16[256,1024]{1,0:T(8,128)(2,1)}, bf16[256,1024]{1,0:T(8,128)(2,1)}, u32[]{:S(2)}, u32[]{:S(2)}) collective-permute-start(bf16[256,1024]{1,0:T(8,128)(2,1)} %slice.1174), channel_id=1, source_target_pairs={{0,1},{1,0},{2,3},{3,2},{4,5},{5,4},{6,7},{7,6},{8,9},{9,8},{10,11... | collective-permute-start | bytes 1572872 | tf_op jit(solution)/shard_map/ppermute | solution.py:353
  227.3 30.4 %collective-permute-start.33 = (bf16[256,1024]{1,0:T(8,128)(2,1)}, bf16[256,1024]{1,0:T(8,128)(2,1)S(1)}, u32[]{:S(2)}, u32[]{:S(2)}) collective-permute-start(bf16[256,1024]{1,0:T(8,128)(2,1)} %maximum_select_fusion.1), channel_id=1, source_target_pairs={{0,0},{2,2},{4,8},{6,10},{8,4},{10,6},{12,12},{14,14},{1,1},{3,3},... | collective-permute-start | bytes 1572872 | tf_op jit(solution)/shard_map/ppermute | solution.py:516
  235.6 24.2 %collective-permute-start.35 = (bf16[256,1024]{1,0:T(8,128)(2,1)}, bf16[256,1024]{1,0:T(8,128)(2,1)S(1)}, u32[]{:S(2)}, u32[]{:S(2)}) collective-permute-start(bf16[256,1024]{1,0:T(8,128)(2,1)} %maximum_select_fusion.1), channel_id=1, source_target_pairs={{0,2},{2,4},{4,10},{6,12},{8,6},{10,0},{12,14},{14,8},{1,3},{3,5},... | collective-permute-start | bytes 1572872 | tf_op jit(solution)/shard_map/ppermute | solution.py:516
  236.9 40.9 %collective-permute-start.43 = (bf16[512,1024]{1,0:T(8,128)(2,1)S(1)}, bf16[512,1024]{1,0:T(8,128)(2,1)S(1)}, u32[]{:S(2)}, u32[]{:S(2)}) collective-permute-start(bf16[512,1024]{1,0:T(8,128)(2,1)S(1)} %pad_maximum_fusion.7), channel_id=1, source_target_pairs={{0,8},{8,0},{1,9},{9,1},{2,10},{10,2},{3,11},{11,3},{4,12},{12,4},... | collective-permute-start | bytes 3145736 | tf_op jit(solution)/shard_map/ppermute | solution.py:353
  257.7 12.7 %collective-permute-start.34 = (bf16[256,1024]{1,0:T(8,128)(2,1)S(1)}, bf16[256,1024]{1,0:T(8,128)(2,1)S(1)}, u32[]{:S(2)}, u32[]{:S(2)}) collective-permute-start(bf16[256,1024]{1,0:T(8,128)(2,1)S(1)} %collective-permute-done.33), channel_id=1, source_target_pairs={{0,1},{1,0},{2,3},{3,2},{4,5},{5,4},{6,7},{7,6},{8,9},{9,8},{10,11... | collective-permute-start | bytes 1572872 | tf_op jit(solution)/shard_map/ppermute | solution.py:353
  259.8 17.1 %collective-permute-start.36 = (bf16[256,1024]{1,0:T(8,128)(2,1)S(1)}, bf16[256,1024]{1,0:T(8,128)(2,1)S(1)}, u32[]{:S(2)}, u32[]{:S(2)}) collective-permute-start(bf16[256,1024]{1,0:T(8,128)(2,1)S(1)} %collective-permute-done.35), channel_id=1, source_target_pairs={{0,1},{1,0},{2,3},{3,2},{4,5},{5,4},{6,7},{7,6},{8,9},{9,8},{10,11... | collective-permute-start | bytes 1572872 | tf_op jit(solution)/shard_map/ppermute | solution.py:353
  295.1 13.4 %collective-permute-start.44 = (bf16[512,1024]{1,0:T(8,128)(2,1)}, bf16[512,1024]{1,0:T(8,128)(2,1)}, u32[]{:S(2)}, u32[]{:S(2)}) collective-permute-start(bf16[512,1024]{1,0:T(8,128)(2,1)} %convolution_convert_fusion.1), channel_id=1, source_target_pairs={{0,8},{8,0},{1,9},{9,1},{2,10},{10,2},{3,11},{11,3},{4,12},{12,4},... | collective-permute-start | bytes 3145736 | tf_op jit(solution)/shard_map/ppermute | solution.py:353
  300.8 11.0 %collective-permute-start.75 = (bf16[512,256]{1,0:T(8,128)(2,1)}, bf16[512,256]{1,0:T(8,128)(2,1)S(1)}, u32[]{:S(2)}, u32[]{:S(2)}) collective-permute-start(bf16[512,256]{1,0:T(8,128)(2,1)} %get-tuple-element.92), channel_id=1, source_target_pairs={{0,16},{16,0},{1,17},{17,1},{2,18},{18,2},{3,19},{19,3},{4,20},{20... | collective-permute-start | bytes 786440 | tf_op jit(solution)/shard_map/ppermute | solution.py:353
  301.0 13.0 %collective-permute-start.77 = (bf16[512,256]{1,0:T(8,128)(2,1)}, bf16[512,256]{1,0:T(8,128)(2,1)S(1)}, u32[]{:S(2)}, u32[]{:S(2)}) collective-permute-start(bf16[512,256]{1,0:T(8,128)(2,1)} %get-tuple-element.91), channel_id=1, source_target_pairs={{0,16},{16,0},{1,17},{17,1},{2,18},{18,2},{3,19},{19,3},{4,20},{20... | collective-permute-start | bytes 786440 | tf_op jit(solution)/shard_map/ppermute | solution.py:353
  302.2 17.4 %collective-permute-start.79 = (bf16[512,256]{1,0:T(8,128)(2,1)}, bf16[512,256]{1,0:T(8,128)(2,1)S(1)}, u32[]{:S(2)}, u32[]{:S(2)}) collective-permute-start(bf16[512,256]{1,0:T(8,128)(2,1)} %get-tuple-element.90), channel_id=1, source_target_pairs={{0,16},{16,0},{1,17},{17,1},{2,18},{18,2},{3,19},{19,3},{4,20},{20... | collective-permute-start | bytes 786440 | tf_op jit(solution)/shard_map/ppermute | solution.py:353
  302.5 42.9 %collective-permute-start.74 = (bf16[512,256]{1,0:T(8,128)(2,1)}, bf16[512,256]{1,0:T(8,128)(2,1)S(1)}, u32[]{:S(2)}, u32[]{:S(2)}) collective-permute-start(bf16[512,256]{1,0:T(8,128)(2,1)} %get-tuple-element.89), channel_id=1, source_target_pairs={{0,16},{16,0},{1,17},{17,1},{2,18},{18,2},{3,19},{19,3},{4,20},{20... | collective-permute-start | bytes 786440 | tf_op jit(solution)/shard_map/ppermute | solution.py:353
  308.6 22.3 %collective-permute-start.67 = (bf16[512,256]{1,0:T(8,128)(2,1)S(1)}, bf16[512,256]{1,0:T(8,128)(2,1)S(1)}, u32[]{:S(2)}, u32[]{:S(2)}) collective-permute-start(bf16[512,256]{1,0:T(8,128)(2,1)S(1)} %get-tuple-element.96), channel_id=1, source_target_pairs={{0,16},{16,0},{1,17},{17,1},{2,18},{18,2},{3,19},{19,3},{4,20},{20... | collective-permute-start | bytes 786440 | tf_op jit(solution)/shard_map/ppermute | solution.py:353
  311.7 24.7 %collective-permute-start.69 = (bf16[512,256]{1,0:T(8,128)(2,1)S(1)}, bf16[512,256]{1,0:T(8,128)(2,1)S(1)}, u32[]{:S(2)}, u32[]{:S(2)}) collective-permute-start(bf16[512,256]{1,0:T(8,128)(2,1)S(1)} %get-tuple-element.95), channel_id=1, source_target_pairs={{0,16},{16,0},{1,17},{17,1},{2,18},{18,2},{3,19},{19,3},{4,20},{20... | collective-permute-start | bytes 786440 | tf_op jit(solution)/shard_map/ppermute | solution.py:353
  314.0 28.1 %collective-permute-start.71 = (bf16[512,256]{1,0:T(8,128)(2,1)S(1)}, bf16[512,256]{1,0:T(8,128)(2,1)S(1)}, u32[]{:S(2)}, u32[]{:S(2)}) collective-permute-start(bf16[512,256]{1,0:T(8,128)(2,1)S(1)} %get-tuple-element.94), channel_id=1, source_target_pairs={{0,16},{16,0},{1,17},{17,1},{2,18},{18,2},{3,19},{19,3},{4,20},{20... | collective-permute-start | bytes 786440 | tf_op jit(solution)/shard_map/ppermute | solution.py:353
  319.6 22.7 %collective-permute-start.45 = (bf16[256,1024]{1,0:T(8,128)(2,1)S(1)}, bf16[256,1024]{1,0:T(8,128)(2,1)S(1)}, u32[]{:S(2)}, u32[]{:S(2)}) collective-permute-start(bf16[256,1024]{1,0:T(8,128)(2,1)S(1)} %slice.1173), channel_id=1, source_target_pairs={{0,1},{1,0},{2,3},{3,2},{4,5},{5,4},{6,7},{7,6},{8,9},{9,8},{10,11... | collective-permute-start | bytes 1572872 | tf_op jit(solution)/shard_map/ppermute | solution.py:353
  330.8 41.5 %collective-permute-start.66 = (bf16[512,256]{1,0:T(8,128)(2,1)S(1)}, bf16[512,256]{1,0:T(8,128)(2,1)S(1)}, u32[]{:S(2)}, u32[]{:S(2)}) collective-permute-start(bf16[512,256]{1,0:T(8,128)(2,1)S(1)} %get-tuple-element.93), channel_id=1, source_target_pairs={{0,16},{16,0},{1,17},{17,1},{2,18},{18,2},{3,19},{19,3},{4,20},{20... | collective-permute-start | bytes 786440 | tf_op jit(solution)/shard_map/ppermute | solution.py:353
  342.1 13.2 %collective-permute-start.78 = (bf16[512,256]{1,0:T(8,128)(2,1)S(1)}, bf16[512,256]{1,0:T(8,128)(2,1)S(1)}, u32[]{:S(2)}, u32[]{:S(2)}) collective-permute-start(bf16[512,256]{1,0:T(8,128)(2,1)S(1)} %get-tuple-element.78), channel_id=1, source_target_pairs={{0,4},{2,6},{4,0},{6,2},{1,5},{3,7},{5,1},{7,3},{8,12},{10,14},{12... | collective-permute-start | bytes 786440 | tf_op jit(solution)/shard_map/ppermute | solution.py:357
  342.3 28.5 %collective-permute-start.80 = (bf16[512,256]{1,0:T(8,128)(2,1)S(1)}, bf16[512,256]{1,0:T(8,128)(2,1)S(1)}, u32[]{:S(2)}, u32[]{:S(2)}) collective-permute-start(bf16[512,256]{1,0:T(8,128)(2,1)S(1)} %get-tuple-element.79), channel_id=1, source_target_pairs={{0,2},{2,4},{4,6},{6,0},{1,3},{3,5},{5,7},{7,1},{8,10},{10,12},{12... | collective-permute-start | bytes 786440 | tf_op jit(solution)/shard_map/ppermute | solution.py:357
  345.3 29.3 %collective-permute-start.68 = (bf16[512,256]{1,0:T(8,128)(2,1)S(1)}, bf16[512,256]{1,0:T(8,128)(2,1)S(1)}, u32[]{:S(2)}, u32[]{:S(2)}) collective-permute-start(bf16[512,256]{1,0:T(8,128)(2,1)S(1)} %get-tuple-element.80), channel_id=1, source_target_pairs={{0,6},{2,0},{4,2},{6,4},{1,7},{3,1},{5,3},{7,5},{8,14},{10,8},{12,... | collective-permute-start | bytes 786440 | tf_op jit(solution)/shard_map/ppermute | solution.py:357
  346.8 42.6 %collective-permute-start.70 = (bf16[512,256]{1,0:T(8,128)(2,1)S(1)}, bf16[512,256]{1,0:T(8,128)(2,1)S(1)}, u32[]{:S(2)}, u32[]{:S(2)}) collective-permute-start(bf16[512,256]{1,0:T(8,128)(2,1)S(1)} %get-tuple-element.81), channel_id=1, source_target_pairs={{0,4},{2,6},{4,0},{6,2},{1,5},{3,7},{5,1},{7,3},{8,12},{10,14},{12... | collective-permute-start | bytes 786440 | tf_op jit(solution)/shard_map/ppermute | solution.py:357
  355.2 38.1 %collective-permute-start.72 = (bf16[512,256]{1,0:T(8,128)(2,1)S(1)}, bf16[512,256]{1,0:T(8,128)(2,1)S(1)}, u32[]{:S(2)}, u32[]{:S(2)}) collective-permute-start(bf16[512,256]{1,0:T(8,128)(2,1)S(1)} %get-tuple-element.82), channel_id=1, source_target_pairs={{0,2},{2,4},{4,6},{6,0},{1,3},{3,5},{5,7},{7,1},{8,10},{10,12},{12... | collective-permute-start | bytes 786440 | tf_op jit(solution)/shard_map/ppermute | solution.py:357
  370.8 24.2 %collective-permute-start.46 = (bf16[256,1024]{1,0:T(8,128)(2,1)}, bf16[256,1024]{1,0:T(8,128)(2,1)}, u32[]{:S(2)}, u32[]{:S(2)}) collective-permute-start(bf16[256,1024]{1,0:T(8,128)(2,1)} %convert_element_type.303), channel_id=1, source_target_pairs={{0,1},{1,0},{2,3},{3,2},{4,5},{5,4},{6,7},{7,6},{8,9},{9,8},{10,11... | collective-permute-start | bytes 1572872 | tf_op jit(solution)/shard_map/ppermute | solution.py:353
  372.4 107.7 %collective-permute-start.37 = (bf16[256,1024]{1,0:T(8,128)(2,1)}, bf16[256,1024]{1,0:T(8,128)(2,1)}, u32[]{:S(2)}, u32[]{:S(2)}) collective-permute-start(bf16[256,1024]{1,0:T(8,128)(2,1)} %maximum_select_fusion.1), channel_id=1, source_target_pairs={{0,4},{2,6},{4,12},{6,14},{8,0},{10,2},{12,8},{14,10},{1,5},{3,7},... | collective-permute-start | bytes 1572872 | tf_op jit(solution)/shard_map/ppermute | solution.py:516
  374.6 108.0 %collective-permute-start.39 = (bf16[256,1024]{1,0:T(8,128)(2,1)}, bf16[256,1024]{1,0:T(8,128)(2,1)}, u32[]{:S(2)}, u32[]{:S(2)}) collective-permute-start(bf16[256,1024]{1,0:T(8,128)(2,1)} %maximum_select_fusion.1), channel_id=1, source_target_pairs={{0,6},{2,0},{4,14},{6,8},{8,2},{10,4},{12,10},{14,12},{1,7},{3,1},... | collective-permute-start | bytes 1572872 | tf_op jit(solution)/shard_map/ppermute | solution.py:516
  389.3 11.6 %collective-permute-start.81 = (bf16[256,256]{1,0:T(8,128)(2,1)S(1)}, bf16[256,256]{1,0:T(8,128)(2,1)S(1)}, u32[]{:S(2)}, u32[]{:S(2)}) collective-permute-start(bf16[256,256]{1,0:T(8,128)(2,1)S(1)} %select_convert_fusion.1), channel_id=1, source_target_pairs={{0,8},{8,0},{1,9},{9,1},{2,10},{10,2},{3,11},{11,3},{4,12},{12,4},... | collective-permute-start | bytes 393224 | tf_op jit(solution)/shard_map/ppermute | solution.py:353
  396.4 17.8 %collective-permute-start.47 = (bf16[512,1024]{1,0:T(8,128)(2,1)S(1)}, bf16[512,1024]{1,0:T(8,128)(2,1)S(1)}, u32[]{:S(2)}, u32[]{:S(2)}) collective-permute-start(bf16[512,1024]{1,0:T(8,128)(2,1)S(1)} %pad_maximum_fusion.8), channel_id=1, source_target_pairs={{0,8},{8,0},{1,9},{9,1},{2,10},{10,2},{3,11},{11,3},{4,12},{12,4},... | collective-permute-start | bytes 3145736 | tf_op jit(solution)/shard_map/ppermute | solution.py:353
  456.1 27.9 %collective-permute-start.58 = (bf16[528,256]{1,0:T(8,128)(2,1)S(1)}, bf16[528,256]{1,0:T(8,128)(2,1)S(1)}, u32[]{:S(2)}, u32[]{:S(2)}) collective-permute-start(bf16[528,256]{1,0:T(8,128)(2,1)S(1)} %fusion.76), channel_id=1, source_target_pairs={{0,16},{16,0},{1,17},{17,1},{2,18},{18,2},{3,19},{19,3},{4,20},{20... | collective-permute-start | bytes 811016 | tf_op jit(solution)/shard_map/ppermute | solution.py:353
  457.7 15.2 %collective-permute-start.61 = (bf16[528,256]{1,0:T(8,128)(2,1)S(1)}, bf16[528,256]{1,0:T(8,128)(2,1)S(1)}, u32[]{:S(2)}, u32[]{:S(2)}) collective-permute-start(bf16[528,256]{1,0:T(8,128)(2,1)S(1)} %fusion.78), channel_id=1, source_target_pairs={{0,16},{16,0},{1,17},{17,1},{2,18},{18,2},{3,19},{19,3},{4,20},{20... | collective-permute-start | bytes 811016 | tf_op jit(solution)/shard_map/ppermute | solution.py:353
  467.1 11.6 %collective-permute-start.63 = (bf16[528,256]{1,0:T(8,128)(2,1)S(1)}, bf16[528,256]{1,0:T(8,128)(2,1)S(1)}, u32[]{:S(2)}, u32[]{:S(2)}) collective-permute-start(bf16[528,256]{1,0:T(8,128)(2,1)S(1)} %fusion.79), channel_id=1, source_target_pairs={{0,16},{16,0},{1,17},{17,1},{2,18},{18,2},{3,19},{19,3},{4,20},{20... | collective-permute-start | bytes 811016 | tf_op jit(solution)/shard_map/ppermute | solution.py:353
  472.9 11.2 %collective-permute-start.60 = (bf16[528,256]{1,0:T(8,128)(2,1)S(1)}, bf16[528,256]{1,0:T(8,128)(2,1)S(1)}, u32[]{:S(2)}, u32[]{:S(2)}) collective-permute-start(bf16[528,256]{1,0:T(8,128)(2,1)S(1)} %fusion.39), channel_id=1, source_target_pairs={{0,6},{2,0},{4,2},{6,4},{1,7},{3,1},{5,3},{7,5},{8,14},{10,8},{12,... | collective-permute-start | bytes 811016 | tf_op jit(solution)/shard_map/ppermute | solution.py:357
  478.7 15.7 %collective-permute-start.62 = (bf16[528,256]{1,0:T(8,128)(2,1)S(1)}, bf16[528,256]{1,0:T(8,128)(2,1)S(1)}, u32[]{:S(2)}, u32[]{:S(2)}) collective-permute-start(bf16[528,256]{1,0:T(8,128)(2,1)S(1)} %fusion.37), channel_id=1, source_target_pairs={{0,4},{2,6},{4,0},{6,2},{1,5},{3,7},{5,1},{7,3},{8,12},{10,14},{12... | collective-permute-start | bytes 811016 | tf_op jit(solution)/shard_map/ppermute | solution.py:357
  480.1 20.1 %collective-permute-start.64 = (bf16[528,256]{1,0:T(8,128)(2,1)S(1)}, bf16[528,256]{1,0:T(8,128)(2,1)S(1)}, u32[]{:S(2)}, u32[]{:S(2)}) collective-permute-start(bf16[528,256]{1,0:T(8,128)(2,1)S(1)} %fusion.35), channel_id=1, source_target_pairs={{0,2},{2,4},{4,6},{6,0},{1,3},{3,5},{5,7},{7,1},{8,10},{10,12},{12... | collective-permute-start | bytes 811016 | tf_op jit(solution)/shard_map/ppermute | solution.py:357
  482.6 35.9 %collective-permute-start.38 = (bf16[256,1024]{1,0:T(8,128)(2,1)}, bf16[256,1024]{1,0:T(8,128)(2,1)}, u32[]{:S(2)}, u32[]{:S(2)}) collective-permute-start(bf16[256,1024]{1,0:T(8,128)(2,1)} %collective-permute-done.37), channel_id=1, source_target_pairs={{0,1},{1,0},{2,3},{3,2},{4,5},{5,4},{6,7},{7,6},{8,9},{9,8},{10,11... | collective-permute-start | bytes 1572872 | tf_op jit(solution)/shard_map/ppermute | solution.py:353
  483.9 41.3 %collective-permute-start.40 = (bf16[256,1024]{1,0:T(8,128)(2,1)}, bf16[256,1024]{1,0:T(8,128)(2,1)}, u32[]{:S(2)}, u32[]{:S(2)}) collective-permute-start(bf16[256,1024]{1,0:T(8,128)(2,1)} %collective-permute-done.39), channel_id=1, source_target_pairs={{0,1},{1,0},{2,3},{3,2},{4,5},{5,4},{6,7},{7,6},{8,9},{9,8},{10,11... | collective-permute-start | bytes 1572872 | tf_op jit(solution)/shard_map/ppermute | solution.py:353
  517.1 13.9 %collective-permute-start.48 = (bf16[512,1024]{1,0:T(8,128)(2,1)S(1)}, bf16[512,1024]{1,0:T(8,128)(2,1)S(1)}, u32[]{:S(2)}, u32[]{:S(2)}) collective-permute-start(bf16[512,1024]{1,0:T(8,128)(2,1)S(1)} %convolution_convert_fusion), channel_id=1, source_target_pairs={{0,8},{8,0},{1,9},{9,1},{2,10},{10,2},{3,11},{11,3},{4,12},{12,4},... | collective-permute-start | bytes 3145736 | tf_op jit(solution)/shard_map/ppermute | solution.py:353
  543.6 39.6 %collective-permute-start.50 = (bf16[256,1024]{1,0:T(8,128)(2,1)S(1)}, bf16[256,1024]{1,0:T(8,128)(2,1)S(1)}, u32[]{:S(2)}, u32[]{:S(2)}) collective-permute-start(bf16[256,1024]{1,0:T(8,128)(2,1)S(1)} %maximum_select_fusion.3), channel_id=1, source_target_pairs={{0,0},{2,2},{4,8},{6,10},{8,4},{10,6},{12,12},{14,14},{1,1},{3,3},... | collective-permute-start | bytes 1572872 | tf_op jit(solution)/shard_map/ppermute | solution.py:516
  552.7 42.2 %collective-permute-start.52 = (bf16[256,1024]{1,0:T(8,128)(2,1)S(1)}, bf16[256,1024]{1,0:T(8,128)(2,1)S(1)}, u32[]{:S(2)}, u32[]{:S(2)}) collective-permute-start(bf16[256,1024]{1,0:T(8,128)(2,1)S(1)} %maximum_select_fusion.3), channel_id=1, source_target_pairs={{0,2},{2,4},{4,10},{6,12},{8,6},{10,0},{12,14},{14,8},{1,3},{3,5},... | collective-permute-start | bytes 1572872 | tf_op jit(solution)/shard_map/ppermute | solution.py:516
  552.7 42.4 %collective-permute-start.54 = (bf16[256,1024]{1,0:T(8,128)(2,1)S(1)}, bf16[256,1024]{1,0:T(8,128)(2,1)S(1)}, u32[]{:S(2)}, u32[]{:S(2)}) collective-permute-start(bf16[256,1024]{1,0:T(8,128)(2,1)S(1)} %maximum_select_fusion.3), channel_id=1, source_target_pairs={{0,4},{2,6},{4,12},{6,14},{8,0},{10,2},{12,8},{14,10},{1,5},{3,7},... | collective-permute-start | bytes 1572872 | tf_op jit(solution)/shard_map/ppermute | solution.py:516
  552.7 43.7 %collective-permute-start.56 = (bf16[256,1024]{1,0:T(8,128)(2,1)S(1)}, bf16[256,1024]{1,0:T(8,128)(2,1)S(1)}, u32[]{:S(2)}, u32[]{:S(2)}) collective-permute-start(bf16[256,1024]{1,0:T(8,128)(2,1)S(1)} %maximum_select_fusion.3), channel_id=1, source_target_pairs={{0,6},{2,0},{4,14},{6,8},{8,2},{10,4},{12,10},{14,12},{1,7},{3,1},... | collective-permute-start | bytes 1572872 | tf_op jit(solution)/shard_map/ppermute | solution.py:516
  583.3 14.5 %collective-permute-start.51 = (bf16[256,1024]{1,0:T(8,128)(2,1)S(1)}, bf16[256,1024]{1,0:T(8,128)(2,1)S(1)}, u32[]{:S(2)}, u32[]{:S(2)}) collective-permute-start(bf16[256,1024]{1,0:T(8,128)(2,1)S(1)} %collective-permute-done.50), channel_id=1, source_target_pairs={{0,1},{1,0},{2,3},{3,2},{4,5},{5,4},{6,7},{7,6},{8,9},{9,8},{10,11... | collective-permute-start | bytes 1572872 | tf_op jit(solution)/shard_map/ppermute | solution.py:353
  594.9 11.8 %collective-permute-start.53 = (bf16[256,1024]{1,0:T(8,128)(2,1)S(1)}, bf16[256,1024]{1,0:T(8,128)(2,1)S(1)}, u32[]{:S(2)}, u32[]{:S(2)}) collective-permute-start(bf16[256,1024]{1,0:T(8,128)(2,1)S(1)} %collective-permute-done.52), channel_id=1, source_target_pairs={{0,1},{1,0},{2,3},{3,2},{4,5},{5,4},{6,7},{7,6},{8,9},{9,8},{10,11... | collective-permute-start | bytes 1572872 | tf_op jit(solution)/shard_map/ppermute | solution.py:353
  595.1 22.8 %collective-permute-start.55 = (bf16[256,1024]{1,0:T(8,128)(2,1)S(1)}, bf16[256,1024]{1,0:T(8,128)(2,1)S(1)}, u32[]{:S(2)}, u32[]{:S(2)}) collective-permute-start(bf16[256,1024]{1,0:T(8,128)(2,1)S(1)} %collective-permute-done.54), channel_id=1, source_target_pairs={{0,1},{1,0},{2,3},{3,2},{4,5},{5,4},{6,7},{7,6},{8,9},{9,8},{10,11... | collective-permute-start | bytes 1572872 | tf_op jit(solution)/shard_map/ppermute | solution.py:353
  596.4 29.0 %collective-permute-start.57 = (bf16[256,1024]{1,0:T(8,128)(2,1)S(1)}, bf16[256,1024]{1,0:T(8,128)(2,1)S(1)}, u32[]{:S(2)}, u32[]{:S(2)}) collective-permute-start(bf16[256,1024]{1,0:T(8,128)(2,1)S(1)} %collective-permute-done.56), channel_id=1, source_target_pairs={{0,1},{1,0},{2,3},{3,2},{4,5},{5,4},{6,7},{7,6},{8,9},{9,8},{10,11... | collective-permute-start | bytes 1572872 | tf_op jit(solution)/shard_map/ppermute | solution.py:353
  (147 other events, 2120.2 us)

commit v2 on v1

--- a/solution.py
+++ b/solution.py
@@ -370,29 +370,6 @@
     )
 
 
-def attend_kernel(length, head_size, block, emb_ref, weight_ref, bias_ref, col_ref, row_ref, proj_ref, ctx_ref):
-    width = 3 * head_size
-    proj = jnp.dot(emb_ref[...], weight_ref[0], preferred_element_type=jnp.float32)
-    proj_ref[0] = (proj[:, :width] + bias_ref[0, 0:1, :width]).astype(jnp.bfloat16)
-    keys = proj_ref[0, :, head_size : 2 * head_size]
-    values = proj_ref[0, :, 2 * head_size : width]
-
-    def one_block(at, carry):
-        rows = pl.ds(pl.multiple_of(at * block, block), block)
-        queries = proj_ref[0, rows, 0:head_size] * jnp.bfloat16(head_size**-0.5)
-        scores = lax.dot_general(queries, keys, ROW_PAIR, preferred_element_type=jnp.float32)
-        scores = jnp.where(col_ref[rows, :] == row_ref[...], scores, -1e30)
-        highest = jnp.max(scores, axis=1, keepdims=True)
-        exponent = jnp.exp(scores - highest)
-        totals = jnp.sum(exponent, axis=1, keepdims=True)
-        probability = (exponent * (1.0 / totals)).astype(jnp.bfloat16)
-        ctx = jnp.dot(probability, values, preferred_element_type=jnp.float32)
-        ctx_ref[0, rows, :] = ctx.astype(jnp.bfloat16)
-        return carry
-
-    lax.fori_loop(0, length // block, one_block, 0)
-
-
 def attend_back_kernel(length, head_size, block, proj_ref, grad_ref, col_ref, row_ref, out_ref, key_sum, value_sum):
     width = 3 * head_size
     keys = proj_ref[0, :, head_size : 2 * head_size]
@@ -424,36 +401,6 @@
     lax.fori_loop(0, length // block, one_block, 0)
     out_ref[0, :, head_size : 2 * head_size] = key_sum[...].astype(jnp.bfloat16)
     out_ref[0, :, 2 * head_size : width] = value_sum[...].astype(jnp.bfloat16)
-
-
-def attend_all(emb_low, weights, biases, segments, head_size):
-    heads, depth, packed = weights.shape
-    length = emb_low.shape[0]
-    whole = lambda shape: pl.BlockSpec(shape, lambda h: (0, 0))
-    each = lambda shape: pl.BlockSpec((1,) + shape, lambda h: (h, 0, 0))
-    return pl.pallas_call(
-        partial(attend_kernel, length, head_size, 256),
-        grid=(heads,),
-        in_specs=[
-            whole((length, depth)),
-            each((depth, packed)),
-            each((8, packed)),
-            whole((length, 1)),
-            whole((1, length)),
-        ],
-        out_specs=[each((length, 3 * head_size)), each((length, head_size))],
-        out_shape=[
-            jax.ShapeDtypeStruct((heads, length, 3 * head_size), jnp.bfloat16),
-            jax.ShapeDtypeStruct((heads, length, head_size), jnp.bfloat16),
-        ],
-        compiler_params=pltpu.CompilerParams(vmem_limit_bytes=48 << 20),
-        cost_estimate=pl.CostEstimate(
-            flops=2 * heads * length * (depth * packed + 2 * length * 128),
-            bytes_accessed=8 << 20,
-            transcendentals=heads * length * length,
-        ),
-        name="attend_all",
-    )(emb_low, weights, biases, segments[:, None], segments[None, :])
 
 
 def attend_all_back(proj, grad_ctx, segments, head_size):
@@ -485,6 +432,384 @@
     )(proj, grad_ctx, segments[:, None], segments[None, :])
 
 
+MESH_ID = pl.DeviceIdType.MESH
+TILE = 16
+
+
+class Wires:
+    def __init__(self, sends, receives):
+        self.sends, self.receives, self.used = sends, receives, 0
+
+    def make(self, source, target, **device):
+        at = self.used
+        self.used += 1
+        return pltpu.make_async_remote_copy(
+            src_ref=source,
+            dst_ref=target,
+            send_sem=self.sends.at[at],
+            recv_sem=self.receives.at[at],
+            device_id=device,
+            device_id_type=MESH_ID,
+        )
+
+
+def spots():
+    return (lax.axis_index("x"), lax.axis_index("core"), lax.axis_index("z"), lax.axis_index("y"))
+
+
+def greet(full):
+    at_x, at_core, at_z, at_y = spots()
+    barrier = pltpu.get_barrier_semaphore()
+    count = 0
+
+    def call(**device):
+        pl.semaphore_signal(barrier, inc=1, device_id=device, device_id_type=MESH_ID)
+
+    for step in range(4):
+        if step:
+            call(z=lax.rem(at_z + step, 4))
+            count += 1
+        if full or step == 0:
+            call(core=1 - at_core, z=lax.rem(at_z + step, 4))
+            count += 1
+    call(x=1 - at_x)
+    call(y=1 - at_y)
+    pl.semaphore_wait(barrier, count + 2)
+
+
+def flipped(value, bit):
+    return 1 - value if bit else value
+
+
+def row_loop(count, step, body):
+    def inner(at, carry):
+        body(pl.ds(pl.multiple_of(at * step, step), step))
+        return carry
+
+    lax.fori_loop(0, count // step, inner, 0)
+
+
+def block_loop(count, body):
+    def inner(at, carry):
+        body(at)
+        return carry
+
+    lax.fori_loop(0, count, inner, 0)
+
+
+def dot_f32(left, right, pairing=(((1,), (0,)), ((), ()))):
+    return lax.dot_general(left, right, pairing, preferred_element_type=jnp.float32)
+
+
+def spread_rows(wires, ref, quarter):
+    _, at_core, _, at_y = spots()
+    own, near = ref.at[pl.ds(0, quarter)], ref.at[pl.ds(quarter, quarter)]
+    to_y = wires.make(own, near, y=1 - at_y)
+    to_core = wires.make(own, ref.at[pl.ds(2 * quarter, quarter)], core=1 - at_core)
+    again = wires.make(near, ref.at[pl.ds(3 * quarter, quarter)], core=1 - at_core)
+    to_y.start()
+    to_core.start()
+    return to_y, to_core, again
+
+
+def add_rows(wires, part, keep, acc, bufs, fill=None):
+    _, at_core, _, at_y = spots()
+    send_c, recv_c, send_y, recv_y = bufs
+    low = jnp.bfloat16
+    half = keep.shape[1] // 2
+    sides = [pl.ds(0, half), pl.ds(half, half)]
+    far = [wires.make(send_c.at[b], recv_c.at[b], core=1 - at_core) for b in range(2)]
+    across = wires.make(send_y, recv_y, y=1 - at_y)
+    for b, r in ((1, 3), (0, 2)):
+        for side in range(2):
+            send_c[b, :, sides[side]] = part(r, side).astype(low)
+        far[b].start()
+    for side in range(2):
+        acc[:, sides[side]] = part(1, side)
+    far[1].wait_recv()
+
+    def to_send(rows):
+        send_y[rows, :] = (acc[rows, :] + recv_c[1, rows, :].astype(jnp.float32)).astype(low)
+
+    row_loop(keep.shape[0], 32, to_send)
+    across.start()
+    for side in range(2):
+        keep[:, sides[side]] = part(0, side)
+    far[0].wait_recv()
+    if fill is not None:
+        fill()
+    across.wait_recv()
+
+    def finish(rows):
+        keep[rows, :] += recv_c[0, rows, :].astype(jnp.float32) + recv_y[rows, :].astype(jnp.float32)
+
+    row_loop(keep.shape[0], 32, finish)
+    far[0].wait_send()
+    far[1].wait_send()
+    across.wait_send()
+
+
+def front_kernel(
+    head_piece, up_piece, down_piece, tokens, time_row, ids_col, ids_row,
+    w_head, w_up, w_down, emb, proj, ctx, w_out, hid, pre, act, normed_one, inverse_one, hidden, summed, vecs,
+    tok, send_c, recv_c, send_y, recv_y, keep, acc, send_sem, recv_sem, local_sem,
+):
+    at_x, at_core, at_z, at_y = spots()
+    low, f32 = jnp.bfloat16, jnp.float32
+    length, width = emb.shape
+    quarter, half = length // 4, width // 2
+    zs = w_head.shape[0]
+    span = half + 2 * TILE
+    head_size = ctx.shape[2]
+    in_size = 3 * head_size
+    wires = Wires(send_sem, recv_sem)
+    greet(False)
+
+    kept, lent = [], []
+    for at, (piece, target) in enumerate(((head_piece, w_head), (up_piece, w_up), (down_piece, w_down))):
+        size = piece.shape[1]
+        place = target.at[0, 0, pl.ds(pl.multiple_of(at_core * size, size), size)]
+        local = pltpu.make_async_copy(piece.at[at_core], place, local_sem.at[at])
+        local.start()
+        remote = wires.make(piece.at[1 - at_core], place, core=1 - at_core)
+        remote.start()
+        kept.append(local)
+        lent.append(remote)
+    turns, cross = [], []
+    for target in (w_head, w_up, w_down):
+        turns.append(
+            [None]
+            + [wires.make(target.at[0, 0], target.at[s, 0], z=lax.rem(at_z + s, zs)) for s in range(1, zs)]
+        )
+        cross.append([wires.make(target.at[s, 0], target.at[s, 1], x=1 - at_x) for s in range(zs)])
+
+    holds = at_core == lax.div(at_z, 2)
+    start = lax.rem(at_z, 2) * length
+    here, there = [], []
+    for r in range(4):
+        for h in range(2):
+            spot = tok.at[pl.ds(r * quarter, quarter), pl.ds(pl.multiple_of(flipped(at_x, h) * half, half), half)]
+
+            def source(core):
+                at = flipped(core, r // 2) * 2 + flipped(at_y, r % 2)
+                return tokens.at[pl.ds(pl.multiple_of(start + at * quarter, quarter), quarter), pl.ds(h * half, half)]
+
+            here.append(pltpu.make_async_copy(source(at_core), spot, local_sem.at[3 + 2 * r + h]))
+            there.append(wires.make(source(1 - at_core), spot, core=1 - at_core))
+
+    @pl.when(holds)
+    def _():
+        for near, far in zip(here, there):
+            near.start()
+            far.start()
+
+    for at in range(3):
+        kept[at].wait()
+        lent[at].wait_recv()
+        for s in range(1, zs):
+            turns[at][s].start()
+        if at == 0:
+            cross[0][0].start()
+
+    @pl.when(holds)
+    def _():
+        for near in here:
+            near.wait()
+
+    @pl.when(jnp.logical_not(holds))
+    def _():
+        for far in there:
+            far.wait_recv()
+
+    def embed(rows):
+        emb[rows, :] = (tok[rows, :].astype(f32) + time_row[...]).astype(low)
+
+    row_loop(length, 32, embed)
+
+    def forward(at, s):
+        turns[at][s].wait_recv()
+        cross[at][s].start()
+
+    def small(s, side):
+        size = half // 2 + TILE
+        return (
+            w_head[s, side, half // 2 : size, :].astype(f32)
+            + w_head[s, side, size + half // 2 : 2 * size, :].astype(f32)
+        )
+
+    for s in range(zs):
+        if s + 1 < zs:
+            forward(0, s + 1)
+        if s == 2:
+            cross[1][0].start()
+            cross[2][0].start()
+        cross[0][s].wait_recv()
+        bias = (small(s, 0) + small(s, 1))[0:1, :in_size]
+        size = half // 2 + TILE
+
+        def project(rows):
+            total = bias
+            for side in range(2):
+                for core in range(2):
+                    at = side * half + core * (half // 2)
+                    total = total + dot_f32(
+                        emb[rows, at : at + half // 2],
+                        w_head[s, side, core * size : core * size + half // 2, :],
+                    )[:, :in_size]
+            proj[s, rows, :] = total.astype(low)
+
+        row_loop(length, quarter, project)
+        for side in range(2):
+            for core in range(2):
+                w_out[side, core * (half // 2) : (core + 1) * (half // 2), s * head_size : (s + 1) * head_size] = w_head[
+                    s, side, core * size : core * size + half // 2, in_size:
+                ]
+        keys = proj[s, :, head_size : 2 * head_size]
+        values = proj[s, :, 2 * head_size : in_size]
+
+        def attend(rows):
+            queries = proj[s, rows, 0:head_size] * jnp.bfloat16(head_size**-0.5)
+            scores = dot_f32(queries, keys, ROW_PAIR)
+            scores = jnp.where(ids_col[rows, :] == ids_row[...], scores, -1e30)
+            highest = jnp.max(scores, axis=1, keepdims=True)
+            exponent = jnp.exp(scores - highest)
+            totals = jnp.sum(exponent, axis=1, keepdims=True)
+            probability = (exponent * (1.0 / totals)).astype(low)
+            ctx[s, rows, :] = dot_f32(probability, values).astype(low)
+
+        row_loop(length, quarter, attend)
+
+    for side in range(2):
+        tile = small(0, side)
+        for k in range(6):
+            vecs[k : k + 1, side * half : side * half + half // 2] = tile[2 + k : 3 + k, :]
+            vecs[k : k + 1, side * half + half // 2 : (side + 1) * half] = tile[8 + k : 9 + k, :]
+
+    for s in range(1, zs):
+        forward(1, s)
+    bufs = (send_c, recv_c, send_y, recv_y)
+
+    def mixed_part(r, side):
+        joined = jnp.concatenate([ctx[s, r * quarter : (r + 1) * quarter, :] for s in range(zs)], axis=1)
+        return dot_f32(joined, w_out[side], ROW_PAIR)
+
+    add_rows(wires, mixed_part, keep, acc, bufs)
+
+    def first_norm(rows):
+        total = tok[rows, :].astype(f32) + time_row[...] + keep[rows, :] + vecs[2:3, :]
+        normed, inverse = norm_stats(total)
+        normed_one[rows, :] = normed
+        inverse_one[rows, :] = inverse
+        value = normed * vecs[0:1, :] + vecs[3:4, :]
+        hidden[rows, :] = value
+        hid[rows, :] = value.astype(low)
+
+    row_loop(quarter, 32, first_norm)
+    to_y, to_core, again = spread_rows(wires, hid, quarter)
+    for s in range(1, zs):
+        forward(2, s)
+    for s in range(zs):
+        cross[1][s].wait_recv()
+
+    def up(r):
+        rows = pl.ds(r * quarter, quarter)
+
+        def one(s):
+            lanes = pl.ds(pl.multiple_of(s * (half // 2), half // 2), half // 2)
+            shift = (small(s, 0) + small(s, 1))[1:2, :]
+            value = dot_f32(hid[rows, 0:half], w_up[s, 0]) + dot_f32(hid[rows, half:], w_up[s, 1]) + shift
+            pre[rows, lanes] = value
+            act[rows, lanes] = gelu_value(value).astype(low)
+
+        block_loop(zs, one)
+
+    up(0)
+    to_core.wait_recv()
+    up(2)
+    to_y.wait_recv()
+    again.start()
+    up(1)
+    again.wait_recv()
+    up(3)
+    for s in range(zs):
+        cross[2][s].wait_recv()
+
+    def down_part(r, side):
+        rows = pl.ds(r * quarter, quarter)
+        total = dot_f32(act[rows, 0 : half // 2], w_down[0, side], ROW_PAIR)
+        for s in range(1, zs):
+            total = total + dot_f32(act[rows, s * (half // 2) : (s + 1) * (half // 2)], w_down[s, side], ROW_PAIR)
+        return total
+
+    add_rows(wires, down_part, keep, acc, bufs)
+
+    def second(rows):
+        summed[rows, :] = hidden[rows, :] + keep[rows, :] + vecs[4:5, :]
+
+    row_loop(quarter, 32, second)
+    for at in range(3):
+        lent[at].wait_send()
+        for s in range(zs):
+            if s:
+                turns[at][s].wait_send()
+            cross[at][s].wait_send()
+
+    @pl.when(holds)
+    def _():
+        for far in there:
+            far.wait_send()
+
+    for member in (to_y, to_core, again):
+        member.wait_send()
+
+
+def run_front(pieces, tokens, time_row, ids, head_size):
+    low, f32 = jnp.bfloat16, jnp.float32
+    length, width = ids.shape[0], tokens.shape[1]
+    quarter, half, zs = length // 4, width // 2, 4
+    blocks = pieces[1].shape[2]
+    vmem = pl.BlockSpec(memory_space=pltpu.VMEM)
+    shapes = [
+        ((zs, 2, half + 2 * TILE, 4 * head_size), low),
+        ((zs, 2, half, blocks), low),
+        ((zs, 2, half, blocks), low),
+        ((length, width), low),
+        ((zs, length, 3 * head_size), low),
+        ((zs, length, head_size), low),
+        ((2, half, zs * head_size), low),
+        ((length, width), low),
+        ((length, zs * blocks), f32),
+        ((length, zs * blocks), low),
+        ((quarter, width), f32),
+        ((quarter, 1), f32),
+        ((quarter, width), f32),
+        ((quarter, width), f32),
+        ((8, width), f32),
+    ]
+    return pl.pallas_call(
+        front_kernel,
+        out_shape=[jax.ShapeDtypeStruct(*s) for s in shapes],
+        in_specs=[vmem] * 3 + [pl.BlockSpec(memory_space=pl.ANY)] + [vmem] * 3,
+        out_specs=[vmem] * len(shapes),
+        scratch_shapes=[
+            pltpu.VMEM((length, width), low),
+            pltpu.VMEM((2, quarter, width), low),
+            pltpu.VMEM((2, quarter, width), low),
+            pltpu.VMEM((quarter, width), low),
+            pltpu.VMEM((quarter, width), low),
+            pltpu.VMEM((quarter, width), f32),
+            pltpu.VMEM((quarter, width), f32),
+            pltpu.SemaphoreType.DMA((64,)),
+            pltpu.SemaphoreType.DMA((64,)),
+            pltpu.SemaphoreType.DMA((16,)),
+        ],
+        compiler_params=pltpu.CompilerParams(
+            collective_id=0, has_side_effects=True, vmem_limit_bytes=60 << 20
+        ),
+        name="front",
+    )(*pieces, tokens, time_row, ids[:, None], ids[None, :])
+
+
 def spread_tokens(own):
     near = flip(own, "y")
     pair = jnp.concatenate([own, near], axis=0)
@@ -557,6 +882,12 @@
     packed = 4 * head_size
     small_rows = head_bias.shape[0]
 
+    position = at_x * 2 + at_core
+    vectors = jnp.concatenate([norm_gains, branch_biases], axis=1).T
+    vectors = lax.dynamic_update_slice(
+        jnp.zeros((TILE, rows), f32), vectors, (2 + 6 * at_core, 0)
+    )
+
     def head_piece(half):
         body = jnp.concatenate(
             [
@@ -565,35 +896,22 @@
             ],
             axis=1,
         )
-        shifts = jnp.concatenate(
-            [head_bias[:, half : half + 1], hidden_bias[:, 2 * half : 2 * half + 2]], axis=1
-        ).T
-        shifts = jnp.pad(shifts, ((0, 0), (0, packed - small_rows)))
-        vectors = jnp.concatenate([norm_gains, branch_biases], axis=1).T
-        vectors = jnp.pad(vectors, ((0, 7), (0, packed - rows)))
-        return jnp.concatenate([body, shifts, vectors], axis=0).astype(low)
-
-    def column_piece(weight):
-        return lambda half: weight[:, half * wide : (half + 1) * wide].astype(low)
-
-    def pair_cores(piece):
-        zero, one = piece(0), piece(1)
-        mine = jnp.where(first_core, zero, one)
-        other = flip(jnp.where(first_core, one, zero), "core")
-        return mine, other
-
-    def spread(block):
-        came = [block] + [turn(block, step, zs) for step in range(1, zs)]
-        return came, [flip(member, "x") for member in came]
-
-    mine, other = pair_cores(head_piece)
-    head_block = jnp.concatenate(
-        [in_order(first_core, mine[:rows], other[:rows]), in_order(first_core, mine[rows:], other[rows:])],
-        axis=0,
-    )
-    head_own, head_far = spread(head_block)
-    up_own, up_far = spread(in_order(first_core, *pair_cores(column_piece(upward_weight))))
-    down_own, down_far = spread(in_order(first_core, *pair_cores(column_piece(downward_weight))))
+        tile = lax.dynamic_update_slice(
+            vectors, head_bias[:, half][None], (0, at_x * 2 * head_size + at_core * small_rows)
+        )
+        units = lax.dynamic_update_slice(
+            jnp.zeros((2, 4 * small_rows), f32),
+            hidden_bias[:, 2 * half : 2 * half + 2].T,
+            (0, position * small_rows),
+        )
+        tile = lax.dynamic_update_slice(tile, units.reshape(1, -1), (1, 0))
+        return jnp.concatenate([body, tile], axis=0)
+
+    pieces = [
+        jnp.stack([head_piece(0), head_piece(1)]).astype(low),
+        jnp.stack([upward_weight[:, :wide], upward_weight[:, wide:]]).astype(low),
+        jnp.stack([downward_weight[:, :wide], downward_weight[:, wide:]]).astype(low),
+    ]
 
     seat = ("core", "z")
     holds = at_core == at_z // 2
@@ -603,8 +921,6 @@
         return jnp.where(holds, kept, lax.ppermute(sent, seat, lend))
 
     local = at_z % 2
-    own_tokens = lax.dynamic_slice_in_dim(tokens, local * length, length, 0)
-    own_tokens = borrow(own_tokens, own_tokens)
     own_time = lax.dynamic_slice_in_dim(time_embed, local, 1, 0)
     own_time = borrow(own_time, own_time)
     own_ids = lax.dynamic_slice_in_dim(segment_ids, local, 1, 0)
@@ -622,62 +938,27 @@
             axis=0,
         )
 
-    embedded_all = swap_halves(
-        relative(own_tokens).astype(f32) + own_time.astype(f32), swapped
-    )
-    embedded = embedded_all[:quarter]
-    embedded_low = embedded_all.astype(low)
+    time_row = swap_halves(own_time.astype(f32), swapped)
     segments = relative(own_ids)
 
     span = 2 * rows
-    small_own = [member[span:] for member in head_own]
-    small_far = [member[span:] for member in head_far]
-    weights_head = jnp.stack(
-        [jnp.concatenate([a[:span], b[:span]], axis=0) for a, b in zip(head_own, head_far)]
-    )
-    vectors = [
-        jnp.concatenate([member[3:9], member[19:25]], axis=1).astype(f32)
-        for member in (small_own[0], small_far[0])
-    ]
-    vectors = jnp.concatenate(vectors, axis=1)
+    (
+        weights_head, weights_up, weights_down, embedded_low, projected, context, weights_out, hidden_low,
+        pre_act, expanded_low, normed_one, inverse_one, hidden, summed_two, vectors,
+    ) = run_front(pieces, tokens, time_row, segments, head_size)
     gains, shifts = vectors[0:2], vectors[2:6]
-
-    def shift_rows(member):
-        return jnp.concatenate([member[0:3, :small_rows], member[16:19, :small_rows]], axis=1)
-
-    biases, unit_offset = [], []
-    for a, b in zip(small_own, small_far):
-        near, distant = shift_rows(a).astype(f32), shift_rows(b).astype(f32)
-        lower = jnp.where(first_x, near, distant)
-        upper = jnp.where(first_x, distant, near)
-        biases.append(
-            jnp.concatenate(
-                [lower[0], jnp.zeros((head_size,), f32), upper[0], jnp.zeros((head_size,), f32)]
-            )
-        )
-        unit_offset.append(jnp.concatenate([lower[1:], upper[1:]], axis=1).reshape(-1))
-    biases = jnp.broadcast_to(jnp.stack(biases)[:, None, :], (zs, 8, packed))
-    unit_offset = jnp.concatenate(unit_offset)
-
-    projected, context = attend_all(embedded_low, weights_head, biases, segments, head_size)
+    body = jnp.concatenate(
+        [weights_head[:, :, :rows], weights_head[:, :, rows + TILE : 2 * rows + TILE]], axis=2
+    ).reshape(zs, 2 * span, packed)
+    weights_in = jnp.concatenate([body[i, :, : 3 * head_size] for i in range(zs)], axis=1)
+    weights_out = weights_out.reshape(2 * span, zs * head_size)
     context_low = jnp.concatenate([context[i] for i in range(zs)], axis=1)
-    weights_in = jnp.concatenate([weights_head[i, :, : 3 * head_size] for i in range(zs)], axis=1)
-    weights_out = jnp.concatenate([weights_head[i, :, 3 * head_size :] for i in range(zs)], axis=1)
-    mixed = sum_tokens(context_low, weights_out, ROW_PAIR)
-    normed_one, inverse_one = norm_stats(embedded + mixed + shifts[0])
-    hidden = normed_one * gains[0] + shifts[1]
-    hidden_low = spread_tokens(hidden.astype(low))
-
-    def joined(own, far):
-        return jnp.concatenate(
-            [jnp.concatenate(own, axis=1), jnp.concatenate(far, axis=1)], axis=0
-        )
-
-    weights_up, weights_down = joined(up_own, up_far), joined(down_own, down_far)
-    pre_act = jnp.dot(hidden_low, weights_up, preferred_element_type=f32) + unit_offset
-    expanded_low = gelu_value(pre_act).astype(low)
-    reduced = sum_tokens(expanded_low, weights_down, ROW_PAIR)
-    normed_two, inverse_two = norm_stats(hidden + reduced + shifts[2])
+
+    def joined(blocks):
+        return jnp.concatenate([blocks[i].reshape(2 * span, wide) for i in range(zs)], axis=1)
+
+    weights_up, weights_down = joined(weights_up), joined(weights_down)
+    normed_two, inverse_two = norm_stats(summed_two)
     out = swap_halves((normed_two * gains[1] + shifts[3]).astype(low), swapped)
     block_output = spread_output(out, zs, low)
 

time: 640 us -> 559 us (0.87)
  the two profiles are of different devices: /device:TPU:9 before, /device:TPU:1 now
where the time goes in v2:
time: 559 us; the launch traced here: 551 us
  Pallas kernels  149 us (27%)
  waiting for transfers between devices  127 us (23%)
  starting transfers between devices  121 us (22%)
  local copies, waits for them, and re-layouts  66.4 us (12%)
  other arithmetic  53.6 us (10%)
  matrix products  24 us (4%)
  between operations  10.1 us (2%)
    pallas_call x1, Pallas kernels, run_front(): pl.pallas_call(front_kernel, out_shape=[jax.ShapeDtypeStruct(*s) for s in...  124 us
    ppermute x37, waiting for transfers between devices, flip(): return lax.ppermute(value, axis, [(0, 1), (1, 0)])  67.3 us
    ppermute x8, starting transfers between devices, spread_output(): came = lax.ppermute(own, ('core', 'z'), pairs)  45 us
    ppermute x9, starting transfers between devices, turn(): lax.ppermute(value, 'z', [(i, (i + amount) % count) for i in range(count)])  34.3 us
    ppermute x37, starting transfers between devices, flip(): return lax.ppermute(value, axis, [(0, 1), (1, 0)])  32.7 us
    ppermute x8, waiting for transfers between devices, spread_output(): came = lax.ppermute(own, ('core', 'z'), pairs)  31 us
    unnamed x235, local copies, waits for them, and re-layouts  29.9 us
    pallas_call x1, Pallas kernels, attend_all_back(): pl.pallas_call(partial(attend_back_kernel, length, head_size, 256), grid=...  25.4 us
  transfers between devices with their start and end apart: 61, of which 23 were waited for; matrix products, arithmetic and copies ran while one was open for 23% of the time, Pallas kernels for 27%

profile of v2, /device:TPU:1, one launch (start us, length us, event | category | flops | bytes accessed | tf_op | source)
XLA Modules:
  0.0 551.1 jit_solution(15392037082333820241)
XLA Ops:
  4.8 1.9 constant_dynamic-slice_fusion
  9.2 2.1 copy.285
  20.9 1.7 copy.274
  22.6 1.7 copy.275
  27.8 123.9 %front.1 = (bf16[4,2,544,256]{3,2,1,0:T(8,128)(2,1)}, bf16[4,2,512,256]{3,2,1,0:T(8,128)(2,1)}, bf16[4,2,512,256]{3,2,1,0:T(8,128)(2,1)}, bf16[1024,1024]{1,0:T(...) custom-call(bf16[2,272,256]{2,1,0:T(8,128)(2,1)} %pad_maximum_fusion, ...), custom_call_target="tpu_custom_call" | custom-call | tf_op jit(solution)/shard_map/front/pallas_call | solution.py:789
  154.0 1.6 multiply_reduce_fusion.2
  162.3 1.9 collective-permute-start.2
  165.6 8.7 %collective-permute-start.4 = (bf16[256,1024]{1,0:T(8,128)(2,1)}, bf16[256,1024]{1,0:T(8,128)(2,1)}, u32[]{:S(2)}, u32[]{:S(2)}) collective-permute-start(bf16[256,1024]{1,0:T(8,128)(2,1)} %maximum_select_fusion), channel_id=1, source_target_pairs={{0,2},{2,4},{4,10},{6,12},{8,6},{10,0},{12,14},{14,8},{1,3},{3,5},... | collective-permute-start | bytes 1572872 | tf_op jit(solution)/shard_map/ppermute | solution.py:841
  178.9 6.8 %collective-permute-done.4 = bf16[256,1024]{1,0:T(8,128)(2,1)} collective-permute-done((bf16[256,1024]{1,0:T(8,128)(2,1)}, bf16[256,1024]{1,0:T(8,128)(2,1)}, u32[]{:S(2)}, u32[]{:S(2)}) %collective-permute-start.4) | collective-permute-done | bytes 524320 | tf_op jit(solution)/shard_map/ppermute | solution.py:841
  186.9 2.7 broadcast_in_dim.12
  190.5 2.1 constant_dynamic-update-slice_fusion.6
  192.5 1.9 constant_dynamic-update-slice_fusion.5
  194.4 5.4 collective-permute-done.5
  200.7 4.7 convert_reduce_fusion
  205.5 2.3 convolution_convert_fusion.1
  209.8 4.5 fusion.133
  214.4 2.3 collective-permute-start.44
  218.3 2.5 fusion.132
  221.6 1.8 collective-permute-done.44
  224.6 4.4 collective-permute-done.46
  230.2 4.4 collective-permute-done.48
  236.1 10.0 %collective-permute-start.45 = (bf16[512,256]{0,1:T(8,128)(2,1)S(1)}, bf16[512,256]{0,1:T(8,128)(2,1)S(1)}, u32[]{:S(2)}, u32[]{:S(2)}) collective-permute-start(bf16[512,256]{0,1:T(8,128)(2,1)S(1)} %get-tuple-element.203), channel_id=1, source_target_pairs={{0,6},{2,0},{4,2},{6,4},{1,7},{3,1},{5,3},{7,5},{8,14},{10,8},{12,... | collective-permute-start | bytes 786440 | tf_op jit(solution)/shard_map/ppermute | solution.py:357
  246.1 2.5 convert_add_fusion.1
  249.7 1.8 collective-permute-done.38
  251.5 6.7 %collective-permute-start.49 = (bf16[512,256]{0,1:T(8,128)(2,1)S(1)}, bf16[512,256]{0,1:T(8,128)(2,1)S(1)}, u32[]{:S(2)}, u32[]{:S(2)}) collective-permute-start(bf16[512,256]{0,1:T(8,128)(2,1)S(1)} %get-tuple-element.204), channel_id=1, source_target_pairs={{0,2},{2,4},{4,6},{6,0},{1,3},{3,5},{5,7},{7,1},{8,10},{10,12},{12... | collective-permute-start | bytes 786440 | tf_op jit(solution)/shard_map/ppermute | solution.py:357
  260.3 9.0 %collective-permute-start.37 = (bf16[512,256]{0,1:T(8,128)(2,1)}, bf16[512,256]{0,1:T(8,128)(2,1)}, u32[]{:S(2)}, u32[]{:S(2)}) collective-permute-start(bf16[512,256]{0,1:T(8,128)(2,1)} %get-tuple-element.206), channel_id=1, source_target_pairs={{0,6},{2,0},{4,2},{6,4},{1,7},{3,1},{5,3},{7,5},{8,14},{10,8},{12,... | collective-permute-start | bytes 786440 | tf_op jit(solution)/shard_map/ppermute | solution.py:357
  272.9 2.2 collective-permute-start.6
  275.8 22.5 %collective-permute-start.8 = (bf16[256,1024]{1,0:T(8,128)(2,1)}, bf16[256,1024]{1,0:T(8,128)(2,1)}, u32[]{:S(2)}, u32[]{:S(2)}) collective-permute-start(bf16[256,1024]{1,0:T(8,128)(2,1)} %maximum_select_fusion), channel_id=1, source_target_pairs={{0,6},{2,0},{4,14},{6,8},{8,2},{10,4},{12,10},{14,12},{1,7},{3,1},... | collective-permute-start | bytes 1572872 | tf_op jit(solution)/shard_map/ppermute | solution.py:841
  298.3 3.1 collective-permute-done.39
  301.4 3.9 collective-permute-start.50
  305.3 1.5 fusion.66
  307.6 2.5 collective-permute-done.52
  311.5 2.9 collective-permute-done.53
  314.4 2.5 collective-permute-start.54
  317.0 2.0 collective-permute-done.54
  326.8 25.4 %attend_all_back.1 = bf16[4,1024,192]{2,1,0:T(8,128)(2,1)S(1)} custom-call(bf16[4,1024,192]{2,1,0:T(8,128)(2,1)S(1)} %copy-done.3, bf16[4,1024,64]{2,1,0:T(8,128)(2,1)S(1)} %pad_maximum_fusion.8.grad_ref, s32[1024,1]{1,0:T(8,128)S(1)} %copy-done, s32[1,1024]{1,0:T(1,128)S(1)} %bitcast.135), custom_call_target="tpu_custom_call" | custom-call | flops 5368709120 | bytes 8388608 | tf_op jit(solution)/shard_map/attend_all_back/pallas_call | solution.py:410
  353.8 1.9 fusion.134
  362.5 1.6 fusion.68
  364.1 1.7 fusion.52
  376.1 8.8 %collective-permute-done.28 = bf16[528,256]{0,1:T(8,128)(2,1)S(1)} collective-permute-done((bf16[528,256]{0,1:T(8,128)(2,1)S(1)}, bf16[528,256]{0,1:T(8,128)(2,1)S(1)}, u32[]{:S(2)}, u32[]{:S(2)}) %collective-permute-start.28) | collective-permute-done | bytes 270368 | tf_op jit(solution)/shard_map/ppermute | solution.py:353
  385.4 6.5 %collective-permute-done.30 = bf16[528,256]{0,1:T(8,128)(2,1)S(1)} collective-permute-done((bf16[528,256]{0,1:T(8,128)(2,1)S(1)}, bf16[528,256]{0,1:T(8,128)(2,1)S(1)}, u32[]{:S(2)}, u32[]{:S(2)}) %collective-permute-start.30) | collective-permute-done | bytes 270368 | tf_op jit(solution)/shard_map/ppermute | solution.py:353
  391.9 3.1 collective-permute-start.29
  395.1 3.8 collective-permute-done.32
  399.3 3.4 collective-permute-start.33
  402.9 1.4 collective-permute-start.9
  404.4 19.3 %collective-permute-done.31 = bf16[528,256]{0,1:T(8,128)(2,1)S(1)} collective-permute-done((bf16[528,256]{0,1:T(8,128)(2,1)S(1)}, bf16[528,256]{0,1:T(8,128)(2,1)S(1)}, u32[]{:S(2)}, u32[]{:S(2)}) %collective-permute-start.31) | collective-permute-done | bytes 270368 | tf_op jit(solution)/shard_map/ppermute | solution.py:357
  424.8 2.4 collective-permute-start.34
  437.7 1.9 constant_dynamic-update-slice_fusion.3
  439.8 2.6 convolution_convert_fusion
  443.7 1.9 constant_dynamic-update-slice_fusion.2
  445.8 2.0 constant_dynamic-update-slice_fusion.1
  448.2 2.6 collective-permute-start.60
  450.8 1.9 constant_dynamic-update-slice_fusion
  457.3 1.8 collective-permute-start.18
  460.2 7.5 %collective-permute-done.18 = bf16[256,1024]{1,0:T(8,128)(2,1)S(1)} collective-permute-done((bf16[256,1024]{1,0:T(8,128)(2,1)S(1)}, bf16[256,1024]{1,0:T(8,128)(2,1)S(1)}, u32[]{:S(2)}, u32[]{:S(2)}) %collective-permute-start.18) | collective-permute-done | bytes 524320 | tf_op jit(solution)/shard_map/ppermute | solution.py:353
  469.1 6.0 %collective-permute-start.19 = (bf16[256,1024]{1,0:T(8,128)(2,1)}, bf16[256,1024]{1,0:T(8,128)(2,1)}, u32[]{:S(2)}, u32[]{:S(2)}) collective-permute-start(bf16[256,1024]{1,0:T(8,128)(2,1)} %maximum_select_fusion.2), channel_id=1, source_target_pairs={{0,0},{2,2},{4,8},{6,10},{8,4},{10,6},{12,12},{14,14},{1,1},{3,3},... | collective-permute-start | bytes 1572872 | tf_op jit(solution)/shard_map/ppermute | solution.py:841
  475.6 2.5 collective-permute-start.21
  479.9 24.2 %collective-permute-done.19 = bf16[256,1024]{1,0:T(8,128)(2,1)} collective-permute-done((bf16[256,1024]{1,0:T(8,128)(2,1)}, bf16[256,1024]{1,0:T(8,128)(2,1)}, u32[]{:S(2)}, u32[]{:S(2)}) %collective-permute-start.19) | collective-permute-done | bytes 524320 | tf_op jit(solution)/shard_map/ppermute | solution.py:841
  504.1 1.5 collective-permute-start.20
  517.8 1.4 collective-permute-start.24
  523.9 8.1 %collective-permute-done.22 = bf16[256,1024]{1,0:T(8,128)(2,1)S(1)} collective-permute-done((bf16[256,1024]{1,0:T(8,128)(2,1)}, bf16[256,1024]{1,0:T(8,128)(2,1)S(1)}, u32[]{:S(2)}, u32[]{:S(2)}) %collective-permute-start.22) | collective-permute-done | bytes 524320 | tf_op jit(solution)/shard_map/ppermute | solution.py:353
  533.2 7.2 %collective-permute-done.24 = bf16[256,1024]{1,0:T(8,128)(2,1)S(1)} collective-permute-done((bf16[256,1024]{1,0:T(8,128)(2,1)}, bf16[256,1024]{1,0:T(8,128)(2,1)S(1)}, u32[]{:S(2)}, u32[]{:S(2)}) %collective-permute-start.24) | collective-permute-done | bytes 524320 | tf_op jit(solution)/shard_map/ppermute | solution.py:353
  541.7 4.3 collective-permute-done.26
  546.2 3.4 copy-done.5
  (500 shorter events, 118.8 us)
Async XLA Ops:
  1.5 25.2 %collective-permute-start.1 = (s32[1,1024]{1,0:T(1,128)S(1)}, s32[1,1024]{1,0:T(1,128)S(1)}, u32[]{:S(2)}, u32[]{:S(2)}) collective-permute-start(s32[1,1024]{1,0:T(1,128)S(1)} %constant_dynamic-slice_fusion.5), channel_id=1, source_target_pairs={{0,8},{2,10},{12,4},{14,6},{1,9},{3,11},{13,5},{15,7},{16,24},{18,... | collective-permute-start | bytes 12296 | tf_op jit(solution)/shard_map/ppermute | solution.py:921
  3.5 22.6 %collective-permute-start = (bf16[1,1024]{1,0:T(2,128)(2,1)S(1)}, bf16[1,1024]{1,0:T(2,128)(2,1)S(1)}, u32[]{:S(2)}, u32[]{:S(2)}) collective-permute-start(bf16[1,1024]{1,0:T(2,128)(2,1)S(1)} %constant_dynamic-slice_fusion.6), channel_id=1, source_target_pairs={{0,8},{2,10},{12,4},{14,6},{1,9},{3,11},{13,5},{15,7},{16,24},{18,... | collective-permute-start | bytes 6152 | tf_op jit(solution)/shard_map/ppermute | solution.py:921
  6.7 150.6 %collective-permute-start.10 = (bf16[256,1024]{1,0:T(8,128)(2,1)}, bf16[256,1024]{1,0:T(8,128)(2,1)}, u32[]{:S(2)}, u32[]{:S(2)}) collective-permute-start(bf16[256,1024]{1,0:T(8,128)(2,1)} %constant_dynamic-slice_fusion), channel_id=1, source_target_pairs={{0,8},{2,10},{12,4},{14,6},{1,9},{3,11},{13,5},{15,7},{16,24},{18,... | collective-permute-start | bytes 1572872 | tf_op jit(solution)/shard_map/ppermute | solution.py:921
  160.0 14.4 %collective-permute-start.11 = (bf16[256,1024]{1,0:T(8,128)(2,1)S(1)}, bf16[256,1024]{1,0:T(8,128)(2,1)S(1)}, u32[]{:S(2)}, u32[]{:S(2)}) collective-permute-start(bf16[256,1024]{1,0:T(8,128)(2,1)S(1)} %convert_element_type.216), channel_id=1, source_target_pairs={{0,1},{1,0},{2,3},{3,2},{4,5},{5,4},{6,7},{7,6},{8,9},{9,8},{10,11... | collective-permute-start | bytes 1572872 | tf_op jit(solution)/shard_map/ppermute | solution.py:353
  162.3 13.2 %collective-permute-start.2 = (bf16[256,1024]{1,0:T(8,128)(2,1)}, bf16[256,1024]{1,0:T(8,128)(2,1)S(1)}, u32[]{:S(2)}, u32[]{:S(2)}) collective-permute-start(bf16[256,1024]{1,0:T(8,128)(2,1)} %maximum_select_fusion), channel_id=1, source_target_pairs={{0,0},{2,2},{4,8},{6,10},{8,4},{10,6},{12,12},{14,14},{1,1},{3,3},... | collective-permute-start | bytes 1572872 | tf_op jit(solution)/shard_map/ppermute | solution.py:841
  165.6 20.1 %collective-permute-start.4 = (bf16[256,1024]{1,0:T(8,128)(2,1)}, bf16[256,1024]{1,0:T(8,128)(2,1)}, u32[]{:S(2)}, u32[]{:S(2)}) collective-permute-start(bf16[256,1024]{1,0:T(8,128)(2,1)} %maximum_select_fusion), channel_id=1, source_target_pairs={{0,2},{2,4},{4,10},{6,12},{8,6},{10,0},{12,14},{14,8},{1,3},{3,5},... | collective-permute-start | bytes 1572872 | tf_op jit(solution)/shard_map/ppermute | solution.py:841
  175.5 25.1 %collective-permute-start.12 = (bf16[512,1024]{1,0:T(8,128)(2,1)}, bf16[512,1024]{1,0:T(8,128)(2,1)}, u32[]{:S(2)}, u32[]{:S(2)}) collective-permute-start(bf16[512,1024]{1,0:T(8,128)(2,1)} %pad_maximum_fusion.6), channel_id=1, source_target_pairs={{0,8},{8,0},{1,9},{9,1},{2,10},{10,2},{3,11},{11,3},{4,12},{12,4},... | collective-permute-start | bytes 3145736 | tf_op jit(solution)/shard_map/ppermute | solution.py:353
  175.6 14.9 %collective-permute-start.3 = (bf16[256,1024]{1,0:T(8,128)(2,1)S(1)}, bf16[256,1024]{1,0:T(8,128)(2,1)}, u32[]{:S(2)}, u32[]{:S(2)}) collective-permute-start(bf16[256,1024]{1,0:T(8,128)(2,1)S(1)} %collective-permute-done.2), channel_id=1, source_target_pairs={{0,1},{1,0},{2,3},{3,2},{4,5},{5,4},{6,7},{7,6},{8,9},{9,8},{10,11... | collective-permute-start | bytes 1572872 | tf_op jit(solution)/shard_map/ppermute | solution.py:353
  185.7 14.1 %collective-permute-start.5 = (bf16[256,1024]{1,0:T(8,128)(2,1)}, bf16[256,1024]{1,0:T(8,128)(2,1)S(1)}, u32[]{:S(2)}, u32[]{:S(2)}) collective-permute-start(bf16[256,1024]{1,0:T(8,128)(2,1)} %collective-permute-done.4), channel_id=1, source_target_pairs={{0,1},{1,0},{2,3},{3,2},{4,5},{5,4},{6,7},{7,6},{8,9},{9,8},{10,11... | collective-permute-start | bytes 1572872 | tf_op jit(solution)/shard_map/ppermute | solution.py:353
  207.8 28.3 %collective-permute-start.13 = (bf16[512,1024]{1,0:T(8,128)(2,1)}, bf16[512,1024]{1,0:T(8,128)(2,1)}, u32[]{:S(2)}, u32[]{:S(2)}) collective-permute-start(bf16[512,1024]{1,0:T(8,128)(2,1)} %convolution_convert_fusion.1), channel_id=1, source_target_pairs={{0,8},{8,0},{1,9},{9,1},{2,10},{10,2},{3,11},{11,3},{4,12},{12,4},... | collective-permute-start | bytes 3145736 | tf_op jit(solution)/shard_map/ppermute | solution.py:353
  214.4 9.0 %collective-permute-start.44 = (bf16[512,256]{0,1:T(8,128)(2,1)S(1)}, bf16[512,256]{0,1:T(8,128)(2,1)S(1)}, u32[]{:S(2)}, u32[]{:S(2)}) collective-permute-start(bf16[512,256]{0,1:T(8,128)(2,1)S(1)} %get-tuple-element.218), channel_id=1, source_target_pairs={{0,16},{16,0},{1,17},{17,1},{2,18},{18,2},{3,19},{19,3},{4,20},{20... | collective-permute-start | bytes 786440 | tf_op jit(solution)/shard_map/ppermute | solution.py:353
  216.7 12.3 %collective-permute-start.46 = (bf16[512,256]{0,1:T(8,128)(2,1)S(1)}, bf16[512,256]{0,1:T(8,128)(2,1)S(1)}, u32[]{:S(2)}, u32[]{:S(2)}) collective-permute-start(bf16[512,256]{0,1:T(8,128)(2,1)S(1)} %get-tuple-element.217), channel_id=1, source_target_pairs={{0,16},{16,0},{1,17},{17,1},{2,18},{18,2},{3,19},{19,3},{4,20},{20... | collective-permute-start | bytes 786440 | tf_op jit(solution)/shard_map/ppermute | solution.py:353
  216.8 17.8 %collective-permute-start.48 = (bf16[512,256]{0,1:T(8,128)(2,1)S(1)}, bf16[512,256]{0,1:T(8,128)(2,1)S(1)}, u32[]{:S(2)}, u32[]{:S(2)}) collective-permute-start(bf16[512,256]{0,1:T(8,128)(2,1)S(1)} %get-tuple-element.216), channel_id=1, source_target_pairs={{0,16},{16,0},{1,17},{17,1},{2,18},{18,2},{3,19},{19,3},{4,20},{20... | collective-permute-start | bytes 786440 | tf_op jit(solution)/shard_map/ppermute | solution.py:353
  218.2 41.3 %collective-permute-start.43 = (bf16[512,256]{0,1:T(8,128)(2,1)S(1)}, bf16[512,256]{0,1:T(8,128)(2,1)S(1)}, u32[]{:S(2)}, u32[]{:S(2)}) collective-permute-start(bf16[512,256]{0,1:T(8,128)(2,1)S(1)} %get-tuple-element.215), channel_id=1, source_target_pairs={{0,16},{16,0},{1,17},{17,1},{2,18},{18,2},{3,19},{19,3},{4,20},{20... | collective-permute-start | bytes 786440 | tf_op jit(solution)/shard_map/ppermute | solution.py:353
  220.8 37.7 %copy-start.38 = (f32[1024,1024]{0,1:T(8,128)}, f32[1024,1024]{0,1:T(8,128)S(1)}, u32[]{:S(2)}) copy-start(f32[1024,1024]{0,1:T(8,128)S(1)} %get-tuple-element.310) | copy-start | bytes 12582916
  223.4 25.3 %collective-permute-start.36 = (bf16[512,256]{0,1:T(8,128)(2,1)S(1)}, bf16[512,256]{0,1:T(8,128)(2,1)S(1)}, u32[]{:S(2)}, u32[]{:S(2)}) collective-permute-start(bf16[512,256]{0,1:T(8,128)(2,1)S(1)} %get-tuple-element.222), channel_id=1, source_target_pairs={{0,16},{16,0},{1,17},{17,1},{2,18},{18,2},{3,19},{19,3},{4,20},{20... | collective-permute-start | bytes 786440 | tf_op jit(solution)/shard_map/ppermute | solution.py:353
  229.0 22.5 %collective-permute-start.38 = (bf16[512,256]{0,1:T(8,128)(2,1)S(1)}, bf16[512,256]{0,1:T(8,128)(2,1)S(1)}, u32[]{:S(2)}, u32[]{:S(2)}) collective-permute-start(bf16[512,256]{0,1:T(8,128)(2,1)S(1)} %get-tuple-element.221), channel_id=1, source_target_pairs={{0,16},{16,0},{1,17},{17,1},{2,18},{18,2},{3,19},{19,3},{4,20},{20... | collective-permute-start | bytes 786440 | tf_op jit(solution)/shard_map/ppermute | solution.py:353
  234.7 23.6 %collective-permute-start.40 = (bf16[512,256]{0,1:T(8,128)(2,1)S(1)}, bf16[512,256]{0,1:T(8,128)(2,1)S(1)}, u32[]{:S(2)}, u32[]{:S(2)}) collective-permute-start(bf16[512,256]{0,1:T(8,128)(2,1)S(1)} %get-tuple-element.220), channel_id=1, source_target_pairs={{0,16},{16,0},{1,17},{17,1},{2,18},{18,2},{3,19},{19,3},{4,20},{20... | collective-permute-start | bytes 786440 | tf_op jit(solution)/shard_map/ppermute | solution.py:353
  236.1 24.2 %collective-permute-start.45 = (bf16[512,256]{0,1:T(8,128)(2,1)S(1)}, bf16[512,256]{0,1:T(8,128)(2,1)S(1)}, u32[]{:S(2)}, u32[]{:S(2)}) collective-permute-start(bf16[512,256]{0,1:T(8,128)(2,1)S(1)} %get-tuple-element.203), channel_id=1, source_target_pairs={{0,6},{2,0},{4,2},{6,4},{1,7},{3,1},{5,3},{7,5},{8,14},{10,8},{12,... | collective-permute-start | bytes 786440 | tf_op jit(solution)/shard_map/ppermute | solution.py:357
  248.8 20.5 %collective-permute-start.47 = (bf16[512,256]{0,1:T(8,128)(2,1)S(1)}, bf16[512,256]{0,1:T(8,128)(2,1)S(1)}, u32[]{:S(2)}, u32[]{:S(2)}) collective-permute-start(bf16[512,256]{0,1:T(8,128)(2,1)S(1)} %get-tuple-element.205), channel_id=1, source_target_pairs={{0,4},{2,6},{4,0},{6,2},{1,5},{3,7},{5,1},{7,3},{8,12},{10,14},{12... | collective-permute-start | bytes 786440 | tf_op jit(solution)/shard_map/ppermute | solution.py:357
  251.5 17.8 %collective-permute-start.49 = (bf16[512,256]{0,1:T(8,128)(2,1)S(1)}, bf16[512,256]{0,1:T(8,128)(2,1)S(1)}, u32[]{:S(2)}, u32[]{:S(2)}) collective-permute-start(bf16[512,256]{0,1:T(8,128)(2,1)S(1)} %get-tuple-element.204), channel_id=1, source_target_pairs={{0,2},{2,4},{4,6},{6,0},{1,3},{3,5},{5,7},{7,1},{8,10},{10,12},{12... | collective-permute-start | bytes 786440 | tf_op jit(solution)/shard_map/ppermute | solution.py:357
  258.2 12.1 %collective-permute-start.14 = (bf16[256,1024]{1,0:T(8,128)(2,1)S(1)}, bf16[256,1024]{1,0:T(8,128)(2,1)S(1)}, u32[]{:S(2)}, u32[]{:S(2)}) collective-permute-start(bf16[256,1024]{1,0:T(8,128)(2,1)S(1)} %slice.855), channel_id=1, source_target_pairs={{0,1},{1,0},{2,3},{3,2},{4,5},{5,4},{6,7},{7,6},{8,9},{9,8},{10,11... | collective-permute-start | bytes 1572872 | tf_op jit(solution)/shard_map/ppermute | solution.py:353
  259.5 13.4 %collective-permute-start.35 = (bf16[512,256]{0,1:T(8,128)(2,1)}, bf16[512,256]{0,1:T(8,128)(2,1)}, u32[]{:S(2)}, u32[]{:S(2)}) collective-permute-start(bf16[512,256]{0,1:T(8,128)(2,1)} %get-tuple-element.219), channel_id=1, source_target_pairs={{0,16},{16,0},{1,17},{17,1},{2,18},{18,2},{3,19},{19,3},{4,20},{20... | collective-permute-start | bytes 786440 | tf_op jit(solution)/shard_map/ppermute | solution.py:353
  260.3 15.4 %collective-permute-start.37 = (bf16[512,256]{0,1:T(8,128)(2,1)}, bf16[512,256]{0,1:T(8,128)(2,1)}, u32[]{:S(2)}, u32[]{:S(2)}) collective-permute-start(bf16[512,256]{0,1:T(8,128)(2,1)} %get-tuple-element.206), channel_id=1, source_target_pairs={{0,6},{2,0},{4,2},{6,4},{1,7},{3,1},{5,3},{7,5},{8,14},{10,8},{12,... | collective-permute-start | bytes 786440 | tf_op jit(solution)/shard_map/ppermute | solution.py:357
  269.3 32.1 %collective-permute-start.39 = (bf16[512,256]{0,1:T(8,128)(2,1)S(1)}, bf16[512,256]{0,1:T(8,128)(2,1)}, u32[]{:S(2)}, u32[]{:S(2)}) collective-permute-start(bf16[512,256]{0,1:T(8,128)(2,1)S(1)} %get-tuple-element.208), channel_id=1, source_target_pairs={{0,4},{2,6},{4,0},{6,2},{1,5},{3,7},{5,1},{7,3},{8,12},{10,14},{12... | collective-permute-start | bytes 786440 | tf_op jit(solution)/shard_map/ppermute | solution.py:357
  269.3 36.0 %collective-permute-start.41 = (bf16[512,256]{0,1:T(8,128)(2,1)S(1)}, bf16[512,256]{0,1:T(8,128)(2,1)}, u32[]{:S(2)}, u32[]{:S(2)}) collective-permute-start(bf16[512,256]{0,1:T(8,128)(2,1)S(1)} %get-tuple-element.207), channel_id=1, source_target_pairs={{0,2},{2,4},{4,6},{6,0},{1,3},{3,5},{5,7},{7,1},{8,10},{10,12},{12... | collective-permute-start | bytes 786440 | tf_op jit(solution)/shard_map/ppermute | solution.py:357
  271.3 35.6 %collective-permute-start.15 = (bf16[256,1024]{1,0:T(8,128)(2,1)S(1)}, bf16[256,1024]{1,0:T(8,128)(2,1)S(1)}, u32[]{:S(2)}, u32[]{:S(2)}) collective-permute-start(bf16[256,1024]{1,0:T(8,128)(2,1)S(1)} %convert_element_type.221), channel_id=1, source_target_pairs={{0,1},{1,0},{2,3},{3,2},{4,5},{5,4},{6,7},{7,6},{8,9},{9,8},{10,11... | collective-permute-start | bytes 1572872 | tf_op jit(solution)/shard_map/ppermute | solution.py:353
  272.9 126.4 %collective-permute-start.6 = (bf16[256,1024]{1,0:T(8,128)(2,1)}, bf16[256,1024]{1,0:T(8,128)(2,1)}, u32[]{:S(2)}, u32[]{:S(2)}) collective-permute-start(bf16[256,1024]{1,0:T(8,128)(2,1)} %maximum_select_fusion), channel_id=1, source_target_pairs={{0,4},{2,6},{4,12},{6,14},{8,0},{10,2},{12,8},{14,10},{1,5},{3,7},... | collective-permute-start | bytes 1572872 | tf_op jit(solution)/shard_map/ppermute | solution.py:841
  275.8 127.0 %collective-permute-start.8 = (bf16[256,1024]{1,0:T(8,128)(2,1)}, bf16[256,1024]{1,0:T(8,128)(2,1)}, u32[]{:S(2)}, u32[]{:S(2)}) collective-permute-start(bf16[256,1024]{1,0:T(8,128)(2,1)} %maximum_select_fusion), channel_id=1, source_target_pairs={{0,6},{2,0},{4,14},{6,8},{8,2},{10,4},{12,10},{14,12},{1,7},{3,1},... | collective-permute-start | bytes 1572872 | tf_op jit(solution)/shard_map/ppermute | solution.py:841
  301.4 10.0 %collective-permute-start.50 = (bf16[256,256]{0,1:T(8,128)(2,1)}, bf16[256,256]{0,1:T(8,128)(2,1)S(1)}, u32[]{:S(2)}, u32[]{:S(2)}) collective-permute-start(bf16[256,256]{0,1:T(8,128)(2,1)} %select_convert_fusion.1), channel_id=1, source_target_pairs={{0,8},{8,0},{1,9},{9,1},{2,10},{10,2},{3,11},{11,3},{4,12},{12,4},... | collective-permute-start | bytes 393224 | tf_op jit(solution)/shard_map/ppermute | solution.py:353
  305.3 1.5 collective-permute-start.51
  306.9 3.2 collective-permute-start.52
  307.0 15.2 %collective-permute-start.16 = (bf16[512,1024]{1,0:T(8,128)(2,1)S(1)}, bf16[512,1024]{1,0:T(8,128)(2,1)S(1)}, u32[]{:S(2)}, u32[]{:S(2)}) collective-permute-start(bf16[512,1024]{1,0:T(8,128)(2,1)S(1)} %pad_maximum_fusion.7), channel_id=1, source_target_pairs={{0,8},{8,0},{1,9},{9,1},{2,10},{10,2},{3,11},{11,3},{4,12},{12,4},... | collective-permute-start | bytes 3145736 | tf_op jit(solution)/shard_map/ppermute | solution.py:353
  310.1 6.8 %collective-permute-start.42 = (bf16[256,256]{0,1:T(8,128)(2,1)S(1)}, bf16[256,256]{0,1:T(8,128)(2,1)S(1)}, u32[]{:S(2)}, u32[]{:S(2)}) collective-permute-start(bf16[256,256]{0,1:T(8,128)(2,1)S(1)} %select_convert_fusion.2), channel_id=1, source_target_pairs={{0,8},{8,0},{1,9},{9,1},{2,10},{10,2},{3,11},{11,3},{4,12},{12,4},... | collective-permute-start | bytes 393224 | tf_op jit(solution)/shard_map/ppermute | solution.py:353
  311.4 3.1 collective-permute-start.53
  314.4 4.6 collective-permute-start.54
  319.0 2.7 collective-permute-start.55
  371.8 31.1 %collective-permute-start.27 = (bf16[528,256]{0,1:T(8,128)(2,1)S(1)}, bf16[528,256]{0,1:T(8,128)(2,1)S(1)}, u32[]{:S(2)}, u32[]{:S(2)}) collective-permute-start(bf16[528,256]{0,1:T(8,128)(2,1)S(1)} %fusion.79), channel_id=1, source_target_pairs={{0,16},{16,0},{1,17},{17,1},{2,18},{18,2},{3,19},{19,3},{4,20},{20... | collective-permute-start | bytes 811016 | tf_op jit(solution)/shard_map/ppermute | solution.py:353
  373.5 11.5 %collective-permute-start.28 = (bf16[528,256]{0,1:T(8,128)(2,1)S(1)}, bf16[528,256]{0,1:T(8,128)(2,1)S(1)}, u32[]{:S(2)}, u32[]{:S(2)}) collective-permute-start(bf16[528,256]{0,1:T(8,128)(2,1)S(1)} %fusion.80), channel_id=1, source_target_pairs={{0,16},{16,0},{1,17},{17,1},{2,18},{18,2},{3,19},{19,3},{4,20},{20... | collective-permute-start | bytes 811016 | tf_op jit(solution)/shard_map/ppermute | solution.py:353
  374.4 17.5 %collective-permute-start.30 = (bf16[528,256]{0,1:T(8,128)(2,1)S(1)}, bf16[528,256]{0,1:T(8,128)(2,1)S(1)}, u32[]{:S(2)}, u32[]{:S(2)}) collective-permute-start(bf16[528,256]{0,1:T(8,128)(2,1)S(1)} %fusion.81), channel_id=1, source_target_pairs={{0,16},{16,0},{1,17},{17,1},{2,18},{18,2},{3,19},{19,3},{4,20},{20... | collective-permute-start | bytes 811016 | tf_op jit(solution)/shard_map/ppermute | solution.py:353
  384.9 14.0 %collective-permute-start.32 = (bf16[528,256]{0,1:T(8,128)(2,1)S(1)}, bf16[528,256]{0,1:T(8,128)(2,1)S(1)}, u32[]{:S(2)}, u32[]{:S(2)}) collective-permute-start(bf16[528,256]{0,1:T(8,128)(2,1)S(1)} %fusion.82), channel_id=1, source_target_pairs={{0,16},{16,0},{1,17},{17,1},{2,18},{18,2},{3,19},{19,3},{4,20},{20... | collective-permute-start | bytes 811016 | tf_op jit(solution)/shard_map/ppermute | solution.py:353
  391.9 12.4 %collective-permute-start.29 = (bf16[528,256]{0,1:T(8,128)(2,1)S(1)}, bf16[528,256]{0,1:T(8,128)(2,1)S(1)}, u32[]{:S(2)}, u32[]{:S(2)}) collective-permute-start(bf16[528,256]{0,1:T(8,128)(2,1)S(1)} %fusion.40), channel_id=1, source_target_pairs={{0,6},{2,0},{4,2},{6,4},{1,7},{3,1},{5,3},{7,5},{8,14},{10,8},{12,... | collective-permute-start | bytes 811016 | tf_op jit(solution)/shard_map/ppermute | solution.py:357
  399.0 24.7 %collective-permute-start.31 = (bf16[528,256]{0,1:T(8,128)(2,1)S(1)}, bf16[528,256]{0,1:T(8,128)(2,1)S(1)}, u32[]{:S(2)}, u32[]{:S(2)}) collective-permute-start(bf16[528,256]{0,1:T(8,128)(2,1)S(1)} %fusion.38), channel_id=1, source_target_pairs={{0,4},{2,6},{4,0},{6,2},{1,5},{3,7},{5,1},{7,3},{8,12},{10,14},{12... | collective-permute-start | bytes 811016 | tf_op jit(solution)/shard_map/ppermute | solution.py:357
  399.3 24.3 %collective-permute-start.33 = (bf16[528,256]{0,1:T(8,128)(2,1)S(1)}, bf16[528,256]{0,1:T(8,128)(2,1)S(1)}, u32[]{:S(2)}, u32[]{:S(2)}) collective-permute-start(bf16[528,256]{0,1:T(8,128)(2,1)S(1)} %fusion.36), channel_id=1, source_target_pairs={{0,2},{2,4},{4,6},{6,0},{1,3},{3,5},{5,7},{7,1},{8,10},{10,12},{12... | collective-permute-start | bytes 811016 | tf_op jit(solution)/shard_map/ppermute | solution.py:357
  402.8 40.8 %collective-permute-start.7 = (bf16[256,1024]{1,0:T(8,128)(2,1)}, bf16[256,1024]{1,0:T(8,128)(2,1)}, u32[]{:S(2)}, u32[]{:S(2)}) collective-permute-start(bf16[256,1024]{1,0:T(8,128)(2,1)} %collective-permute-done.6), channel_id=1, source_target_pairs={{0,1},{1,0},{2,3},{3,2},{4,5},{5,4},{6,7},{7,6},{8,9},{9,8},{10,11... | collective-permute-start | bytes 1572872 | tf_op jit(solution)/shard_map/ppermute | solution.py:353
  402.9 47.9 %collective-permute-start.9 = (bf16[256,1024]{1,0:T(8,128)(2,1)}, bf16[256,1024]{1,0:T(8,128)(2,1)}, u32[]{:S(2)}, u32[]{:S(2)}) collective-permute-start(bf16[256,1024]{1,0:T(8,128)(2,1)} %collective-permute-done.8), channel_id=1, source_target_pairs={{0,1},{1,0},{2,3},{3,2},{4,5},{5,4},{6,7},{7,6},{8,9},{9,8},{10,11... | collective-permute-start | bytes 1572872 | tf_op jit(solution)/shard_map/ppermute | solution.py:353
  424.8 4.9 collective-permute-start.34
  437.7 2.0 collective-permute-start.56
  439.6 3.7 collective-permute-start.57
  442.5 13.5 %collective-permute-start.17 = (bf16[512,1024]{1,0:T(8,128)(2,1)S(1)}, bf16[512,1024]{1,0:T(8,128)(2,1)S(1)}, u32[]{:S(2)}, u32[]{:S(2)}) collective-permute-start(bf16[512,1024]{1,0:T(8,128)(2,1)S(1)} %convolution_convert_fusion), channel_id=1, source_target_pairs={{0,8},{8,0},{1,9},{9,1},{2,10},{10,2},{3,11},{11,3},{4,12},{12,4},... | collective-permute-start | bytes 3145736 | tf_op jit(solution)/shard_map/ppermute | solution.py:353
  443.3 2.5 collective-permute-start.58
  445.8 2.5 collective-permute-start.59
  448.2 4.5 collective-permute-start.60
  457.3 10.4 %collective-permute-start.18 = (bf16[256,1024]{1,0:T(8,128)(2,1)S(1)}, bf16[256,1024]{1,0:T(8,128)(2,1)S(1)}, u32[]{:S(2)}, u32[]{:S(2)}) collective-permute-start(bf16[256,1024]{1,0:T(8,128)(2,1)S(1)} %slice.854), channel_id=1, source_target_pairs={{0,1},{1,0},{2,3},{3,2},{4,5},{5,4},{6,7},{7,6},{8,9},{9,8},{10,11... | collective-permute-start | bytes 1572872 | tf_op jit(solution)/shard_map/ppermute | solution.py:353
  468.0 37.5 %copy-start.88 = (f32[32,2]{0,1:T(2,128)S(1)}, f32[32,2]{0,1:T(2,128)}, u32[]{:S(2)}) copy-start(f32[32,2]{0,1:T(2,128)} %param.44) | copy-start | bytes 772
  468.0 37.5 %copy-start.94 = (f32[32,1]{0,1:T(1,128)S(1)}, f32[32,1]{0,1:T(1,128)}, u32[]{:S(2)}) copy-start(f32[32,1]{0,1:T(1,128)} %copy-done.93) | copy-start | bytes 388
  469.1 35.0 %collective-permute-start.19 = (bf16[256,1024]{1,0:T(8,128)(2,1)}, bf16[256,1024]{1,0:T(8,128)(2,1)}, u32[]{:S(2)}, u32[]{:S(2)}) collective-permute-start(bf16[256,1024]{1,0:T(8,128)(2,1)} %maximum_select_fusion.2), channel_id=1, source_target_pairs={{0,0},{2,2},{4,8},{6,10},{8,4},{10,6},{12,12},{14,14},{1,1},{3,3},... | collective-permute-start | bytes 1572872 | tf_op jit(solution)/shard_map/ppermute | solution.py:841
  475.6 42.2 %collective-permute-start.21 = (bf16[256,1024]{1,0:T(8,128)(2,1)}, bf16[256,1024]{1,0:T(8,128)(2,1)}, u32[]{:S(2)}, u32[]{:S(2)}) collective-permute-start(bf16[256,1024]{1,0:T(8,128)(2,1)} %maximum_select_fusion.2), channel_id=1, source_target_pairs={{0,2},{2,4},{4,10},{6,12},{8,6},{10,0},{12,14},{14,8},{1,3},{3,5},... | collective-permute-start | bytes 1572872 | tf_op jit(solution)/shard_map/ppermute | solution.py:841
  478.0 39.8 %collective-permute-start.23 = (bf16[256,1024]{1,0:T(8,128)(2,1)}, bf16[256,1024]{1,0:T(8,128)(2,1)}, u32[]{:S(2)}, u32[]{:S(2)}) collective-permute-start(bf16[256,1024]{1,0:T(8,128)(2,1)} %maximum_select_fusion.2), channel_id=1, source_target_pairs={{0,4},{2,6},{4,12},{6,14},{8,0},{10,2},{12,8},{14,10},{1,5},{3,7},... | collective-permute-start | bytes 1572872 | tf_op jit(solution)/shard_map/ppermute | solution.py:841
  479.3 40.0 %collective-permute-start.25 = (bf16[256,1024]{1,0:T(8,128)(2,1)}, bf16[256,1024]{1,0:T(8,128)(2,1)}, u32[]{:S(2)}, u32[]{:S(2)}) collective-permute-start(bf16[256,1024]{1,0:T(8,128)(2,1)} %maximum_select_fusion.2), channel_id=1, source_target_pairs={{0,6},{2,0},{4,14},{6,8},{8,2},{10,4},{12,10},{14,12},{1,7},{3,1},... | collective-permute-start | bytes 1572872 | tf_op jit(solution)/shard_map/ppermute | solution.py:841
  504.1 17.5 %collective-permute-start.20 = (bf16[256,1024]{1,0:T(8,128)(2,1)}, bf16[256,1024]{1,0:T(8,128)(2,1)}, u32[]{:S(2)}, u32[]{:S(2)}) collective-permute-start(bf16[256,1024]{1,0:T(8,128)(2,1)} %collective-permute-done.19), channel_id=1, source_target_pairs={{0,1},{1,0},{2,3},{3,2},{4,5},{5,4},{6,7},{7,6},{8,9},{9,8},{10,11... | collective-permute-start | bytes 1572872 | tf_op jit(solution)/shard_map/ppermute | solution.py:353
  517.8 14.2 %collective-permute-start.22 = (bf16[256,1024]{1,0:T(8,128)(2,1)}, bf16[256,1024]{1,0:T(8,128)(2,1)S(1)}, u32[]{:S(2)}, u32[]{:S(2)}) collective-permute-start(bf16[256,1024]{1,0:T(8,128)(2,1)} %collective-permute-done.21), channel_id=1, source_target_pairs={{0,1},{1,0},{2,3},{3,2},{4,5},{5,4},{6,7},{7,6},{8,9},{9,8},{10,11... | collective-permute-start | bytes 1572872 | tf_op jit(solution)/shard_map/ppermute | solution.py:353
  517.8 22.6 %collective-permute-start.24 = (bf16[256,1024]{1,0:T(8,128)(2,1)}, bf16[256,1024]{1,0:T(8,128)(2,1)S(1)}, u32[]{:S(2)}, u32[]{:S(2)}) collective-permute-start(bf16[256,1024]{1,0:T(8,128)(2,1)} %collective-permute-done.23), channel_id=1, source_target_pairs={{0,1},{1,0},{2,3},{3,2},{4,5},{5,4},{6,7},{7,6},{8,9},{9,8},{10,11... | collective-permute-start | bytes 1572872 | tf_op jit(solution)/shard_map/ppermute | solution.py:353
  519.3 26.7 %collective-permute-start.26 = (bf16[256,1024]{1,0:T(8,128)(2,1)}, bf16[256,1024]{1,0:T(8,128)(2,1)S(1)}, u32[]{:S(2)}, u32[]{:S(2)}) collective-permute-start(bf16[256,1024]{1,0:T(8,128)(2,1)} %collective-permute-done.25), channel_id=1, source_target_pairs={{0,1},{1,0},{2,3},{3,2},{4,5},{5,4},{6,7},{7,6},{8,9},{9,8},{10,11... | collective-permute-start | bytes 1572872 | tf_op jit(solution)/shard_map/ppermute | solution.py:353
  (102 other events, 1001.2 us)

commit v3 on v2

--- a/solution.py
+++ b/solution.py
@@ -368,68 +368,6 @@
     return jnp.where(
         first, jnp.concatenate([mine, other], axis=0), jnp.concatenate([other, mine], axis=0)
     )
-
-
-def attend_back_kernel(length, head_size, block, proj_ref, grad_ref, col_ref, row_ref, out_ref, key_sum, value_sum):
-    width = 3 * head_size
-    keys = proj_ref[0, :, head_size : 2 * head_size]
-    values = proj_ref[0, :, 2 * head_size : width]
-    key_sum[...] = jnp.zeros_like(key_sum)
-    value_sum[...] = jnp.zeros_like(value_sum)
-    scale = head_size**-0.5
-
-    def one_block(at, carry):
-        rows = pl.ds(pl.multiple_of(at * block, block), block)
-        queries = proj_ref[0, rows, 0:head_size] * jnp.bfloat16(scale)
-        grads = grad_ref[0, rows, :]
-        scores = lax.dot_general(keys, queries, ROW_PAIR, preferred_element_type=jnp.float32)
-        scores = jnp.where(col_ref[...] == row_ref[0:1, rows], scores, -1e30)
-        highest = jnp.max(scores, axis=0, keepdims=True)
-        exponent = jnp.exp(scores - highest)
-        probability = exponent * (1.0 / jnp.sum(exponent, axis=0, keepdims=True))
-        grad_prob = lax.dot_general(values, grads, ROW_PAIR, preferred_element_type=jnp.float32)
-        weighted = jnp.sum(probability * grad_prob, axis=0, keepdims=True)
-        grad_score = (probability * (grad_prob - weighted)).astype(jnp.bfloat16)
-        value_sum[...] += jnp.dot(
-            probability.astype(jnp.bfloat16), grads, preferred_element_type=jnp.float32
-        )
-        key_sum[...] += jnp.dot(grad_score, queries, preferred_element_type=jnp.float32)
-        grad_query = lax.dot_general(grad_score, keys, COL_PAIR, preferred_element_type=jnp.float32)
-        out_ref[0, rows, 0:head_size] = (grad_query * scale).astype(jnp.bfloat16)
-        return carry
-
-    lax.fori_loop(0, length // block, one_block, 0)
-    out_ref[0, :, head_size : 2 * head_size] = key_sum[...].astype(jnp.bfloat16)
-    out_ref[0, :, 2 * head_size : width] = value_sum[...].astype(jnp.bfloat16)
-
-
-def attend_all_back(proj, grad_ctx, segments, head_size):
-    heads, length, width = proj.shape
-    whole = lambda shape: pl.BlockSpec(shape, lambda h: (0, 0))
-    each = lambda shape: pl.BlockSpec((1,) + shape, lambda h: (h, 0, 0))
-    return pl.pallas_call(
-        partial(attend_back_kernel, length, head_size, 256),
-        grid=(heads,),
-        in_specs=[
-            each((length, width)),
-            each((length, head_size)),
-            whole((length, 1)),
-            whole((1, length)),
-        ],
-        out_specs=each((length, width)),
-        out_shape=jax.ShapeDtypeStruct((heads, length, width), jnp.bfloat16),
-        scratch_shapes=[
-            pltpu.VMEM((length, head_size), jnp.float32),
-            pltpu.VMEM((length, head_size), jnp.float32),
-        ],
-        compiler_params=pltpu.CompilerParams(vmem_limit_bytes=48 << 20),
-        cost_estimate=pl.CostEstimate(
-            flops=2 * heads * length * length * 128 * 5,
-            bytes_accessed=8 << 20,
-            transcendentals=heads * length * length,
-        ),
-        name="attend_all_back",
-    )(proj, grad_ctx, segments[:, None], segments[None, :])
 
 
 MESH_ID = pl.DeviceIdType.MESH
@@ -810,54 +748,525 @@
     )(*pieces, tokens, time_row, ids[:, None], ids[None, :])
 
 
-def spread_tokens(own):
-    near = flip(own, "y")
-    pair = jnp.concatenate([own, near], axis=0)
-    return jnp.concatenate([pair, flip(pair, "core")], axis=0)
-
-
-def sum_tokens(left, right, pairing):
-    half = left.shape[0] // 2
-    far = lax.dot_general(left[half:], right, pairing, preferred_element_type=jnp.float32)
-    came = flip(far.astype(jnp.bfloat16), "core")
-    near = lax.dot_general(left[:half], right, pairing, preferred_element_type=jnp.float32)
-    near = near + came.astype(jnp.float32)
-    quarter = half // 2
-    return near[:quarter] + flip(near[quarter:].astype(jnp.bfloat16), "y").astype(jnp.float32)
-
-
-def spread_output(own, zs, dtype):
-    count = 4
-    at_z, at_y = lax.axis_index("z"), lax.axis_index("y")
-    quarter, width = own.shape
-    result = jnp.zeros((2 * count * quarter, width), dtype)
-    for step in range(count):
-        pairs = []
+def plane_sum(wires, value, slots):
+    at_x, at_core, at_z, at_y = spots()
+    own = at_core * 4 + at_z
+    sent = []
+    for step in range(8):
+        core, turned = step // 4, step % 4
+        if step == 0:
+            slots[own] = value[...]
+            continue
+        sent.append(
+            wires.make(
+                value,
+                slots.at[own],
+                core=flipped(at_core, core),
+                z=lax.rem(at_z + turned, 4),
+            )
+        )
+        sent[-1].start()
+    return sent
+
+
+def plane_total(sent, slots):
+    for member in sent:
+        member.wait_recv()
+    total = slots[0]
+    for at in range(1, 8):
+        total = total + slots[at]
+    return total
+
+
+class Outlet:
+    def __init__(self, own, result, sends, receives, y_sends, y_receives, local):
+        self.own, self.result, self.local = own, result, local
+        self.sends, self.receives = sends, receives
+        self.y_sends, self.y_receives = y_sends, y_receives
+        self.at_x, self.at_core, self.at_z, self.at_y = spots()
+        self.quarter = own.shape[0]
+
+    def spot(self, place, core, at_y):
+        row = (place * 4 + core * 2 + at_y) * self.quarter
+        return self.result.at[pl.ds(pl.multiple_of(row, self.quarter), self.quarter)]
+
+    def copy(self, step):
+        at = 2 * step + self.at_core
+        return pltpu.make_async_remote_copy(
+            src_ref=self.own,
+            dst_ref=self.spot(lax.rem(self.at_z, 2), self.at_core, self.at_y),
+            send_sem=self.sends.at[at],
+            recv_sem=self.receives.at[at],
+            device_id={"core": lax.div(self.at_z, 2), "z": lax.rem(self.at_z + step, 4)},
+            device_id_type=MESH_ID,
+        )
+
+    def stay(self):
+        return pltpu.make_async_copy(
+            self.own, self.spot(lax.rem(self.at_z, 2), self.at_core, self.at_y), self.local
+        )
+
+    def start(self):
+        home = self.at_core == lax.div(self.at_z, 2)
+
+        @pl.when(home)
+        def _():
+            self.stay().start()
+
+        @pl.when(jnp.logical_not(home))
+        def _():
+            self.copy(0).start()
+
+        for step in (1, 3, 2):
+            self.copy(step).start()
+
+    def across(self, place, core):
+        spot = self.spot(place, core, self.at_y)
+        at = place * 2 + core
+        return pltpu.make_async_remote_copy(
+            src_ref=spot,
+            dst_ref=spot,
+            send_sem=self.y_sends.at[at],
+            recv_sem=self.y_receives.at[at],
+            device_id={"y": 1 - self.at_y},
+            device_id_type=MESH_ID,
+        )
+
+    def forward(self, place, core):
+        source = 2 * self.at_core + place
+        step = lax.rem(self.at_z - source + 4, 4)
+        own = jnp.logical_and(step == 0, self.at_core == core)
+
+        @pl.when(own)
+        def _():
+            self.stay().wait()
+
+        @pl.when(jnp.logical_not(own))
+        def _():
+            spot = self.spot(place, core, self.at_y)
+            at = 2 * step + core
+            pltpu.make_async_remote_copy(
+                src_ref=spot,
+                dst_ref=spot,
+                send_sem=self.sends.at[at],
+                recv_sem=self.receives.at[at],
+                device_id={"y": 1 - self.at_y},
+                device_id_type=MESH_ID,
+            ).wait_recv()
+
+        self.across(place, core).start()
+
+    def finish(self):
+        home = self.at_core == lax.div(self.at_z, 2)
+        for place in range(2):
+            for core in range(2):
+                self.across(place, core).wait()
+
+        @pl.when(jnp.logical_not(home))
+        def _():
+            self.copy(0).wait_send()
+
+        for step in range(1, 4):
+            self.copy(step).wait_send()
+
+
+def back_kernel(
+    w_head, w_up, w_down, emb, proj, ctx, w_out, hid, pre, act, normed_one, inverse_one, summed, vecs, upstream,
+    ids_col, ids_row,
+    block_out, input_out, res_head, res_up, res_down, res_tile, feature, norm,
+    two, slope, one, grad_ctx, grad_proj, two_full, one_full, send_c, recv_c, send_y, recv_y, keep, acc,
+    near_head, far_head, got_head, came_head, near_up, far_up, got_up, came_up, near_down, far_down, got_down, came_down,
+    out_one, out_two, feat, slots, scalar, scalar_slots, key_sum, value_sum, y_feat, x_feat, y_scalar, x_scalar,
+    send_sem, recv_sem, out_sem, local_sem,
+):
+    at_x, at_core, at_z, at_y = spots()
+    low, f32 = jnp.bfloat16, jnp.float32
+    length, width = emb.shape
+    quarter, half = length // 4, width // 2
+    zs = w_head.shape[0]
+    block = half // 2
+    head_size = ctx.shape[2]
+    in_size = 3 * head_size
+    wires = Wires(send_sem, recv_sem)
+    greet(True)
+    feat[...] = jnp.zeros_like(feat)
+
+    def lanes(h):
+        return pl.ds(pl.multiple_of(flipped(at_x, h) * half, half), half)
+
+    def second_norm(rows):
+        normed, inverse = norm_stats(summed[rows, :])
+        gain, shift = vecs[1:2, :], vecs[5:6, :]
+        value = (normed * gain + shift).astype(low)
+        for h in range(2):
+            out_one[rows, lanes(h)] = value[:, h * half : (h + 1) * half]
+        above = upstream[rows, :].astype(f32)
+        grad = norm_back(above * gain, normed, inverse)
+        feat[1:2, :] += jnp.sum(above * normed, axis=0, keepdims=True)
+        feat[5:6, :] += jnp.sum(above, axis=0, keepdims=True)
+        feat[4:5, :] += jnp.sum(grad, axis=0, keepdims=True)
+        two_full[rows, :] = grad
+        two[rows, :] = grad.astype(low)
+
+    row_loop(quarter, 32, second_norm)
+    to_y, to_core, again = spread_rows(wires, two, quarter)
+    outlets = [
+        Outlet(own, result, *[out_sem.at[n, k] for k in range(4)], local_sem.at[n])
+        for n, (own, result) in enumerate(((out_one, block_out), (out_two, input_out)))
+    ]
+    outlets[0].start()
+
+    def slopes(r):
+        rows = pl.ds(r * quarter, quarter)
+
+        def inner(s):
+            units = pl.ds(pl.multiple_of(s * block, block), block)
+            value = dot_f32(two[rows, 0:half], w_down[s, 0]) + dot_f32(two[rows, half:], w_down[s, 1])
+            slope[rows, units] = (value * gelu_slope(pre[rows, units])).astype(low)
+
+        block_loop(zs, inner)
+
+    slopes(0)
+    to_core.wait_recv()
+    slopes(2)
+    to_y.wait_recv()
+    again.start()
+    slopes(1)
+    again.wait_recv()
+    slopes(3)
+    ended = [to_y, to_core, again]
+
+    def group(near, far, got, came):
+        crossed = [wires.make(far.at[s], got.at[s], x=1 - at_x) for s in range(zs)]
+        turned = [
+            wires.make(far.at[s], came.at[s - 1], z=lax.rem(at_z + zs - s, zs)) for s in range(1, zs)
+        ]
+        return near, far, got, crossed, turned, came
+
+    groups = {
+        "head": group(near_head, far_head, got_head, came_head),
+        "up": group(near_up, far_up, got_up, came_up),
+        "down": group(near_down, far_down, got_down, came_down),
+    }
+
+    def weight_grads(name, left, right):
+        near, far, got, crossed, turned, came = groups[name]
+
+        for s in range(zs):
+            far[s] = dot_f32(left[:, half:], right[:, s * block : (s + 1) * block], COL_PAIR).astype(low)
+            crossed[s].start()
+
+        def inner(s):
+            units = pl.ds(pl.multiple_of(s * block, block), block)
+            near[s] = dot_f32(left[:, 0:half], right[:, units], COL_PAIR)
+
+        block_loop(zs, inner)
+
+    def turn_blocks(name):
+        near, far, got, crossed, turned, came = groups[name]
+        size = near.shape[1]
+        for s in range(zs):
+            crossed[s].wait()
+
+        def inner(s):
+            def add(rows):
+                near[s, rows, :] += got[s, rows, :].astype(f32)
+                far[s, rows, :] = near[s, rows, :].astype(low)
+
+            row_loop(size, 16, add)
+
+        block_loop(zs, inner)
+
+    def start_turns(name):
+        for member in groups[name][4]:
+            member.start()
+
+    def settle(name):
+        near, far, got, crossed, turned, came = groups[name]
+        size = near.shape[1]
+        for member in turned:
+            member.wait()
+
+        def add(rows):
+            total = near[0, rows, :]
+            for s in range(1, zs):
+                total = total + came[s - 1, rows, :].astype(f32)
+            near[0, rows, :] = total
+
+        row_loop(size, 16, add)
+
+    bufs = (send_c, recv_c, send_y, recv_y)
+
+    def back_part(r, side):
+        rows = pl.ds(r * quarter, quarter)
+        total = dot_f32(slope[rows, 0:block], w_up[0, side], ROW_PAIR)
+        for s in range(1, zs):
+            total = total + dot_f32(slope[rows, s * block : (s + 1) * block], w_up[s, side], ROW_PAIR)
+        return total
+
+    add_rows(wires, back_part, keep, acc, bufs, lambda: weight_grads("down", two, act))
+
+    def first_norm(rows):
+        grad_hidden = keep[rows, :] + two_full[rows, :]
+        normed = normed_one[rows, :]
+        grad = norm_back(grad_hidden * vecs[0:1, :], normed, inverse_one[rows, :])
+        feat[0:1, :] += jnp.sum(grad_hidden * normed, axis=0, keepdims=True)
+        feat[3:4, :] += jnp.sum(grad_hidden, axis=0, keepdims=True)
+        feat[2:3, :] += jnp.sum(grad, axis=0, keepdims=True)
+        one_full[rows, :] = grad
+        one[rows, :] = grad.astype(low)
+
+    row_loop(quarter, 32, first_norm)
+    to_y, to_core, again = spread_rows(wires, one, quarter)
+    ended += [to_y, to_core, again]
+    feat_sent = plane_sum(wires, feat, slots)
+    weight_grads("up", hid, slope)
+
+    def contexts(r):
+        rows = pl.ds(r * quarter, quarter)
+        value = dot_f32(one[rows, 0:half], w_out[0]) + dot_f32(one[rows, half:], w_out[1])
+        value = value.astype(low)
+        for s in range(zs):
+            grad_ctx[s, rows, :] = value[:, s * head_size : (s + 1) * head_size]
+
+    contexts(0)
+    to_core.wait_recv()
+    contexts(2)
+    to_y.wait_recv()
+    again.start()
+    contexts(1)
+    turn_blocks("down")
+    start_turns("down")
+    again.wait_recv()
+    contexts(3)
+    for place in range(2):
         for core in range(2):
-            for place in range(count):
-                index = core * 2 + place % 2
-                target = (place // 2) * count + (index + step) % count
-                pairs.append((core * count + place, target))
-        came = lax.ppermute(own, ("core", "z"), pairs)
-        crossed = flip(came, "y")
-        index = (at_z - step) % count
-        start = (index % 2) * count + (index // 2) * 2
-        result = lax.dynamic_update_slice(
-            result, came.astype(dtype), ((start + at_y) * quarter, 0)
-        )
-        result = lax.dynamic_update_slice(
-            result, crossed.astype(dtype), ((start + 1 - at_y) * quarter, 0)
-        )
-    return result
-
-
-def sum_scalar(value):
-    value = jnp.broadcast_to(value, (8, 128))
-    for axis in ("core", "y", "x"):
-        value = value + flip(value, axis)
-    value = value + lax.ppermute(value, "z", [(0, 1), (1, 0), (2, 3), (3, 2)])
-    value = value + lax.ppermute(value, "z", [(0, 3), (3, 0), (1, 2), (2, 1)])
-    return value[0, 0]
+            outlets[0].forward(place, core)
+    scale = head_size**-0.5
+
+    def attend(s):
+        keys = proj[s, :, head_size : 2 * head_size]
+        values = proj[s, :, 2 * head_size : in_size]
+        key_sum[...] = jnp.zeros_like(key_sum)
+        value_sum[...] = jnp.zeros_like(value_sum)
+
+        def inner(rows):
+            queries = proj[s, rows, 0:head_size] * low(scale)
+            grads = grad_ctx[s, rows, :]
+            scores = dot_f32(keys, queries, ROW_PAIR)
+            scores = jnp.where(ids_col[...] == ids_row[0:1, rows], scores, -1e30)
+            highest = jnp.max(scores, axis=0, keepdims=True)
+            exponent = jnp.exp(scores - highest)
+            probability = exponent * (1.0 / jnp.sum(exponent, axis=0, keepdims=True))
+            grad_prob = dot_f32(values, grads, ROW_PAIR)
+            weighted = jnp.sum(probability * grad_prob, axis=0, keepdims=True)
+            grad_score = (probability * (grad_prob - weighted)).astype(low)
+            value_sum[...] += dot_f32(probability.astype(low), grads)
+            key_sum[...] += dot_f32(grad_score, queries)
+            grad_query = dot_f32(grad_score, keys, COL_PAIR)
+            grad_proj[s, rows, 0:head_size] = (grad_query * scale).astype(low)
+
+        row_loop(length, quarter, inner)
+        grad_proj[s, :, head_size : 2 * head_size] = key_sum[...].astype(low)
+        grad_proj[s, :, 2 * head_size : in_size] = value_sum[...].astype(low)
+
+    block_loop(2, attend)
+    turn_blocks("up")
+    start_turns("up")
+    block_loop(2, lambda s: attend(s + 2))
+
+    size = block + TILE
+
+    def input_part(r, side):
+        rows = pl.ds(r * quarter, quarter)
+        parts = []
+        for core in range(2):
+            total = None
+            for s in range(zs):
+                value = dot_f32(
+                    grad_proj[s, rows, :], w_head[s, side, core * size : core * size + block, 0:in_size], ROW_PAIR
+                )
+                total = value if total is None else total + value
+            parts.append(total)
+        return jnp.concatenate(parts, axis=1)
+
+    near, far, got, crossed, turned, came = groups["head"]
+
+    def head_far():
+        for s in range(zs):
+            far[s, 0:half, 0:in_size] = dot_f32(emb[:, half:], grad_proj[s], COL_PAIR).astype(low)
+            far[s, 0:half, in_size:] = dot_f32(one[:, half:], ctx[s], COL_PAIR).astype(low)
+            sums = jnp.sum(grad_proj[s].astype(f32), axis=0, keepdims=True)
+            near[s, half:, :] = jnp.zeros((TILE, near.shape[2]), f32)
+            near[s, half : half + 1, 0:head_size] = sums[:, 0:head_size]
+            near[s, half : half + 1, 2 * head_size : in_size] = sums[:, 2 * head_size :]
+            near[s, half + 1 : half + 2, :] = jnp.sum(
+                slope[:, s * block : (s + 1) * block].astype(f32), axis=0, keepdims=True
+            )
+            far[s, half:, :] = near[s, half:, :].astype(low)
+            crossed[s].start()
+
+    add_rows(wires, input_part, keep, acc, bufs, head_far)
+
+    def leave(rows):
+        value = (keep[rows, :] + one_full[rows, :]).astype(low)
+        for h in range(2):
+            out_two[rows, lanes(h)] = value[:, h * half : (h + 1) * half]
+
+    row_loop(quarter, 32, leave)
+    outlets[1].start()
+
+    def head_near(s):
+        near[s, 0:half, 0:in_size] = dot_f32(emb[:, 0:half], grad_proj[s], COL_PAIR)
+        near[s, 0:half, in_size:] = dot_f32(one[:, 0:half], ctx[s], COL_PAIR)
+
+    block_loop(zs, head_near)
+    turn_blocks("head")
+    start_turns("head")
+
+    acc[0:8, :] = plane_total(feat_sent, slots)
+    y_copy = wires.make(acc.at[pl.ds(0, 8)], y_feat, y=1 - at_y)
+    y_copy.start()
+    y_copy.wait_recv()
+    feat_all = acc[0:8, :] + y_feat[...]
+    keep[0:8, :] = feat_all
+    x_copy = wires.make(keep.at[pl.ds(0, 8), pl.ds(half, half)], x_feat, x=1 - at_x)
+    x_copy.start()
+    x_copy.wait_recv()
+    feature[...] = feat_all[:, 0:half] + x_feat[...]
+
+    settle("down")
+    settle("up")
+    for place in range(2):
+        for core in range(2):
+            outlets[1].forward(place, core)
+    settle("head")
+
+    backs = []
+    results = (("head", res_head), ("up", res_up), ("down", res_down))
+    for at, (name, result) in enumerate(results):
+        near = groups[name][0]
+        mine = near.at[0, pl.ds(pl.multiple_of(at_core * block, block), block)]
+        other = near.at[0, pl.ds(pl.multiple_of((1 - at_core) * block, block), block)]
+        local = pltpu.make_async_copy(mine, result.at[at_core], local_sem.at[2 + at])
+        local.start()
+        remote = wires.make(other, result.at[at_core], core=1 - at_core)
+        remote.start()
+        backs += [local, remote]
+    tile = near_head.at[0, pl.ds(half, TILE)]
+    local = pltpu.make_async_copy(tile, res_tile.at[at_core], local_sem.at[5])
+    remote = wires.make(tile, res_tile.at[at_core], core=1 - at_core)
+    local.start()
+    remote.start()
+    backs += [local, remote]
+
+    acc[8:16, 0:block] = jnp.zeros((8, block), f32)
+    for name, _ in results:
+        near = groups[name][0]
+
+        def add(rows):
+            value = near[0, rows, :]
+            acc[8:16, 0:block] += value * value
+
+        row_loop(half, 8, add)
+    value = near_head[0, half : half + 8, :]
+    acc[8:16, 0:block] += 0.5 * value * value
+    shared = feature[...] * feature[...] * (1.0 / 16.0)
+    shared = shared[:, 0:block] + shared[:, block:]
+    summed_squares = jnp.sum(acc[8:16, 0:block] + shared)
+    scalar[...] = jnp.broadcast_to(summed_squares, scalar.shape)
+    scalar_sent = plane_sum(wires, scalar, scalar_slots)
+    value = plane_total(scalar_sent, scalar_slots)
+    norm[...] = value
+    y_two = wires.make(norm, y_scalar, y=1 - at_y)
+    y_two.start()
+    y_two.wait()
+    value = value + y_scalar[...]
+    send_scalar = scalar_slots.at[8]
+    send_scalar[...] = value
+    x_two = wires.make(send_scalar, x_scalar, x=1 - at_x)
+    x_two.start()
+    x_two.wait()
+    norm[...] = value + x_scalar[...]
+
+    for member in ended + feat_sent + scalar_sent + [y_copy, x_copy]:
+        member.wait_send()
+    for member in backs:
+        member.wait()
+    for outlet in outlets:
+        outlet.finish()
+
+
+def run_back(front, upstream, ids, tokens_shape):
+    low, f32 = jnp.bfloat16, jnp.float32
+    (w_head, w_up, w_down, emb, proj, ctx, w_out, hid, pre, act, normed_one, inverse_one, _, summed, vecs) = front
+    length, width = emb.shape
+    zs, _, span, packed = w_head.shape
+    quarter, half, block = length // 4, width // 2, width // 4
+    head_size = ctx.shape[2]
+    vmem = pl.BlockSpec(memory_space=pltpu.VMEM)
+    anywhere = pl.BlockSpec(memory_space=pl.ANY)
+    shape = jax.ShapeDtypeStruct
+    inputs = (w_head, w_up, w_down, emb, proj, ctx, w_out, hid, pre, act, normed_one, inverse_one, summed, vecs,
+              upstream, ids[:, None], ids[None, :])
+    head_rows = half + TILE
+
+    def triple(size):
+        return [pltpu.VMEM((n, size, block), d) for n, d in ((zs, f32), (zs, low), (zs, low), (zs - 1, low))]
+
+    return pl.pallas_call(
+        back_kernel,
+        out_shape=[
+            shape(tokens_shape, low),
+            shape(tokens_shape, low),
+            shape((2, block, block), f32),
+            shape((2, block, block), f32),
+            shape((2, block, block), f32),
+            shape((2, TILE, block), f32),
+            shape((8, half), f32),
+            shape((8, 128), f32),
+        ],
+        in_specs=[vmem] * len(inputs),
+        out_specs=[anywhere] * 2 + [vmem] * 6,
+        scratch_shapes=[
+            pltpu.VMEM((length, width), low),
+            pltpu.VMEM((length, width), low),
+            pltpu.VMEM((length, width), low),
+            pltpu.VMEM((zs, length, head_size), low),
+            pltpu.VMEM((zs, length, 3 * head_size), low),
+            pltpu.VMEM((quarter, width), f32),
+            pltpu.VMEM((quarter, width), f32),
+            pltpu.VMEM((2, quarter, width), low),
+            pltpu.VMEM((2, quarter, width), low),
+            pltpu.VMEM((quarter, width), low),
+            pltpu.VMEM((quarter, width), low),
+            pltpu.VMEM((quarter, width), f32),
+            pltpu.VMEM((quarter, width), f32),
+            *triple(head_rows),
+            *triple(half),
+            *triple(half),
+            pltpu.VMEM((quarter, width), low),
+            pltpu.VMEM((quarter, width), low),
+            pltpu.VMEM((8, width), f32),
+            pltpu.VMEM((8, 8, width), f32),
+            pltpu.VMEM((8, 128), f32),
+            pltpu.VMEM((9, 8, 128), f32),
+            pltpu.VMEM((length, head_size), f32),
+            pltpu.VMEM((length, head_size), f32),
+            pltpu.VMEM((8, width), f32),
+            pltpu.VMEM((8, half), f32),
+            pltpu.VMEM((8, 128), f32),
+            pltpu.VMEM((8, 128), f32),
+            pltpu.SemaphoreType.DMA((72,)),
+            pltpu.SemaphoreType.DMA((72,)),
+            pltpu.SemaphoreType.DMA((2, 4, 8)),
+            pltpu.SemaphoreType.DMA((6,)),
+        ],
+        compiler_params=pltpu.CompilerParams(
+            collective_id=1, has_side_effects=True, vmem_limit_bytes=67000000
+        ),
+        name="back",
+    )(*inputs)
 
 
 def on_grid(*arguments):
@@ -930,7 +1339,7 @@
         return lax.dynamic_slice_in_dim(cotangent, local * length + which * quarter, quarter, 0)
 
     upstream = borrow(at_quarter(place), at_quarter(place ^ 2))
-    upstream = swap_halves(upstream, swapped).astype(f32)
+    upstream = swap_halves(upstream, swapped)
 
     def relative(values):
         return jnp.concatenate(
@@ -941,142 +1350,28 @@
     time_row = swap_halves(own_time.astype(f32), swapped)
     segments = relative(own_ids)
 
-    span = 2 * rows
-    (
-        weights_head, weights_up, weights_down, embedded_low, projected, context, weights_out, hidden_low,
-        pre_act, expanded_low, normed_one, inverse_one, hidden, summed_two, vectors,
-    ) = run_front(pieces, tokens, time_row, segments, head_size)
-    gains, shifts = vectors[0:2], vectors[2:6]
-    body = jnp.concatenate(
-        [weights_head[:, :, :rows], weights_head[:, :, rows + TILE : 2 * rows + TILE]], axis=2
-    ).reshape(zs, 2 * span, packed)
-    weights_in = jnp.concatenate([body[i, :, : 3 * head_size] for i in range(zs)], axis=1)
-    weights_out = weights_out.reshape(2 * span, zs * head_size)
-    context_low = jnp.concatenate([context[i] for i in range(zs)], axis=1)
-
-    def joined(blocks):
-        return jnp.concatenate([blocks[i].reshape(2 * span, wide) for i in range(zs)], axis=1)
-
-    weights_up, weights_down = joined(weights_up), joined(weights_down)
-    normed_two, inverse_two = norm_stats(summed_two)
-    out = swap_halves((normed_two * gains[1] + shifts[3]).astype(low), swapped)
-    block_output = spread_output(out, zs, low)
-
-    gain_two = jnp.sum(upstream * normed_two, axis=0)
-    shift_three = jnp.sum(upstream, axis=0)
-    grad_pre_two = norm_back(upstream * gains[1], normed_two, inverse_two)
-    shift_two = jnp.sum(grad_pre_two, axis=0)
-    grad_two_low = spread_tokens(grad_pre_two.astype(low))
-    grad_down = lax.dot_general(grad_two_low, expanded_low, COL_PAIR, preferred_element_type=f32)
-    grad_act = jnp.dot(grad_two_low, weights_down, preferred_element_type=f32)
-    grad_pre_act = (grad_act * gelu_slope(pre_act)).astype(low)
-    unit_sums = jnp.sum(grad_pre_act, axis=0, dtype=f32)
-    back = sum_tokens(grad_pre_act, weights_up, ROW_PAIR)
-    grad_up = lax.dot_general(hidden_low, grad_pre_act, COL_PAIR, preferred_element_type=f32)
-    grad_hidden = back + grad_pre_two
-    gain_one = jnp.sum(grad_hidden * normed_one, axis=0)
-    shift_one = jnp.sum(grad_hidden, axis=0)
-    grad_pre_one = norm_back(grad_hidden * gains[0], normed_one, inverse_one)
-    shift_zero = jnp.sum(grad_pre_one, axis=0)
-    grad_one_low = spread_tokens(grad_pre_one.astype(low))
-    grad_context = jnp.dot(grad_one_low, weights_out, preferred_element_type=f32).astype(low)
-    grad_context = jnp.stack(
-        [grad_context[:, i * head_size : (i + 1) * head_size] for i in range(zs)]
-    )
-    grad_out = lax.dot_general(grad_one_low, context_low, COL_PAIR, preferred_element_type=f32)
-    grad_heads = attend_all_back(projected, grad_context, segments, head_size)
-    grad_projected = jnp.concatenate([grad_heads[i] for i in range(zs)], axis=1)
-    input_part = sum_tokens(grad_projected, weights_in, ROW_PAIR)
-    input_grad = swap_halves((input_part + grad_pre_one).astype(low), swapped)
-    input_grad = spread_output(input_grad, zs, f32)
-    grad_in = lax.dot_general(embedded_low, grad_projected, COL_PAIR, preferred_element_type=f32)
-    head_sums = jnp.sum(grad_projected, axis=0, dtype=f32).reshape(zs, 3, head_size)
-
-    def collect(own, far):
-        near = [
-            (a + flip(b.astype(low), "x").astype(f32)) for a, b in zip(own, far)
-        ]
-        total = near[0]
-        for step in range(1, zs):
-            total = total + turn(near[step].astype(low), -step, zs).astype(f32)
-        return total
-
-    def return_cores(block):
-        half = block.shape[0] // 2
-        mine = jnp.where(first_core, block[:half], block[half:])
-        sent = jnp.where(first_core, block[half:], block[:half])
-        came = flip(sent.astype(low), "core").astype(f32)
-        return jnp.where(first_core, mine, came), jnp.where(first_core, came, mine)
-
-    def split_blocks(grad):
-        parts = [grad[:, i * wide : (i + 1) * wide] for i in range(zs)]
-        return [p[:span] for p in parts], [p[span:] for p in parts]
-
-    total_down = collect(*split_blocks(grad_down))
-    total_up = collect(*split_blocks(grad_up))
-    head_near, head_distant = [], []
-    units = unit_sums.reshape(zs, 2, 2, 2 * small_rows)
-    for i in range(zs):
-        whole = jnp.concatenate(
-            [
-                grad_in[:, i * 3 * head_size : (i + 1) * 3 * head_size],
-                grad_out[:, i * head_size : (i + 1) * head_size],
-            ],
-            axis=1,
-        )
-        lower = jnp.concatenate([head_sums[i, 0][None], units[i, :, 0]], axis=0)
-        upper = jnp.concatenate([head_sums[i, 2][None], units[i, :, 1]], axis=0)
-        kept = jnp.where(first_x, lower, upper)
-        sent = jnp.where(first_x, upper, lower)
-        pad = ((0, 13), (0, packed - 2 * small_rows))
-        head_near.append(jnp.concatenate([whole[:span], jnp.pad(kept, pad)], axis=0))
-        head_distant.append(jnp.concatenate([whole[span:], jnp.pad(sent, pad)], axis=0))
-    total_head = collect(head_near, head_distant)
-    small_total = total_head[span : span + 3]
-    small_total = jnp.concatenate(
-        [small_total[:, :small_rows], small_total[:, small_rows : 2 * small_rows]], axis=0
-    )
-    tail = jnp.pad(small_total, ((0, 0), (0, packed - small_rows)))
-    head_zero, head_one = return_cores(
-        jnp.concatenate(
-            [
-                total_head[:rows],
-                jnp.pad(tail[:3], ((0, 13), (0, 0))),
-                total_head[rows:span],
-                jnp.pad(tail[3:], ((0, 13), (0, 0))),
-            ],
-            axis=0,
-        )
-    )
-    up_zero, up_one = return_cores(total_up)
-    down_zero, down_one = return_cores(total_down)
+    front = run_front(pieces, tokens, time_row, segments, head_size)
+    block_output, input_grad, res_head, res_up, res_down, tiles, feature, norm = run_back(
+        front, upstream, segments, tokens.shape
+    )
     in_size = 3 * head_size
-    sent_in = jnp.concatenate([head_zero[:rows, :in_size], head_one[:rows, :in_size]], axis=1)
-    sent_out = jnp.concatenate([head_zero[:rows, in_size:], head_one[:rows, in_size:]], axis=1)
-    sent_up = jnp.concatenate([up_zero, up_one], axis=1)
-    sent_down = jnp.concatenate([down_zero, down_one], axis=1)
-    tails = [member[rows : rows + 3, :small_rows].T for member in (head_zero, head_one)]
-    sent_head = jnp.concatenate([tails[0][:, :1], tails[1][:, :1]], axis=1)
-    sent_unit = jnp.concatenate([tails[0][:, 1:], tails[1][:, 1:]], axis=1)
-
-    feature = jnp.stack([gain_one, gain_two, shift_zero, shift_one, shift_two, shift_three])
-    feature = jnp.pad(feature, ((0, 2), (0, 0)))
-    for axis in ("core", "y"):
-        feature = feature + flip(feature, axis)
-    feature = feature + lax.ppermute(feature, "z", [(0, 1), (1, 0), (2, 3), (3, 2)])
-    feature = feature + lax.ppermute(feature, "z", [(0, 3), (3, 0), (1, 2), (2, 1)])
-    feature = feature[:, :span] + flip(feature[:, span:], "x")
-    feature = jnp.where(first_core, feature[:, :rows], feature[:, rows:])
+    sent_in = jnp.concatenate([res_head[0, :, :in_size], res_head[1, :, :in_size]], axis=1)
+    sent_out = jnp.concatenate([res_head[0, :, in_size:], res_head[1, :, in_size:]], axis=1)
+    sent_up = jnp.concatenate([res_up[0], res_up[1]], axis=1)
+    sent_down = jnp.concatenate([res_down[0], res_down[1]], axis=1)
+    sent_head = lax.dynamic_slice(
+        tiles[:, 0], (0, at_x * 2 * head_size + at_core * small_rows), (2, small_rows)
+    ).T
+    units = lax.dynamic_slice(
+        tiles[:, 1].reshape(4, 4 * small_rows), (0, position * small_rows), (4, small_rows)
+    )
+    sent_unit = units.T
+    feature = lax.dynamic_slice(feature, (0, at_core * rows), (8, rows))
     sent_gains, sent_shifts = feature[0:2].T, feature[2:6].T
-
+    grad_norm = jnp.sqrt(norm[0, 0])
     gradients = (sent_in, sent_out, sent_up, sent_down, sent_head, sent_unit, sent_gains, sent_shifts)
-    split_part = reduce(add_squares, gradients[:6], jnp.zeros((), f32))
-    copied_part = reduce(add_squares, gradients[6:], jnp.zeros((), f32)) / (
-        lax.axis_size("z") * lax.axis_size("y")
-    )
-    grad_norm = jnp.sqrt(sum_scalar(split_part + copied_part))
     factor = CLIP / jnp.maximum(grad_norm, CLIP)
-    results = [block_output, input_grad, grad_norm.reshape(1)]
+    results = [block_output, input_grad.astype(f32), grad_norm.reshape(1)]
     for position in range(8):
         results += adam_update(
             masters[position],

time: 559 us -> 385 us (0.69); the launches traced: 551 us -> 384 us
  Pallas kernels: 149 us -> 338 us
  waiting for transfers between devices: 127 us -> 0.01 us
  starting transfers between devices: 121 us -> 3.85 us
  local copies, waits for them, and re-layouts: 66.4 us -> 15 us
  other arithmetic: 53.6 us -> 24.3 us
  matrix products: 24 us -> 0 us
  between operations: 10.1 us -> 3.05 us
    pallas_call x1, Pallas kernels: 25.4 us -> 215 us  [run_back(): pl.pallas_call(back_kernel, out_shape=[shape(tokens_shape, low), shape(to...]
    ppermute x58 -> x0, waiting for transfers between devices: 127 us -> none  [the longest x37 67.3 us: flip(): return lax.ppermute(value, axis, [(0, 1), (1, 0)])]
    ppermute x58 -> x0, starting transfers between devices: 117 us -> none  [the longest x8 45 us: spread_output(): came = lax.ppermute(own, ('core', 'z'), pairs)]
    unnamed x235 -> x60, local copies, waits for them, and re-layouts: 29.9 us -> 2.19 us
    dot_general x10 -> x0, matrix products: 24 us -> none  [the longest x2 4.89 us: sum_tokens(): lax.dot_general(left[half:], right, pairing, preferred_element_type=jnp.f...]
    dynamic_update_slice x8 -> x0, local copies, waits for them, and re-layouts: 13.2 us -> none  [the longest x4 6.63 us: spread_output(): lax.dynamic_update_slice(result, crossed.astype(dtype), ((start + 1 - at_...]
    reduce_sum x15 -> x0, other arithmetic: 11.1 us -> none  [the longest x8 5.29 us: add_squares(): return running + jnp.sum(member * member)]
    concatenate x20 -> x0, other arithmetic: 9.92 us -> none  [the longest x4 2.81 us: on_grid(): lower = jnp.concatenate([head_sums[i, 0][None], units[i, :, 0]], axis=0)]
  transfers between devices with their start and end apart: 61 -> 3, of which waited for: 23 -> 0; matrix products, arithmetic and copies ran while one was open for 23% -> 3% of each run, Pallas kernels for 27% -> 32%
where the time goes in v3:
time: 385 us; the launch traced here: 384 us
  Pallas kernels  338 us (88%)
  other arithmetic  24.3 us (6%)
  local copies, waits for them, and re-layouts  15 us (4%)
  starting transfers between devices  3.85 us (1%)
    pallas_call x1, Pallas kernels, run_back(): pl.pallas_call(back_kernel, out_shape=[shape(tokens_shape, low), shape(to...  215 us
    pallas_call x1, Pallas kernels, run_front(): pl.pallas_call(front_kernel, out_shape=[jax.ShapeDtypeStruct(*s) for s in...  123 us
    sub x8, other arithmetic, adam_update(): return (weight - rate * (corrected + decay * weight), moment, square)  9.15 us
  transfers between devices with their start and end apart: 3, of which 0 were waited for; matrix products, arithmetic and copies ran while one was open for 3% of the time, Pallas kernels for 32%

profile of v3, /device:TPU:1, one launch (start us, length us, event | category | flops | bytes accessed | tf_op | source)
XLA Modules:
  0.0 383.8 jit_solution(12841110306436846535)
XLA Ops:
  0.7 0.0 copy-start.15
  0.7 0.0 copy-start.2
  0.7 0.8 constant_dynamic-slice_fusion.8
  1.5 1.3 collective-permute-start.1
  2.8 0.7 constant_dynamic-slice_fusion.9
  3.5 1.3 collective-permute-start
  4.8 1.1 constant_dynamic-slice_fusion.3
  5.9 1.3 collective-permute-start.2
  7.2 0.7 maximum_bitcast_fusion.2
  7.9 0.1 dynamic_update_slice.21
  8.0 0.8 slice_bitcast_fusion.15
  8.8 0.8 slice_bitcast_fusion.13
  9.6 0.2 dynamic_update_slice.25
  9.8 0.3 dynamic_update_slice.22
  10.1 1.0 convert.40
  11.1 0.1 fusion.24
  11.2 0.9 convert.41
  12.1 0.1 fusion.25
  12.2 1.1 convert.45
  13.4 0.3 dynamic_update_slice.26
  13.7 0.3 dynamic_update_slice.23
  14.0 0.8 pad_maximum_fusion.1
  14.8 0.1 maximum_bitcast_fusion
  14.9 0.7 pad_maximum_fusion.head_piece
  15.7 0.6 broadcast_select_fusion.2.time_row
  16.4 0.0 copy-start.14
  16.4 1.0 copy.55.ids_col
  17.4 123.0 %front.1 = (bf16[4,2,544,256]{3,2,1,0:T(8,128)(2,1)}, bf16[4,2,512,256]{3,2,1,0:T(8,128)(2,1)}, bf16[4,2,512,256]{3,2,1,0:T(8,128)(2,1)}, bf16[1024,1024]{1,0:T(...) custom-call(bf16[2,272,256]{2,1,0:T(8,128)(2,1)} %pad_maximum_fusion, ...), custom_call_target="tpu_custom_call" | custom-call | tf_op jit(solution)/shard_map/front/pallas_call | solution.py:727
  140.5 1.2 dynamic-slice_select_fusion
  141.8 1.0 maximum_select_fusion.upstream
  142.7 214.6 %back.1 = (bf16[2048,1024]{1,0:T(8,128)(2,1)}, bf16[2048,1024]{1,0:T(8,128)(2,1)}, f32[2,256,256]{2,1,0:T(8,128)}, f32[2,256,256]{2,1,0:T(8,128)}, f32[2,256,256...) custom-call(bf16[4,2,544,256]{3,2,1,0:T(8,128)(2,1)} %get-tuple-element.49.w_head, ...), custom_call_target="tpu_custom_call" | custom-call | tf_op jit(solution)/shard_map/back/pallas_call | solution.py:1217
  357.3 1.1 slice_bitcast_fusion.11
  358.4 1.1 slice_bitcast_fusion.5
  359.5 1.2 slice.111
  361.4 0.8 fusion.26
  362.2 1.1 slice_bitcast_fusion.1
  363.3 1.1 slice_bitcast_fusion.3
  364.3 0.0 copy-start.17
  364.3 0.0 copy-start.23
  364.4 0.0 copy-start.24
  364.4 0.0 copy-start.16
  364.4 0.0 copy-start.21
  364.4 0.0 copy-start.22
  364.4 0.0 copy-start.18
  364.4 0.0 copy-start.25
  364.4 0.0 copy-start.26
  364.4 0.0 copy-start.20
  364.5 0.0 copy-start.27
  364.5 0.0 copy-start.28
  364.5 0.0 copy-start.1
  364.5 0.0 copy-start.3
  364.5 0.0 copy-start.7
  364.6 6.8 %convert_element_type.10 = f32[2048,1024]{1,0:T(8,128)} convert(bf16[2048,1024]{1,0:T(8,128)(2,1)} %get-tuple-element.64) | non-fusion elementwise | flops 2097152 | bytes 12582912 | tf_op jit(solution)/shard_map/convert_element_type | solution.py:1374
  371.3 0.1 fusion.14
  371.4 1.4 multiply_subtract_fusion.5
  372.8 1.4 multiply_subtract_fusion.4
  374.2 0.7 multiply_subtract_fusion.6
  374.9 0.6 multiply_subtract_fusion.7
  375.5 0.0 copy-start.4
  375.6 1.4 multiply_subtract_fusion
  377.0 1.4 multiply_subtract_fusion.1
  378.4 0.9 multiply_subtract_fusion.3
  379.4 1.3 multiply_subtract_fusion.2
  380.7 2.0 copy.65
  (57 shorter events, 0.3 us)
Async XLA Ops:
  0.7 15.6 %copy-start.19 = (s32[2,1024]{1,0:T(2,128)S(1)}, s32[2,1024]{1,0:T(2,128)}, u32[]{:S(2)}) copy-start(s32[2,1024]{1,0:T(2,128)} %param.30) | copy-start | bytes 24580
  0.7 15.0 %copy-start.15 = (bf16[2,1024]{1,0:T(2,128)(2,1)S(1)}, bf16[2,1024]{1,0:T(2,128)(2,1)}, u32[]{:S(2)}) copy-start(bf16[2,1024]{1,0:T(2,128)(2,1)} %param.29) | copy-start | bytes 12292
  0.7 12.6 %copy-start.2 = (f32[256,512]{1,0:T(8,128)S(1)}, f32[256,512]{1,0:T(8,128)}, u32[]{:S(2)}) copy-start(f32[256,512]{1,0:T(8,128)} %param.38) | copy-start | bytes 1572868
  1.5 14.8 %collective-permute-start.1 = (s32[1,1024]{1,0:T(1,128)S(1)}, s32[1,1024]{1,0:T(1,128)S(1)}, u32[]{:S(2)}, u32[]{:S(2)}) collective-permute-start(s32[1,1024]{1,0:T(1,128)S(1)} %constant_dynamic-slice_fusion.8), channel_id=1, source_target_pairs={{0,8},{2,10},{12,4},{14,6},{1,9},{3,11},{13,5},{15,7},{16,24},{18,... | collective-permute-start | bytes 12296 | tf_op jit(solution)/shard_map/ppermute | solution.py:1330
  3.5 12.2 %collective-permute-start = (bf16[1,1024]{1,0:T(2,128)(2,1)S(1)}, bf16[1,1024]{1,0:T(2,128)(2,1)S(1)}, u32[]{:S(2)}, u32[]{:S(2)}) collective-permute-start(bf16[1,1024]{1,0:T(2,128)(2,1)S(1)} %constant_dynamic-slice_fusion.9), channel_id=1, source_target_pairs={{0,8},{2,10},{12,4},{14,6},{1,9},{3,11},{13,5},{15,7},{16,24},{18,... | collective-permute-start | bytes 6152 | tf_op jit(solution)/shard_map/ppermute | solution.py:1330
  5.9 134.6 %collective-permute-start.2 = (bf16[256,1024]{1,0:T(8,128)(2,1)S(1)}, bf16[256,1024]{1,0:T(8,128)(2,1)S(1)}, u32[]{:S(2)}, u32[]{:S(2)}) collective-permute-start(bf16[256,1024]{1,0:T(8,128)(2,1)S(1)} %constant_dynamic-slice_fusion.3), channel_id=1, source_target_pairs={{0,8},{2,10},{12,4},{14,6},{1,9},{3,11},{13,5},{15,7},{16,24},{18,... | collective-permute-start | bytes 1572872 | tf_op jit(solution)/shard_map/ppermute | solution.py:1330
  16.4 1.0 copy-start.14
  364.3 7.1 %copy-start.17 = (f32[256,2]{0,1:T(2,128)S(1)}, f32[256,2]{0,1:T(2,128)}, u32[]{:S(2)}) copy-start(f32[256,2]{0,1:T(2,128)} %param.50) | copy-start | bytes 6148
  364.3 7.1 %copy-start.23 = (f32[256,2]{0,1:T(2,128)S(1)}, f32[256,2]{0,1:T(2,128)}, u32[]{:S(2)}) copy-start(f32[256,2]{0,1:T(2,128)} %param.51) | copy-start | bytes 6148
  364.4 7.1 %copy-start.24 = (f32[256,2]{0,1:T(2,128)S(1)}, f32[256,2]{0,1:T(2,128)}, u32[]{:S(2)}) copy-start(f32[256,2]{0,1:T(2,128)} %param.52) | copy-start | bytes 6148
  364.4 8.5 %copy-start.16 = (f32[256,4]{0,1:T(4,128)S(1)}, f32[256,4]{0,1:T(4,128)}, u32[]{:S(2)}) copy-start(f32[256,4]{0,1:T(4,128)} %param.53) | copy-start | bytes 12292
  364.4 8.4 %copy-start.21 = (f32[256,4]{0,1:T(4,128)S(1)}, f32[256,4]{0,1:T(4,128)}, u32[]{:S(2)}) copy-start(f32[256,4]{0,1:T(4,128)} %param.54) | copy-start | bytes 12292
  364.4 8.4 %copy-start.22 = (f32[256,4]{0,1:T(4,128)S(1)}, f32[256,4]{0,1:T(4,128)}, u32[]{:S(2)}) copy-start(f32[256,4]{0,1:T(4,128)} %param.55) | copy-start | bytes 12292
  364.4 9.8 %copy-start.18 = (f32[32,4]{0,1:T(4,128)S(1)}, f32[32,4]{0,1:T(4,128)}, u32[]{:S(2)}) copy-start(f32[32,4]{0,1:T(4,128)} %param.47) | copy-start | bytes 1540
  364.4 9.8 %copy-start.25 = (f32[32,4]{0,1:T(4,128)S(1)}, f32[32,4]{0,1:T(4,128)}, u32[]{:S(2)}) copy-start(f32[32,4]{0,1:T(4,128)} %param.48) | copy-start | bytes 1540
  364.4 9.8 %copy-start.26 = (f32[32,4]{0,1:T(4,128)S(1)}, f32[32,4]{0,1:T(4,128)}, u32[]{:S(2)}) copy-start(f32[32,4]{0,1:T(4,128)} %param.49) | copy-start | bytes 1540
  364.4 10.5 %copy-start.20 = (f32[32,2]{0,1:T(2,128)S(1)}, f32[32,2]{0,1:T(2,128)}, u32[]{:S(2)}) copy-start(f32[32,2]{0,1:T(2,128)} %param.44) | copy-start | bytes 772
  364.5 10.5 %copy-start.27 = (f32[32,2]{0,1:T(2,128)S(1)}, f32[32,2]{0,1:T(2,128)}, u32[]{:S(2)}) copy-start(f32[32,2]{0,1:T(2,128)} %param.45) | copy-start | bytes 772
  364.5 10.5 %copy-start.28 = (f32[32,2]{0,1:T(2,128)S(1)}, f32[32,2]{0,1:T(2,128)}, u32[]{:S(2)}) copy-start(f32[32,2]{0,1:T(2,128)} %param.46) | copy-start | bytes 772
  364.5 11.1 %copy-start.1 = (f32[256,512]{1,0:T(8,128)S(1)}, f32[256,512]{1,0:T(8,128)}, u32[]{:S(2)}) copy-start(f32[256,512]{1,0:T(8,128)} %param.41) | copy-start | bytes 1572868
  364.5 11.0 %copy-start.5 = (f32[256,512]{1,0:T(8,128)S(1)}, f32[256,512]{1,0:T(8,128)}, u32[]{:S(2)}) copy-start(f32[256,512]{1,0:T(8,128)} %param.42) | copy-start | bytes 1572868
  364.5 11.0 %copy-start.6 = (f32[256,512]{1,0:T(8,128)S(1)}, f32[256,512]{1,0:T(8,128)}, u32[]{:S(2)}) copy-start(f32[256,512]{1,0:T(8,128)} %param.43) | copy-start | bytes 1572868
  364.5 12.5 %copy-start.3 = (f32[256,512]{1,0:T(8,128)S(1)}, f32[256,512]{1,0:T(8,128)}, u32[]{:S(2)}) copy-start(f32[256,512]{1,0:T(8,128)} %param.38) | copy-start | bytes 1572868
  364.5 12.5 %copy-start.7 = (f32[256,512]{1,0:T(8,128)S(1)}, f32[256,512]{1,0:T(8,128)}, u32[]{:S(2)}) copy-start(f32[256,512]{1,0:T(8,128)} %param.39) | copy-start | bytes 1572868
  364.5 12.5 %copy-start.8 = (f32[256,512]{1,0:T(8,128)S(1)}, f32[256,512]{1,0:T(8,128)}, u32[]{:S(2)}) copy-start(f32[256,512]{1,0:T(8,128)} %param.40) | copy-start | bytes 1572868
  371.3 7.1 %copy-start.9 = (f32[256,128]{1,0:T(8,128)S(1)}, f32[256,128]{1,0:T(8,128)}, u32[]{:S(2)}) copy-start(f32[256,128]{1,0:T(8,128)} %param.35) | copy-start | bytes 393220
  371.3 7.1 %copy-start.12 = (f32[256,128]{1,0:T(8,128)S(1)}, f32[256,128]{1,0:T(8,128)}, u32[]{:S(2)}) copy-start(f32[256,128]{1,0:T(8,128)} %param.36) | copy-start | bytes 393220
  371.3 7.1 %copy-start.13 = (f32[256,128]{1,0:T(8,128)S(1)}, f32[256,128]{1,0:T(8,128)}, u32[]{:S(2)}) copy-start(f32[256,128]{1,0:T(8,128)} %param.37) | copy-start | bytes 393220
  375.5 3.8 copy-start.4
  375.5 3.8 copy-start.10
  375.6 3.8 copy-start.11
  377.0 3.7 copy-start

commit v4 on v3

--- a/solution.py
+++ b/solution.py
@@ -487,10 +487,80 @@
     across.wait_send()
 
 
-def front_kernel(
-    head_piece, up_piece, down_piece, tokens, time_row, ids_col, ids_row,
-    w_head, w_up, w_down, emb, proj, ctx, w_out, hid, pre, act, normed_one, inverse_one, hidden, summed, vecs,
-    tok, send_c, recv_c, send_y, recv_y, keep, acc, send_sem, recv_sem, local_sem,
+class Relay:
+    def __init__(self, targets, z_sends, z_receives, x_sends, x_receives):
+        self.targets, self.z_sends, self.z_receives = targets, z_sends, z_receives
+        self.x_sends, self.x_receives = x_sends, x_receives
+        self.at_x, _, self.at_z, _ = spots()
+        middle = lax.rem(lax.div(self.at_z + 1, 2), 2)
+        first = 3 - 2 * lax.rem(self.at_z, 2)
+        second = 2 * (1 - middle) + middle * (4 - first)
+        self.order = [0, first, second, 6 - first - second]
+
+    def hop(self, at, slot, rising, send):
+        to = lax.rem(slot + (1 if rising else 3), 4)
+        target = self.targets[at]
+        return pltpu.make_async_remote_copy(
+            src_ref=target.at[slot, 0],
+            dst_ref=target.at[to, 0],
+            send_sem=self.z_sends.at[at, send],
+            recv_sem=self.z_receives.at[at, to],
+            device_id={"z": self.at_z + (1 if rising else -1)},
+            device_id_type=MESH_ID,
+        )
+
+    def cross(self, at, slot):
+        target = self.targets[at]
+        return pltpu.make_async_remote_copy(
+            src_ref=target.at[slot, 0],
+            dst_ref=target.at[slot, 1],
+            send_sem=self.x_sends.at[at, slot],
+            recv_sem=self.x_receives.at[at, slot],
+            device_id={"x": 1 - self.at_x},
+            device_id_type=MESH_ID,
+        )
+
+    def hops(self, at, turn, act):
+        slot = self.order[turn]
+        for rising in (True, False):
+            inside = self.at_z < 3 if rising else self.at_z > 0
+            if turn:
+                below = slot <= self.at_z
+                inside = jnp.logical_and(inside, below if rising else jnp.logical_not(below))
+            send = turn + 1 if turn else int(rising)
+
+            @pl.when(inside)
+            def _():
+                act(self.hop(at, jnp.int32(slot) if not turn else slot, rising, send))
+
+    def begin(self, at):
+        self.hops(at, 0, lambda copy: copy.start())
+
+    def arrive(self, at, turn):
+        slot = self.order[turn]
+        target = self.targets[at]
+        pltpu.make_async_remote_copy(
+            src_ref=target.at[slot, 0],
+            dst_ref=target.at[slot, 0],
+            send_sem=self.z_sends.at[at, 0],
+            recv_sem=self.z_receives.at[at, slot],
+            device_id={"x": 1 - self.at_x},
+            device_id_type=MESH_ID,
+        ).wait_recv()
+        self.hops(at, turn, lambda copy: copy.start())
+        self.cross(at, slot).start()
+
+    def finish(self):
+        for at in range(3):
+            for turn in range(4):
+                self.hops(at, turn, lambda copy: copy.wait_send())
+                self.cross(at, turn).wait_send()
+
+
+def front_part(
+    wires, head_piece, up_piece, down_piece, tokens, cotangent, time_row, ids_col, ids_row,
+    w_head, w_up, w_down, emb, proj, ctx, w_out, hid, pre, act, normed_one, inverse_one, hidden, vecs, upstream,
+    tok, send_c, recv_c, send_y, recv_y, keep, acc, local_sem, gather_sems,
 ):
     at_x, at_core, at_z, at_y = spots()
     low, f32 = jnp.bfloat16, jnp.float32
@@ -500,8 +570,6 @@
     span = half + 2 * TILE
     head_size = ctx.shape[2]
     in_size = 3 * head_size
-    wires = Wires(send_sem, recv_sem)
-    greet(False)
 
     kept, lent = [], []
     for at, (piece, target) in enumerate(((head_piece, w_head), (up_piece, w_up), (down_piece, w_down))):
@@ -513,13 +581,7 @@
         remote.start()
         kept.append(local)
         lent.append(remote)
-    turns, cross = [], []
-    for target in (w_head, w_up, w_down):
-        turns.append(
-            [None]
-            + [wires.make(target.at[0, 0], target.at[s, 0], z=lax.rem(at_z + s, zs)) for s in range(1, zs)]
-        )
-        cross.append([wires.make(target.at[s, 0], target.at[s, 1], x=1 - at_x) for s in range(zs)])
+    relay = Relay((w_head, w_up, w_down), *gather_sems)
 
     holds = at_core == lax.div(at_z, 2)
     start = lax.rem(at_z, 2) * length
@@ -534,6 +596,15 @@
 
             here.append(pltpu.make_async_copy(source(at_core), spot, local_sem.at[3 + 2 * r + h]))
             there.append(wires.make(source(1 - at_core), spot, core=1 - at_core))
+    for h in range(2):
+        spot = upstream.at[:, pl.ds(pl.multiple_of(flipped(at_x, h) * half, half), half)]
+
+        def above(core):
+            at = start + (core * 2 + at_y) * quarter
+            return cotangent.at[pl.ds(pl.multiple_of(at, quarter), quarter), pl.ds(h * half, half)]
+
+        here.append(pltpu.make_async_copy(above(at_core), spot, local_sem.at[11 + h]))
+        there.append(wires.make(above(1 - at_core), spot, core=1 - at_core))
 
     @pl.when(holds)
     def _():
@@ -544,10 +615,9 @@
     for at in range(3):
         kept[at].wait()
         lent[at].wait_recv()
-        for s in range(1, zs):
-            turns[at][s].start()
+        relay.begin(at)
         if at == 0:
-            cross[0][0].start()
+            relay.cross(0, 0).start()
 
     @pl.when(holds)
     def _():
@@ -563,10 +633,6 @@
         emb[rows, :] = (tok[rows, :].astype(f32) + time_row[...]).astype(low)
 
     row_loop(length, 32, embed)
-
-    def forward(at, s):
-        turns[at][s].wait_recv()
-        cross[at][s].start()
 
     def small(s, side):
         size = half // 2 + TILE
@@ -575,13 +641,13 @@
             + w_head[s, side, size + half // 2 : 2 * size, :].astype(f32)
         )
 
-    for s in range(zs):
-        if s + 1 < zs:
-            forward(0, s + 1)
-        if s == 2:
-            cross[1][0].start()
-            cross[2][0].start()
-        cross[0][s].wait_recv()
+    for turn in range(zs):
+        s = relay.order[turn]
+        if turn + 1 < zs:
+            relay.arrive(0, turn + 1)
+        if turn == 2:
+            relay.cross(1, 0).start()
+        relay.cross(0, s).wait_recv()
         bias = (small(s, 0) + small(s, 1))[0:1, :in_size]
         size = half // 2 + TILE
 
@@ -597,11 +663,6 @@
             proj[s, rows, :] = total.astype(low)
 
         row_loop(length, quarter, project)
-        for side in range(2):
-            for core in range(2):
-                w_out[side, core * (half // 2) : (core + 1) * (half // 2), s * head_size : (s + 1) * head_size] = w_head[
-                    s, side, core * size : core * size + half // 2, in_size:
-                ]
         keys = proj[s, :, head_size : 2 * head_size]
         values = proj[s, :, 2 * head_size : in_size]
 
@@ -623,15 +684,24 @@
             vecs[k : k + 1, side * half : side * half + half // 2] = tile[2 + k : 3 + k, :]
             vecs[k : k + 1, side * half + half // 2 : (side + 1) * half] = tile[8 + k : 9 + k, :]
 
-    for s in range(1, zs):
-        forward(1, s)
+    relay.arrive(1, 1)
+    relay.arrive(1, 2)
+    size = half // 2 + TILE
+    for s in range(zs):
+        for side in range(2):
+            for core in range(2):
+                w_out[side, core * (half // 2) : (core + 1) * (half // 2), s * head_size : (s + 1) * head_size] = w_head[
+                    s, side, core * size : core * size + half // 2, in_size:
+                ]
     bufs = (send_c, recv_c, send_y, recv_y)
 
     def mixed_part(r, side):
         joined = jnp.concatenate([ctx[s, r * quarter : (r + 1) * quarter, :] for s in range(zs)], axis=1)
         return dot_f32(joined, w_out[side], ROW_PAIR)
 
-    add_rows(wires, mixed_part, keep, acc, bufs)
+    add_rows(wires, mixed_part, keep, acc, bufs, lambda: relay.arrive(1, 3))
+    relay.cross(2, 0).start()
+    relay.arrive(2, 1)
 
     def first_norm(rows):
         total = tok[rows, :].astype(f32) + time_row[...] + keep[rows, :] + vecs[2:3, :]
@@ -644,10 +714,9 @@
 
     row_loop(quarter, 32, first_norm)
     to_y, to_core, again = spread_rows(wires, hid, quarter)
-    for s in range(1, zs):
-        forward(2, s)
     for s in range(zs):
-        cross[1][s].wait_recv()
+        relay.cross(1, s).wait_recv()
+    relay.arrive(2, 2)
 
     def up(r):
         rows = pl.ds(r * quarter, quarter)
@@ -664,13 +733,14 @@
     up(0)
     to_core.wait_recv()
     up(2)
+    relay.arrive(2, 3)
     to_y.wait_recv()
     again.start()
     up(1)
     again.wait_recv()
     up(3)
     for s in range(zs):
-        cross[2][s].wait_recv()
+        relay.cross(2, s).wait_recv()
 
     def down_part(r, side):
         rows = pl.ds(r * quarter, quarter)
@@ -682,70 +752,24 @@
     add_rows(wires, down_part, keep, acc, bufs)
 
     def second(rows):
-        summed[rows, :] = hidden[rows, :] + keep[rows, :] + vecs[4:5, :]
+        hidden[rows, :] += keep[rows, :] + vecs[4:5, :]
 
     row_loop(quarter, 32, second)
-    for at in range(3):
-        lent[at].wait_send()
-        for s in range(zs):
-            if s:
-                turns[at][s].wait_send()
-            cross[at][s].wait_send()
-
-    @pl.when(holds)
-    def _():
-        for far in there:
-            far.wait_send()
-
-    for member in (to_y, to_core, again):
-        member.wait_send()
-
-
-def run_front(pieces, tokens, time_row, ids, head_size):
-    low, f32 = jnp.bfloat16, jnp.float32
-    length, width = ids.shape[0], tokens.shape[1]
-    quarter, half, zs = length // 4, width // 2, 4
-    blocks = pieces[1].shape[2]
-    vmem = pl.BlockSpec(memory_space=pltpu.VMEM)
-    shapes = [
-        ((zs, 2, half + 2 * TILE, 4 * head_size), low),
-        ((zs, 2, half, blocks), low),
-        ((zs, 2, half, blocks), low),
-        ((length, width), low),
-        ((zs, length, 3 * head_size), low),
-        ((zs, length, head_size), low),
-        ((2, half, zs * head_size), low),
-        ((length, width), low),
-        ((length, zs * blocks), f32),
-        ((length, zs * blocks), low),
-        ((quarter, width), f32),
-        ((quarter, 1), f32),
-        ((quarter, width), f32),
-        ((quarter, width), f32),
-        ((8, width), f32),
-    ]
-    return pl.pallas_call(
-        front_kernel,
-        out_shape=[jax.ShapeDtypeStruct(*s) for s in shapes],
-        in_specs=[vmem] * 3 + [pl.BlockSpec(memory_space=pl.ANY)] + [vmem] * 3,
-        out_specs=[vmem] * len(shapes),
-        scratch_shapes=[
-            pltpu.VMEM((length, width), low),
-            pltpu.VMEM((2, quarter, width), low),
-            pltpu.VMEM((2, quarter, width), low),
-            pltpu.VMEM((quarter, width), low),
-            pltpu.VMEM((quarter, width), low),
-            pltpu.VMEM((quarter, width), f32),
-            pltpu.VMEM((quarter, width), f32),
-            pltpu.SemaphoreType.DMA((64,)),
-            pltpu.SemaphoreType.DMA((64,)),
-            pltpu.SemaphoreType.DMA((16,)),
-        ],
-        compiler_params=pltpu.CompilerParams(
-            collective_id=0, has_side_effects=True, vmem_limit_bytes=60 << 20
-        ),
-        name="front",
-    )(*pieces, tokens, time_row, ids[:, None], ids[None, :])
+
+    def finish():
+        for at in range(3):
+            lent[at].wait_send()
+        relay.finish()
+
+        @pl.when(holds)
+        def _():
+            for far in there:
+                far.wait_send()
+
+        for member in (to_y, to_core, again):
+            member.wait_send()
+
+    return finish
 
 
 def plane_sum(wires, value, slots):
@@ -870,14 +894,14 @@
             self.copy(step).wait_send()
 
 
-def back_kernel(
-    w_head, w_up, w_down, emb, proj, ctx, w_out, hid, pre, act, normed_one, inverse_one, summed, vecs, upstream,
+def back_part_of(
+    wires, w_head, w_up, w_down, emb, proj, ctx, w_out, hid, pre, act, normed_one, inverse_one, summed, vecs, upstream,
     ids_col, ids_row,
     block_out, input_out, res_head, res_up, res_down, res_tile, feature, norm,
     two, slope, one, grad_ctx, grad_proj, two_full, one_full, send_c, recv_c, send_y, recv_y, keep, acc,
     near_head, far_head, got_head, came_head, near_up, far_up, got_up, came_up, near_down, far_down, got_down, came_down,
     out_one, out_two, feat, slots, scalar, scalar_slots, key_sum, value_sum, y_feat, x_feat, y_scalar, x_scalar,
-    send_sem, recv_sem, out_sem, local_sem,
+    out_sem, local_sem,
 ):
     at_x, at_core, at_z, at_y = spots()
     low, f32 = jnp.bfloat16, jnp.float32
@@ -887,8 +911,6 @@
     block = half // 2
     head_size = ctx.shape[2]
     in_size = 3 * head_size
-    wires = Wires(send_sem, recv_sem)
-    greet(True)
     feat[...] = jnp.zeros_like(feat)
 
     def lanes(h):
@@ -929,8 +951,11 @@
     slopes(0)
     to_core.wait_recv()
     slopes(2)
+    apart = (at_core - lax.div(at_z, 2)) * (at_core - lax.div(at_z, 2))
+    close = (1 - apart) * lax.rem(at_z, 2) + apart * (1 - at_core)
     to_y.wait_recv()
     again.start()
+    outlets[0].forward(close, 0)
     slopes(1)
     again.wait_recv()
     slopes(3)
@@ -1039,9 +1064,9 @@
     start_turns("down")
     again.wait_recv()
     contexts(3)
-    for place in range(2):
-        for core in range(2):
-            outlets[0].forward(place, core)
+    outlets[0].forward(close, 1)
+    outlets[0].forward(1 - close, 0)
+    outlets[0].forward(1 - close, 1)
     scale = head_size**-0.5
 
     def attend(s):
@@ -1148,9 +1173,12 @@
         near = groups[name][0]
         mine = near.at[0, pl.ds(pl.multiple_of(at_core * block, block), block)]
         other = near.at[0, pl.ds(pl.multiple_of((1 - at_core) * block, block), block)]
-        local = pltpu.make_async_copy(mine, result.at[at_core], local_sem.at[2 + at])
+        place = result.at[at_core]
+        if name != "head":
+            place = result.at[:, pl.ds(pl.multiple_of(at_core * block, block), block)]
+        local = pltpu.make_async_copy(mine, place, local_sem.at[2 + at])
         local.start()
-        remote = wires.make(other, result.at[at_core], core=1 - at_core)
+        remote = wires.make(other, place, core=1 - at_core)
         remote.start()
         backs += [local, remote]
     tile = near_head.at[0, pl.ds(half, TILE)]
@@ -1197,76 +1225,123 @@
         outlet.finish()
 
 
-def run_back(front, upstream, ids, tokens_shape):
+def layer_kernel(
+    head_piece, up_piece, down_piece, tokens, cotangent, time_row, ids_col, ids_row,
+    block_out, input_out, res_head, res_up, res_down, res_tile, feature, norm,
+    w_head, w_up, w_down, emb, proj, ctx, w_out, hid, pre, act, normed_one, inverse_one, hidden, vecs, upstream, tok,
+    *rest,
+):
+    mids, gather_sems = rest[:-9], rest[-4:]
+    send_sem, recv_sem, out_sem, local_sem, front_sem = rest[-9:-4]
+    shared = mids[7:13]
+    wires = Wires(send_sem, recv_sem)
+    greet(True)
+    finish = front_part(
+        wires, head_piece, up_piece, down_piece, tokens, cotangent, time_row, ids_col, ids_row,
+        w_head, w_up, w_down, emb, proj, ctx, w_out, hid, pre, act, normed_one, inverse_one, hidden, vecs, upstream,
+        tok, *shared, front_sem, gather_sems,
+    )
+    quarter = hidden.shape[0]
+    out_one, out_two = tok.at[pl.ds(2 * quarter, quarter)], tok.at[pl.ds(3 * quarter, quarter)]
+    back_part_of(
+        wires, w_head, w_up, w_down, emb, proj, ctx, w_out, hid, pre, act, normed_one, inverse_one, hidden, vecs,
+        upstream, ids_col, ids_row,
+        block_out, input_out, res_head, res_up, res_down, res_tile, feature, norm,
+        *mids[:25], out_one, out_two, *mids[25:], out_sem, local_sem,
+    )
+    finish()
+
+
+def run_layer(pieces, tokens, cotangent, time_row, ids, head_size):
     low, f32 = jnp.bfloat16, jnp.float32
-    (w_head, w_up, w_down, emb, proj, ctx, w_out, hid, pre, act, normed_one, inverse_one, _, summed, vecs) = front
-    length, width = emb.shape
-    zs, _, span, packed = w_head.shape
+    length, width = ids.shape[0], tokens.shape[1]
+    zs = 4
     quarter, half, block = length // 4, width // 2, width // 4
-    head_size = ctx.shape[2]
+    units = pieces[1].shape[2]
     vmem = pl.BlockSpec(memory_space=pltpu.VMEM)
     anywhere = pl.BlockSpec(memory_space=pl.ANY)
     shape = jax.ShapeDtypeStruct
-    inputs = (w_head, w_up, w_down, emb, proj, ctx, w_out, hid, pre, act, normed_one, inverse_one, summed, vecs,
-              upstream, ids[:, None], ids[None, :])
-    head_rows = half + TILE
-
-    def triple(size):
-        return [pltpu.VMEM((n, size, block), d) for n, d in ((zs, f32), (zs, low), (zs, low), (zs - 1, low))]
-
+    kept = [
+        ((zs, 2, half + 2 * TILE, 4 * head_size), low),
+        ((zs, 2, half, units), low),
+        ((zs, 2, half, units), low),
+        ((length, width), low),
+        ((zs, length, 3 * head_size), low),
+        ((zs, length, head_size), low),
+        ((2, half, zs * head_size), low),
+        ((length, width), low),
+        ((length, zs * units), f32),
+        ((length, zs * units), low),
+        ((quarter, width), f32),
+        ((quarter, 1), f32),
+        ((quarter, width), f32),
+        ((8, width), f32),
+        ((quarter, width), low),
+        ((length, width), low),
+    ]
+
+    def group(size):
+        return [((n, size, block), d) for n, d in ((zs, f32), (zs, low), (zs, low), (zs - 1, low))]
+
+    worked = [
+        ((length, width), low),
+        ((length, width), low),
+        ((length, width), low),
+        ((zs, length, head_size), low),
+        ((zs, length, 3 * head_size), low),
+        ((quarter, width), f32),
+        ((quarter, width), f32),
+        ((2, quarter, width), low),
+        ((2, quarter, width), low),
+        ((quarter, width), low),
+        ((quarter, width), low),
+        ((quarter, width), f32),
+        ((quarter, width), f32),
+        *group(half + TILE),
+        *group(half),
+        *group(half),
+        ((8, width), f32),
+        ((8, 8, width), f32),
+        ((8, 128), f32),
+        ((9, 8, 128), f32),
+        ((length, head_size), f32),
+        ((length, head_size), f32),
+        ((8, width), f32),
+        ((8, half), f32),
+        ((8, 128), f32),
+        ((8, 128), f32),
+    ]
     return pl.pallas_call(
-        back_kernel,
+        layer_kernel,
         out_shape=[
-            shape(tokens_shape, low),
-            shape(tokens_shape, low),
+            shape(tokens.shape, low),
+            shape(tokens.shape, low),
             shape((2, block, block), f32),
-            shape((2, block, block), f32),
-            shape((2, block, block), f32),
+            shape((block, 2 * block), f32),
+            shape((block, 2 * block), f32),
             shape((2, TILE, block), f32),
             shape((8, half), f32),
             shape((8, 128), f32),
         ],
-        in_specs=[vmem] * len(inputs),
+        in_specs=[vmem] * 3 + [anywhere] * 2 + [vmem] * 3,
         out_specs=[anywhere] * 2 + [vmem] * 6,
-        scratch_shapes=[
-            pltpu.VMEM((length, width), low),
-            pltpu.VMEM((length, width), low),
-            pltpu.VMEM((length, width), low),
-            pltpu.VMEM((zs, length, head_size), low),
-            pltpu.VMEM((zs, length, 3 * head_size), low),
-            pltpu.VMEM((quarter, width), f32),
-            pltpu.VMEM((quarter, width), f32),
-            pltpu.VMEM((2, quarter, width), low),
-            pltpu.VMEM((2, quarter, width), low),
-            pltpu.VMEM((quarter, width), low),
-            pltpu.VMEM((quarter, width), low),
-            pltpu.VMEM((quarter, width), f32),
-            pltpu.VMEM((quarter, width), f32),
-            *triple(head_rows),
-            *triple(half),
-            *triple(half),
-            pltpu.VMEM((quarter, width), low),
-            pltpu.VMEM((quarter, width), low),
-            pltpu.VMEM((8, width), f32),
-            pltpu.VMEM((8, 8, width), f32),
-            pltpu.VMEM((8, 128), f32),
-            pltpu.VMEM((9, 8, 128), f32),
-            pltpu.VMEM((length, head_size), f32),
-            pltpu.VMEM((length, head_size), f32),
-            pltpu.VMEM((8, width), f32),
-            pltpu.VMEM((8, half), f32),
-            pltpu.VMEM((8, 128), f32),
-            pltpu.VMEM((8, 128), f32),
-            pltpu.SemaphoreType.DMA((72,)),
-            pltpu.SemaphoreType.DMA((72,)),
+        scratch_shapes=[pltpu.VMEM(*member) for member in kept + worked]
+        + [
+            pltpu.SemaphoreType.DMA((128,)),
+            pltpu.SemaphoreType.DMA((128,)),
             pltpu.SemaphoreType.DMA((2, 4, 8)),
             pltpu.SemaphoreType.DMA((6,)),
+            pltpu.SemaphoreType.DMA((16,)),
+            pltpu.SemaphoreType.DMA((3, 6)),
+            pltpu.SemaphoreType.DMA((3, 4)),
+            pltpu.SemaphoreType.DMA((3, 4)),
+            pltpu.SemaphoreType.DMA((3, 4)),
         ],
         compiler_params=pltpu.CompilerParams(
-            collective_id=1, has_side_effects=True, vmem_limit_bytes=67000000
+            collective_id=0, has_side_effects=True, vmem_limit_bytes=67000000
         ),
-        name="back",
-    )(*inputs)
+        name="layer",
+    )(*pieces, tokens, cotangent, time_row, ids[:, None], ids[None, :])
 
 
 def on_grid(*arguments):
@@ -1335,12 +1410,6 @@
     own_ids = lax.dynamic_slice_in_dim(segment_ids, local, 1, 0)
     own_ids = borrow(own_ids, own_ids)[0]
 
-    def at_quarter(which):
-        return lax.dynamic_slice_in_dim(cotangent, local * length + which * quarter, quarter, 0)
-
-    upstream = borrow(at_quarter(place), at_quarter(place ^ 2))
-    upstream = swap_halves(upstream, swapped)
-
     def relative(values):
         return jnp.concatenate(
             [lax.dynamic_slice_in_dim(values, (place ^ turnover) * quarter, quarter, 0) for turnover in range(4)],
@@ -1350,15 +1419,12 @@
     time_row = swap_halves(own_time.astype(f32), swapped)
     segments = relative(own_ids)
 
-    front = run_front(pieces, tokens, time_row, segments, head_size)
-    block_output, input_grad, res_head, res_up, res_down, tiles, feature, norm = run_back(
-        front, upstream, segments, tokens.shape
+    block_output, input_grad, res_head, sent_up, sent_down, tiles, feature, norm = run_layer(
+        pieces, tokens, cotangent, time_row, segments, head_size
     )
     in_size = 3 * head_size
     sent_in = jnp.concatenate([res_head[0, :, :in_size], res_head[1, :, :in_size]], axis=1)
     sent_out = jnp.concatenate([res_head[0, :, in_size:], res_head[1, :, in_size:]], axis=1)
-    sent_up = jnp.concatenate([res_up[0], res_up[1]], axis=1)
-    sent_down = jnp.concatenate([res_down[0], res_down[1]], axis=1)
     sent_head = lax.dynamic_slice(
         tiles[:, 0], (0, at_x * 2 * head_size + at_core * small_rows), (2, small_rows)
     ).T

time: 385 us -> 352 us (0.914)
  Pallas kernels: 338 us -> 308 us
    pallas_call x2 -> x1, Pallas kernels: 338 us -> 308 us  [run_layer(): pl.pallas_call(layer_kernel, out_shape=[shape(tokens.shape, low), shape(t...]
  transfers between devices with their start and end apart: 3 -> 2, of which waited for: 0 -> 0; matrix products, arithmetic and copies ran while one was open for 3% -> 3% of each run, Pallas kernels for 32% -> 0%
where the time goes in v4:
time: 352 us; the launch traced here: 349 us
  Pallas kernels  308 us (88%)
  other arithmetic  23.1 us (7%)
  local copies, waits for them, and re-layouts  11.9 us (3%)
    pallas_call x1, Pallas kernels, run_layer(): pl.pallas_call(layer_kernel, out_shape=[shape(tokens.shape, low), shape(t...  308 us
    sub x8, other arithmetic, adam_update(): return (weight - rate * (corrected + decay * weight), moment, square)  9.09 us
  transfers between devices with their start and end apart: 2, of which 0 were waited for; matrix products, arithmetic and copies ran while one was open for 3% of the time, Pallas kernels for 0%

profile of v4, /device:TPU:1, one launch (start us, length us, event | category | flops | bytes accessed | tf_op | source)
XLA Modules:
  0.0 348.9 jit_solution(5980740974213891623)
XLA Ops:
  0.7 0.0 copy-start.20
  0.7 0.7 constant_dynamic-slice_fusion.8
  1.4 1.3 collective-permute-start
  2.7 0.7 constant_dynamic-slice_fusion.7
  3.4 1.3 collective-permute-start.1
  4.7 0.7 maximum_bitcast_fusion.2
  5.5 0.1 dynamic_update_slice.21
  5.6 0.8 slice_bitcast_fusion.11
  6.4 0.8 slice_bitcast_fusion.9
  7.1 0.9 convert.41
  8.0 0.1 fusion.24
  8.1 1.0 convert.40
  9.2 0.1 fusion.23
  9.3 0.3 dynamic_update_slice.22
  9.6 0.3 dynamic_update_slice.25
  9.9 1.1 convert.44
  11.0 1.1 convert.45
  12.1 0.3 dynamic_update_slice.23
  12.4 0.3 dynamic_update_slice.26
  12.6 0.1 maximum_bitcast_fusion
  12.8 0.7 pad_maximum_fusion.head_piece
  13.5 0.8 pad_maximum_fusion.1
  14.3 0.0 collective-permute-done
  14.4 0.6 broadcast_select_fusion.2.time_row
  15.0 0.0 collective-permute-done.1
  15.0 0.0 copy-done.20
  15.0 0.0 copy-start.15
  15.0 1.0 copy.55.ids_col
  16.1 308.4 %layer.1 = (bf16[2048,1024]{1,0:T(8,128)(2,1)}, bf16[2048,1024]{1,0:T(8,128)(2,1)}, f32[2,256,256]{2,1,0:T(8,128)}, f32[256,512]{1,0:T(8,128)}, f32[256,512]{1,0...) custom-call(bf16[2,272,256]{2,1,0:T(8,128)(2,1)} %pad_maximum_fusion.head_piece, ...), custom_call_target="tpu_custom_call" | custom-call | tf_op jit(solution)/shard_map/layer/pallas_call | solution.py:1314
  324.5 1.1 slice_bitcast_fusion.1
  325.5 1.1 slice_bitcast_fusion.7
  326.6 0.0 copy-start.1
  326.6 0.0 copy-start.4
  326.6 0.0 copy-start.5
  326.7 0.0 copy-start.2
  326.7 0.0 copy-start.6
  326.7 0.0 copy-start.7
  326.7 0.0 copy-start.8
  326.7 6.8 %convert_element_type.10 = f32[2048,1024]{1,0:T(8,128)} convert(bf16[2048,1024]{1,0:T(8,128)(2,1)} %get-tuple-element.36) | non-fusion elementwise | flops 2097152 | bytes 12582912 | tf_op jit(solution)/shard_map/convert_element_type | solution.py:1440
  333.5 0.0 copy-start.24
  333.5 0.0 copy-start.25
  333.5 0.0 copy-start.18
  333.6 0.0 copy-start.26
  333.6 0.0 copy-start.27
  333.6 0.0 copy-start.17
  333.6 0.0 copy-start.22
  333.6 0.0 copy-start.23
  333.6 0.0 copy-start.3
  333.6 0.0 copy-start.11
  333.6 0.0 copy-start.12
  333.7 1.3 slice.91
  335.7 0.8 fusion.25
  336.5 0.1 fusion.14
  336.6 0.0 copy-done.1
  336.6 0.0 copy-done.5
  336.6 1.4 multiply_subtract_fusion.1
  338.1 1.4 multiply_subtract_fusion
  339.5 0.6 multiply_subtract_fusion.7
  340.1 0.7 multiply_subtract_fusion.6
  340.8 1.3 multiply_subtract_fusion.5
  342.1 1.4 multiply_subtract_fusion.4
  343.5 1.3 multiply_subtract_fusion.2
  344.9 0.9 multiply_subtract_fusion.3
  345.8 2.0 copy.64
  (50 shorter events, 0.2 us)
Async XLA Ops:
  0.7 13.7 %copy-start.16 = (bf16[2,1024]{1,0:T(2,128)(2,1)S(1)}, bf16[2,1024]{1,0:T(2,128)(2,1)}, u32[]{:S(2)}) copy-start(bf16[2,1024]{1,0:T(2,128)(2,1)} %param.29) | copy-start | bytes 12292
  0.7 14.3 %copy-start.20 = (s32[2,1024]{1,0:T(2,128)S(1)}, s32[2,1024]{1,0:T(2,128)}, u32[]{:S(2)}) copy-start(s32[2,1024]{1,0:T(2,128)} %param.30) | copy-start | bytes 24580
  1.4 12.9 %collective-permute-start = (bf16[1,1024]{1,0:T(2,128)(2,1)S(1)}, bf16[1,1024]{1,0:T(2,128)(2,1)S(1)}, u32[]{:S(2)}, u32[]{:S(2)}) collective-permute-start(bf16[1,1024]{1,0:T(2,128)(2,1)S(1)} %constant_dynamic-slice_fusion.8), channel_id=1, source_target_pairs={{0,8},{2,10},{12,4},{14,6},{1,9},{3,11},{13,5},{15,7},{16,24},{18,... | collective-permute-start | bytes 6152 | tf_op jit(solution)/shard_map/ppermute | solution.py:1405
  3.4 11.5 %collective-permute-start.1 = (s32[1,1024]{1,0:T(1,128)S(1)}, s32[1,1024]{1,0:T(1,128)S(1)}, u32[]{:S(2)}, u32[]{:S(2)}) collective-permute-start(s32[1,1024]{1,0:T(1,128)S(1)} %constant_dynamic-slice_fusion.7), channel_id=1, source_target_pairs={{0,8},{2,10},{12,4},{14,6},{1,9},{3,11},{13,5},{15,7},{16,24},{18,... | collective-permute-start | bytes 12296 | tf_op jit(solution)/shard_map/ppermute | solution.py:1405
  15.0 1.0 copy-start.15
  326.6 9.9 %copy-start.1 = (f32[256,512]{1,0:T(8,128)S(1)}, f32[256,512]{1,0:T(8,128)}, u32[]{:S(2)}) copy-start(f32[256,512]{1,0:T(8,128)} %param.38) | copy-start | bytes 1572868
  326.6 9.9 %copy-start.4 = (f32[256,512]{1,0:T(8,128)S(1)}, f32[256,512]{1,0:T(8,128)}, u32[]{:S(2)}) copy-start(f32[256,512]{1,0:T(8,128)} %param.39) | copy-start | bytes 1572868
  326.6 9.9 %copy-start.5 = (f32[256,512]{1,0:T(8,128)S(1)}, f32[256,512]{1,0:T(8,128)}, u32[]{:S(2)}) copy-start(f32[256,512]{1,0:T(8,128)} %param.40) | copy-start | bytes 1572868
  326.7 9.9 %copy-start.9 = (f32[256,512]{1,0:T(8,128)S(1)}, f32[256,512]{1,0:T(8,128)}, u32[]{:S(2)}) copy-start(f32[256,512]{1,0:T(8,128)} %get-tuple-element.39) | copy-start | bytes 1572868
  326.7 11.4 %copy-start.2 = (f32[256,512]{1,0:T(8,128)S(1)}, f32[256,512]{1,0:T(8,128)}, u32[]{:S(2)}) copy-start(f32[256,512]{1,0:T(8,128)} %param.41) | copy-start | bytes 1572868
  326.7 11.3 %copy-start.6 = (f32[256,512]{1,0:T(8,128)S(1)}, f32[256,512]{1,0:T(8,128)}, u32[]{:S(2)}) copy-start(f32[256,512]{1,0:T(8,128)} %param.42) | copy-start | bytes 1572868
  326.7 11.3 %copy-start.7 = (f32[256,512]{1,0:T(8,128)S(1)}, f32[256,512]{1,0:T(8,128)}, u32[]{:S(2)}) copy-start(f32[256,512]{1,0:T(8,128)} %param.43) | copy-start | bytes 1572868
  326.7 11.3 %copy-start.8 = (f32[256,512]{1,0:T(8,128)S(1)}, f32[256,512]{1,0:T(8,128)}, u32[]{:S(2)}) copy-start(f32[256,512]{1,0:T(8,128)} %get-tuple-element.40) | copy-start | bytes 1572868
  333.5 6.0 %copy-start.21 = (f32[32,2]{0,1:T(2,128)S(1)}, f32[32,2]{0,1:T(2,128)}, u32[]{:S(2)}) copy-start(f32[32,2]{0,1:T(2,128)} %param.44) | copy-start | bytes 772
  333.5 6.0 %copy-start.28 = (f32[32,2]{0,1:T(2,128)S(1)}, f32[32,2]{0,1:T(2,128)}, u32[]{:S(2)}) copy-start(f32[32,2]{0,1:T(2,128)} %param.45) | copy-start | bytes 772
  333.5 6.0 %copy-start.29 = (f32[32,2]{0,1:T(2,128)S(1)}, f32[32,2]{0,1:T(2,128)}, u32[]{:S(2)}) copy-start(f32[32,2]{0,1:T(2,128)} %param.46) | copy-start | bytes 772
  333.5 6.6 %copy-start.19 = (f32[32,4]{0,1:T(4,128)S(1)}, f32[32,4]{0,1:T(4,128)}, u32[]{:S(2)}) copy-start(f32[32,4]{0,1:T(4,128)} %param.47) | copy-start | bytes 1540
  333.5 6.6 %copy-start.24 = (f32[32,4]{0,1:T(4,128)S(1)}, f32[32,4]{0,1:T(4,128)}, u32[]{:S(2)}) copy-start(f32[32,4]{0,1:T(4,128)} %param.48) | copy-start | bytes 1540
  333.5 6.6 %copy-start.25 = (f32[32,4]{0,1:T(4,128)S(1)}, f32[32,4]{0,1:T(4,128)}, u32[]{:S(2)}) copy-start(f32[32,4]{0,1:T(4,128)} %param.49) | copy-start | bytes 1540
  333.5 7.2 %copy-start.18 = (f32[256,2]{0,1:T(2,128)S(1)}, f32[256,2]{0,1:T(2,128)}, u32[]{:S(2)}) copy-start(f32[256,2]{0,1:T(2,128)} %param.50) | copy-start | bytes 6148
  333.6 7.2 %copy-start.26 = (f32[256,2]{0,1:T(2,128)S(1)}, f32[256,2]{0,1:T(2,128)}, u32[]{:S(2)}) copy-start(f32[256,2]{0,1:T(2,128)} %param.51) | copy-start | bytes 6148
  333.6 7.2 %copy-start.27 = (f32[256,2]{0,1:T(2,128)S(1)}, f32[256,2]{0,1:T(2,128)}, u32[]{:S(2)}) copy-start(f32[256,2]{0,1:T(2,128)} %param.52) | copy-start | bytes 6148
  333.6 8.5 %copy-start.17 = (f32[256,4]{0,1:T(4,128)S(1)}, f32[256,4]{0,1:T(4,128)}, u32[]{:S(2)}) copy-start(f32[256,4]{0,1:T(4,128)} %param.53) | copy-start | bytes 12292
  333.6 8.5 %copy-start.22 = (f32[256,4]{0,1:T(4,128)S(1)}, f32[256,4]{0,1:T(4,128)}, u32[]{:S(2)}) copy-start(f32[256,4]{0,1:T(4,128)} %param.54) | copy-start | bytes 12292
  333.6 8.5 %copy-start.23 = (f32[256,4]{0,1:T(4,128)S(1)}, f32[256,4]{0,1:T(4,128)}, u32[]{:S(2)}) copy-start(f32[256,4]{0,1:T(4,128)} %param.55) | copy-start | bytes 12292
  333.6 9.9 %copy-start.3 = (f32[256,384]{1,0:T(8,128)S(1)}, f32[256,384]{1,0:T(8,128)}, u32[]{:S(2)}) copy-start(f32[256,384]{1,0:T(8,128)} %param.32) | copy-start | bytes 1179652
  333.6 9.9 %copy-start.11 = (f32[256,384]{1,0:T(8,128)S(1)}, f32[256,384]{1,0:T(8,128)}, u32[]{:S(2)}) copy-start(f32[256,384]{1,0:T(8,128)} %param.33) | copy-start | bytes 1179652
  333.6 9.9 %copy-start.12 = (f32[256,384]{1,0:T(8,128)S(1)}, f32[256,384]{1,0:T(8,128)}, u32[]{:S(2)}) copy-start(f32[256,384]{1,0:T(8,128)} %param.34) | copy-start | bytes 1179652
  338.0 6.8 %copy-start.10 = (f32[256,128]{1,0:T(8,128)S(1)}, f32[256,128]{1,0:T(8,128)}, u32[]{:S(2)}) copy-start(f32[256,128]{1,0:T(8,128)} %param.35) | copy-start | bytes 393220
  338.0 6.8 %copy-start.13 = (f32[256,128]{1,0:T(8,128)S(1)}, f32[256,128]{1,0:T(8,128)}, u32[]{:S(2)}) copy-start(f32[256,128]{1,0:T(8,128)} %param.36) | copy-start | bytes 393220
  338.0 6.8 %copy-start.14 = (f32[256,128]{1,0:T(8,128)S(1)}, f32[256,128]{1,0:T(8,128)}, u32[]{:S(2)}) copy-start(f32[256,128]{1,0:T(8,128)} %param.37) | copy-start | bytes 393220
  338.0 7.8 %copy-start = (bf16[2048,1024]{1,0:T(8,128)(2,1)S(1)}, bf16[2048,1024]{1,0:T(8,128)(2,1)}, u32[]{:S(2)}) copy-start(bf16[2048,1024]{1,0:T(8,128)(2,1)} %get-tuple-element.122) | copy-start | bytes 12582916

commit v5 on v4

--- a/solution.py
+++ b/solution.py
@@ -558,7 +558,8 @@
 
 
 def front_part(
-    wires, head_piece, up_piece, down_piece, tokens, cotangent, time_row, ids_col, ids_row,
+    wires, in_full, out_full, up_full, down_full, tiles, tokens, cotangent, times, ids,
+    head_piece, up_piece, down_piece, time_row, ids_col, ids_row,
     w_head, w_up, w_down, emb, proj, ctx, w_out, hid, pre, act, normed_one, inverse_one, hidden, vecs, upstream,
     tok, send_c, recv_c, send_y, recv_y, keep, acc, local_sem, gather_sems,
 ):
@@ -571,6 +572,15 @@
     head_size = ctx.shape[2]
     in_size = 3 * head_size
 
+    split = in_full.shape[1] // 2
+    for h in range(2):
+        head_piece[h, 0 : half // 2, 0:split] = in_full[:, h * split : (h + 1) * split].astype(low)
+        head_piece[h, 0 : half // 2, split:] = out_full[:, h * head_size : (h + 1) * head_size].astype(low)
+        head_piece[h, half // 2 :, :] = tiles[h].astype(low)
+    for full, piece in ((up_full, up_piece), (down_full, down_piece)):
+        for h in range(2):
+            piece[h] = full[:, h * piece.shape[2] : (h + 1) * piece.shape[2]].astype(low)
+
     kept, lent = [], []
     for at, (piece, target) in enumerate(((head_piece, w_head), (up_piece, w_up), (down_piece, w_down))):
         size = piece.shape[1]
@@ -606,6 +616,22 @@
         here.append(pltpu.make_async_copy(above(at_core), spot, local_sem.at[11 + h]))
         there.append(wires.make(above(1 - at_core), spot, core=1 - at_core))
 
+    local = lax.rem(at_z, 2)
+    for h in range(2):
+        source = times.at[local, :, pl.ds(h * half, half)]
+        spot = time_row.at[:, pl.ds(pl.multiple_of(flipped(at_x, h) * half, half), half)]
+        here.append(pltpu.make_async_copy(source, spot, local_sem.at[13 + h]))
+        there.append(wires.make(source, spot, core=1 - at_core))
+    for r in range(4):
+        spot = ids_row.at[:, pl.ds(r * quarter, quarter)]
+
+        def stretch(core):
+            at = flipped(core, r // 2) * 2 + flipped(at_y, r % 2)
+            return ids.at[local, :, pl.ds(pl.multiple_of(at * quarter, quarter), quarter)]
+
+        here.append(pltpu.make_async_copy(stretch(at_core), spot, local_sem.at[15 + r]))
+        there.append(wires.make(stretch(1 - at_core), spot, core=1 - at_core))
+
     @pl.when(holds)
     def _():
         for near, far in zip(here, there):
@@ -628,6 +654,8 @@
     def _():
         for far in there:
             far.wait_recv()
+
+    ids_col[...] = jnp.transpose(jnp.broadcast_to(ids_row[...], (8, length)))[:, 0:1]
 
     def embed(rows):
         emb[rows, :] = (tok[rows, :].astype(f32) + time_row[...]).astype(low)
@@ -894,6 +922,77 @@
             self.copy(step).wait_send()
 
 
+class Chain(Outlet):
+    def leave(self, rise, send):
+        return pltpu.make_async_remote_copy(
+            src_ref=self.own,
+            dst_ref=self.spot(lax.rem(self.at_z, 2), self.at_core, self.at_y),
+            send_sem=self.sends.at[send],
+            recv_sem=self.receives.at[lax.rem(self.at_z, 2) * 2 + self.at_core],
+            device_id={"core": lax.div(self.at_z, 2), "z": self.at_z + rise},
+            device_id_type=MESH_ID,
+        )
+
+    def leaving(self, act):
+        apart = jnp.logical_not(self.at_core == lax.div(self.at_z, 2))
+        for rise, send, inside in ((1, 1, self.at_z < 3), (-1, 2, self.at_z > 0), (0, 0, apart)):
+
+            @pl.when(inside)
+            def _():
+                act(self.leave(rise, send))
+
+    def start(self):
+        @pl.when(self.at_core == lax.div(self.at_z, 2))
+        def _():
+            self.stay().start()
+
+        self.leaving(lambda copy: copy.start())
+
+    def hop(self, place, core, rise):
+        spot = self.spot(place, core, self.at_y)
+        at = place * 2 + core
+        return pltpu.make_async_remote_copy(
+            src_ref=spot,
+            dst_ref=spot,
+            send_sem=self.sends.at[4 + at],
+            recv_sem=self.receives.at[at],
+            device_id={"z": self.at_z + rise},
+            device_id_type=MESH_ID,
+        )
+
+    def hops(self, place, core, act):
+        source = 2 * self.at_core + place
+        for rise, inside in (
+            (1, jnp.logical_and(source < self.at_z, self.at_z < 3)),
+            (-1, jnp.logical_and(source > self.at_z, self.at_z > 0)),
+        ):
+
+            @pl.when(inside)
+            def _():
+                act(self.hop(place, core, rise))
+
+    def forward(self, place, core):
+        own = jnp.logical_and(2 * self.at_core + place == self.at_z, self.at_core == core)
+
+        @pl.when(own)
+        def _():
+            self.stay().wait()
+
+        @pl.when(jnp.logical_not(own))
+        def _():
+            self.hop(place, core, 0).wait_recv()
+
+        self.hops(place, core, lambda copy: copy.start())
+        self.across(place, core).start()
+
+    def finish(self):
+        self.leaving(lambda copy: copy.wait_send())
+        for place in range(2):
+            for core in range(2):
+                self.hops(place, core, lambda copy: copy.wait_send())
+                self.across(place, core).wait()
+
+
 def back_part_of(
     wires, w_head, w_up, w_down, emb, proj, ctx, w_out, hid, pre, act, normed_one, inverse_one, summed, vecs, upstream,
     ids_col, ids_row,
@@ -933,8 +1032,8 @@
     row_loop(quarter, 32, second_norm)
     to_y, to_core, again = spread_rows(wires, two, quarter)
     outlets = [
-        Outlet(own, result, *[out_sem.at[n, k] for k in range(4)], local_sem.at[n])
-        for n, (own, result) in enumerate(((out_one, block_out), (out_two, input_out)))
+        kind(own, result, *[out_sem.at[n, k] for k in range(4)], local_sem.at[n])
+        for n, (kind, own, result) in enumerate(((Outlet, out_one, block_out), (Chain, out_two, input_out)))
     ]
     outlets[0].start()
 
@@ -1147,6 +1246,9 @@
 
     block_loop(zs, head_near)
     turn_blocks("head")
+    edge = at_core * lax.div(at_z, 3) + (1 - at_core) * (1 - lax.div(3 - at_z, 3))
+    outlets[1].forward(edge, 0)
+    outlets[1].forward(edge, 1)
     start_turns("head")
 
     acc[0:8, :] = plane_total(feat_sent, slots)
@@ -1162,9 +1264,8 @@
 
     settle("down")
     settle("up")
-    for place in range(2):
-        for core in range(2):
-            outlets[1].forward(place, core)
+    outlets[1].forward(1 - edge, 0)
+    outlets[1].forward(1 - edge, 1)
     settle("head")
 
     backs = []
@@ -1226,8 +1327,9 @@
 
 
 def layer_kernel(
-    head_piece, up_piece, down_piece, tokens, cotangent, time_row, ids_col, ids_row,
+    in_full, out_full, up_full, down_full, tiles, tokens, cotangent, times, ids,
     block_out, input_out, res_head, res_up, res_down, res_tile, feature, norm,
+    head_piece, up_piece, down_piece, time_row, ids_col, ids_row,
     w_head, w_up, w_down, emb, proj, ctx, w_out, hid, pre, act, normed_one, inverse_one, hidden, vecs, upstream, tok,
     *rest,
 ):
@@ -1237,7 +1339,8 @@
     wires = Wires(send_sem, recv_sem)
     greet(True)
     finish = front_part(
-        wires, head_piece, up_piece, down_piece, tokens, cotangent, time_row, ids_col, ids_row,
+        wires, in_full, out_full, up_full, down_full, tiles, tokens, cotangent, times, ids,
+        head_piece, up_piece, down_piece, time_row, ids_col, ids_row,
         w_head, w_up, w_down, emb, proj, ctx, w_out, hid, pre, act, normed_one, inverse_one, hidden, vecs, upstream,
         tok, *shared, front_sem, gather_sems,
     )
@@ -1252,16 +1355,22 @@
     finish()
 
 
-def run_layer(pieces, tokens, cotangent, time_row, ids, head_size):
+def run_layer(weights, tiles, tokens, cotangent, times, ids, head_size):
     low, f32 = jnp.bfloat16, jnp.float32
-    length, width = ids.shape[0], tokens.shape[1]
+    length, width = ids.shape[2], tokens.shape[1]
     zs = 4
     quarter, half, block = length // 4, width // 2, width // 4
-    units = pieces[1].shape[2]
+    units = weights[2].shape[1] // 2
     vmem = pl.BlockSpec(memory_space=pltpu.VMEM)
     anywhere = pl.BlockSpec(memory_space=pl.ANY)
     shape = jax.ShapeDtypeStruct
     kept = [
+        ((2, block + TILE, 4 * head_size), low),
+        ((2, block, units), low),
+        ((2, block, units), low),
+        ((1, width), f32),
+        ((length, 1), f32),
+        ((1, length), f32),
         ((zs, 2, half + 2 * TILE, 4 * head_size), low),
         ((zs, 2, half, units), low),
         ((zs, 2, half, units), low),
@@ -1323,7 +1432,7 @@
             shape((8, half), f32),
             shape((8, 128), f32),
         ],
-        in_specs=[vmem] * 3 + [anywhere] * 2 + [vmem] * 3,
+        in_specs=[vmem] * 5 + [anywhere] * 4,
         out_specs=[anywhere] * 2 + [vmem] * 6,
         scratch_shapes=[pltpu.VMEM(*member) for member in kept + worked]
         + [
@@ -1331,7 +1440,7 @@
             pltpu.SemaphoreType.DMA((128,)),
             pltpu.SemaphoreType.DMA((2, 4, 8)),
             pltpu.SemaphoreType.DMA((6,)),
-            pltpu.SemaphoreType.DMA((16,)),
+            pltpu.SemaphoreType.DMA((20,)),
             pltpu.SemaphoreType.DMA((3, 6)),
             pltpu.SemaphoreType.DMA((3, 4)),
             pltpu.SemaphoreType.DMA((3, 4)),
@@ -1341,7 +1450,7 @@
             collective_id=0, has_side_effects=True, vmem_limit_bytes=67000000
         ),
         name="layer",
-    )(*pieces, tokens, cotangent, time_row, ids[:, None], ids[None, :])
+    )(*weights, tiles, tokens, cotangent, times, ids)
 
 
 def on_grid(*arguments):
@@ -1372,14 +1481,7 @@
         jnp.zeros((TILE, rows), f32), vectors, (2 + 6 * at_core, 0)
     )
 
-    def head_piece(half):
-        body = jnp.concatenate(
-            [
-                input_weight[:, half * 3 * head_size : (half + 1) * 3 * head_size],
-                output_weight[:, half * head_size : (half + 1) * head_size],
-            ],
-            axis=1,
-        )
+    def small_tile(half):
         tile = lax.dynamic_update_slice(
             vectors, head_bias[:, half][None], (0, at_x * 2 * head_size + at_core * small_rows)
         )
@@ -1388,39 +1490,14 @@
             hidden_bias[:, 2 * half : 2 * half + 2].T,
             (0, position * small_rows),
         )
-        tile = lax.dynamic_update_slice(tile, units.reshape(1, -1), (1, 0))
-        return jnp.concatenate([body, tile], axis=0)
-
-    pieces = [
-        jnp.stack([head_piece(0), head_piece(1)]).astype(low),
-        jnp.stack([upward_weight[:, :wide], upward_weight[:, wide:]]).astype(low),
-        jnp.stack([downward_weight[:, :wide], downward_weight[:, wide:]]).astype(low),
-    ]
-
-    seat = ("core", "z")
-    holds = at_core == at_z // 2
-    lend = [((i // 2) * zs + i, (1 - i // 2) * zs + i) for i in range(zs)]
-
-    def borrow(kept, sent):
-        return jnp.where(holds, kept, lax.ppermute(sent, seat, lend))
-
-    local = at_z % 2
-    own_time = lax.dynamic_slice_in_dim(time_embed, local, 1, 0)
-    own_time = borrow(own_time, own_time)
-    own_ids = lax.dynamic_slice_in_dim(segment_ids, local, 1, 0)
-    own_ids = borrow(own_ids, own_ids)[0]
-
-    def relative(values):
-        return jnp.concatenate(
-            [lax.dynamic_slice_in_dim(values, (place ^ turnover) * quarter, quarter, 0) for turnover in range(4)],
-            axis=0,
-        )
-
-    time_row = swap_halves(own_time.astype(f32), swapped)
-    segments = relative(own_ids)
-
+        return lax.dynamic_update_slice(tile, units.reshape(1, -1), (1, 0))
+
+    seqs = segment_ids.shape[0]
+    times = time_embed.astype(f32).reshape(seqs, 1, -1)
+    ids = segment_ids.astype(f32).reshape(seqs, 1, length)
+    small = jnp.stack([small_tile(0), small_tile(1)])
     block_output, input_grad, res_head, sent_up, sent_down, tiles, feature, norm = run_layer(
-        pieces, tokens, cotangent, time_row, segments, head_size
+        masters[:4], small, tokens, cotangent, times, ids, head_size
     )
     in_size = 3 * head_size
     sent_in = jnp.concatenate([res_head[0, :, :in_size], res_head[1, :, :in_size]], axis=1)

time: 352 us -> 342 us (0.972)
  other arithmetic: 23.1 us -> 17.3 us
    another operation x7 -> x2, other arithmetic: 5.77 us -> 1.33 us  [on_grid(): small = jnp.stack([small_tile(0), small_tile(1)])]
    sub x8 -> x7, other arithmetic: 9.09 us -> 8.46 us  [adam_update(): return (weight - rate * (corrected + decay * weight), moment, square)]
  transfers between devices with their start and end apart: 2 -> 0, of which waited for: 0 -> 0; matrix products, arithmetic and copies ran while one was open for 3% -> 0% of each run, Pallas kernels for 0% -> 0%
where the time goes in v5:
time: 342 us; the launch traced here: 339 us
  Pallas kernels  307 us (90%)
  other arithmetic  17.3 us (5%)
  local copies, waits for them, and re-layouts  11.7 us (3%)
    pallas_call x1, Pallas kernels, run_layer(): pl.pallas_call(layer_kernel, out_shape=[shape(tokens.shape, low), shape(t...  307 us
    sub x7, other arithmetic, adam_update(): return (weight - rate * (corrected + decay * weight), moment, square)  8.46 us

profile of v5, /device:TPU:1, one launch (start us, length us, event | category | flops | bytes accessed | tf_op | source)
XLA Modules:
  0.0 338.6 jit_solution(1205661164304186041)
XLA Ops:
  0.7 0.7 maximum_bitcast_fusion
  1.4 0.1 dynamic_update_slice.26
  1.5 0.8 slice_bitcast_fusion.7
  2.3 0.2 dynamic_update_slice.30
  2.5 0.8 slice_bitcast_fusion.5
  3.3 0.2 dynamic_update_slice.31
  3.5 0.3 dynamic_update_slice.27
  3.9 0.3 dynamic_update_slice.28
  4.2 0.6 pad_maximum_fusion.tiles
  4.8 1.3 reshape.95.times
  6.1 0.7 convert_element_type.7
  6.8 0.6 reshape.92.ids
  7.4 306.7 %layer.1 = (bf16[2048,1024]{1,0:T(8,128)(2,1)}, bf16[2048,1024]{1,0:T(8,128)(2,1)}, f32[2,256,256]{2,1,0:T(8,128)}, f32[256,512]{1,0:T(8,128)}, f32[256,512]{1,0...) custom-call(f32[256,384]{1,0:T(8,128)} %in_full.1, f32[256,128]{1,0:T(8,128)} %out_full.1, ...), custom_call_target="tpu_custom_call" | custom-call | tf_op jit(solution)/shard_map/layer/pallas_call | solution.py:1423
  314.1 0.0 copy-start.3
  314.1 0.0 copy-start.2
  314.1 0.0 copy-start.11
  314.1 0.0 copy-start.12
  314.1 0.0 copy-start.14
  314.1 6.8 %convert_element_type.8 = f32[2048,1024]{1,0:T(8,128)} convert(bf16[2048,1024]{1,0:T(8,128)(2,1)} %get-tuple-element.36) | non-fusion elementwise | flops 2097152 | bytes 12582912 | tf_op jit(solution)/shard_map/convert_element_type | solution.py:1517
  320.9 0.0 copy-start.5
  320.9 0.0 copy-start.6
  320.9 0.0 copy-start.7
  321.0 0.0 copy-start.8
  321.0 0.0 copy-start.9
  321.0 0.0 copy-start.10
  321.0 1.3 slice.43
  323.0 0.0 copy-done.3
  323.1 0.0 copy-done.2
  323.1 0.0 copy-done.11
  323.1 0.0 copy-done.12
  323.1 1.3 multiply_subtract_fusion.2
  324.5 0.1 slice_bitcast_fusion.3
  324.6 0.0 copy-done.14
  324.6 0.0 copy-done.4
  324.6 0.0 copy-done.13
  324.6 0.0 copy-start.18
  324.6 0.0 copy-start.25
  324.6 0.0 copy-start.26
  324.6 0.0 copy-start.17
  324.7 0.0 copy-start.21
  324.7 0.0 copy-start.22
  324.7 0.0 copy-start.16
  324.7 0.0 copy-start.23
  324.7 0.0 copy-start.24
  324.7 0.0 copy-start.15
  324.7 0.0 copy-start.19
  324.7 0.0 copy-start.20
  324.8 0.9 multiply_subtract_fusion.3
  325.7 0.0 copy-done
  325.7 0.0 copy-done.1
  325.7 0.0 copy-done.5
  325.7 0.0 copy-done.6
  325.7 0.0 copy-done.7
  325.7 2.2 multiply_subtract_fusion
  328.0 0.8 fusion.20
  328.8 0.1 dynamic-slice_multiply_fusion.3
  328.8 0.0 copy-done.18
  328.9 0.0 copy-done.26
  328.9 0.6 multiply_subtract_fusion.7
  329.5 0.7 multiply_subtract_fusion.6
  330.1 0.0 copy-done.23
  330.2 1.3 multiply_subtract_fusion.5
  331.5 1.4 multiply_subtract_fusion.4
  332.9 4.6 %copy.63 = bf16[2048,1024]{1,0:T(8,128)(2,1)} copy(bf16[2048,1024]{1,0:T(8,128)(2,1)} %get-tuple-element.107) | data formatting | bytes 8388608
  (23 shorter events, 0.1 us)
Async XLA Ops:
  314.1 9.0 %copy-start.3 = (f32[2,256,256]{2,1,0:T(8,128)S(1)}, f32[2,256,256]{2,1,0:T(8,128)}, u32[]{:S(2)}) copy-start(f32[2,256,256]{2,1,0:T(8,128)} %get-tuple-element.38) | copy-start | bytes 1572868
  314.1 9.0 %copy-start.2 = (f32[256,384]{1,0:T(8,128)S(1)}, f32[256,384]{1,0:T(8,128)}, u32[]{:S(2)}) copy-start(f32[256,384]{1,0:T(8,128)} %in_full.1) | copy-start | bytes 1179652
  314.1 9.0 %copy-start.11 = (f32[256,384]{1,0:T(8,128)S(1)}, f32[256,384]{1,0:T(8,128)}, u32[]{:S(2)}) copy-start(f32[256,384]{1,0:T(8,128)} %param.33) | copy-start | bytes 1179652
  314.1 9.0 %copy-start.12 = (f32[256,384]{1,0:T(8,128)S(1)}, f32[256,384]{1,0:T(8,128)}, u32[]{:S(2)}) copy-start(f32[256,384]{1,0:T(8,128)} %param.34) | copy-start | bytes 1179652
  314.1 10.4 %copy-start.14 = (f32[256,128]{1,0:T(8,128)S(1)}, f32[256,128]{1,0:T(8,128)}, u32[]{:S(2)}) copy-start(f32[256,128]{1,0:T(8,128)} %param.37) | copy-start | bytes 393220
  320.9 3.7 %copy-start.4 = (f32[256,128]{1,0:T(8,128)S(1)}, f32[256,128]{1,0:T(8,128)}, u32[]{:S(2)}) copy-start(f32[256,128]{1,0:T(8,128)} %out_full.1) | copy-start | bytes 393220
  320.9 3.7 %copy-start.13 = (f32[256,128]{1,0:T(8,128)S(1)}, f32[256,128]{1,0:T(8,128)}, u32[]{:S(2)}) copy-start(f32[256,128]{1,0:T(8,128)} %param.36) | copy-start | bytes 393220
  320.9 4.8 %copy-start = (f32[256,512]{1,0:T(8,128)S(1)}, f32[256,512]{1,0:T(8,128)}, u32[]{:S(2)}) copy-start(f32[256,512]{1,0:T(8,128)} %up_full.1) | copy-start | bytes 1572868
  320.9 4.8 %copy-start.1 = (f32[256,512]{1,0:T(8,128)S(1)}, f32[256,512]{1,0:T(8,128)}, u32[]{:S(2)}) copy-start(f32[256,512]{1,0:T(8,128)} %down_full.1) | copy-start | bytes 1572868
  320.9 4.8 %copy-start.5 = (f32[256,512]{1,0:T(8,128)S(1)}, f32[256,512]{1,0:T(8,128)}, u32[]{:S(2)}) copy-start(f32[256,512]{1,0:T(8,128)} %param.42) | copy-start | bytes 1572868
  320.9 4.8 %copy-start.6 = (f32[256,512]{1,0:T(8,128)S(1)}, f32[256,512]{1,0:T(8,128)}, u32[]{:S(2)}) copy-start(f32[256,512]{1,0:T(8,128)} %param.43) | copy-start | bytes 1572868
  320.9 4.8 %copy-start.7 = (f32[256,512]{1,0:T(8,128)S(1)}, f32[256,512]{1,0:T(8,128)}, u32[]{:S(2)}) copy-start(f32[256,512]{1,0:T(8,128)} %param.40) | copy-start | bytes 1572868
  321.0 4.8 %copy-start.8 = (f32[256,512]{1,0:T(8,128)S(1)}, f32[256,512]{1,0:T(8,128)}, u32[]{:S(2)}) copy-start(f32[256,512]{1,0:T(8,128)} %param.39) | copy-start | bytes 1572868
  321.0 4.8 %copy-start.9 = (f32[256,512]{1,0:T(8,128)S(1)}, f32[256,512]{1,0:T(8,128)}, u32[]{:S(2)}) copy-start(f32[256,512]{1,0:T(8,128)} %get-tuple-element.39) | copy-start | bytes 1572868
  321.0 4.8 %copy-start.10 = (f32[256,512]{1,0:T(8,128)S(1)}, f32[256,512]{1,0:T(8,128)}, u32[]{:S(2)}) copy-start(f32[256,512]{1,0:T(8,128)} %get-tuple-element.40) | copy-start | bytes 1572868
  324.6 4.2 %copy-start.18 = (f32[32,2]{0,1:T(2,128)S(1)}, f32[32,2]{0,1:T(2,128)}, u32[]{:S(2)}) copy-start(f32[32,2]{0,1:T(2,128)} %param.44) | copy-start | bytes 772
  324.6 4.2 %copy-start.25 = (f32[32,2]{0,1:T(2,128)S(1)}, f32[32,2]{0,1:T(2,128)}, u32[]{:S(2)}) copy-start(f32[32,2]{0,1:T(2,128)} %param.45) | copy-start | bytes 772
  324.6 4.2 %copy-start.26 = (f32[32,2]{0,1:T(2,128)S(1)}, f32[32,2]{0,1:T(2,128)}, u32[]{:S(2)}) copy-start(f32[32,2]{0,1:T(2,128)} %param.46) | copy-start | bytes 772
  324.6 4.8 %copy-start.17 = (f32[32,4]{0,1:T(4,128)S(1)}, f32[32,4]{0,1:T(4,128)}, u32[]{:S(2)}) copy-start(f32[32,4]{0,1:T(4,128)} %param.47) | copy-start | bytes 1540
  324.7 4.8 %copy-start.21 = (f32[32,4]{0,1:T(4,128)S(1)}, f32[32,4]{0,1:T(4,128)}, u32[]{:S(2)}) copy-start(f32[32,4]{0,1:T(4,128)} %param.48) | copy-start | bytes 1540
  324.7 4.8 %copy-start.22 = (f32[32,4]{0,1:T(4,128)S(1)}, f32[32,4]{0,1:T(4,128)}, u32[]{:S(2)}) copy-start(f32[32,4]{0,1:T(4,128)} %param.49) | copy-start | bytes 1540
  324.7 5.5 %copy-start.16 = (f32[256,2]{0,1:T(2,128)S(1)}, f32[256,2]{0,1:T(2,128)}, u32[]{:S(2)}) copy-start(f32[256,2]{0,1:T(2,128)} %param.50) | copy-start | bytes 6148
  324.7 5.4 %copy-start.23 = (f32[256,2]{0,1:T(2,128)S(1)}, f32[256,2]{0,1:T(2,128)}, u32[]{:S(2)}) copy-start(f32[256,2]{0,1:T(2,128)} %param.51) | copy-start | bytes 6148
  324.7 5.4 %copy-start.24 = (f32[256,2]{0,1:T(2,128)S(1)}, f32[256,2]{0,1:T(2,128)}, u32[]{:S(2)}) copy-start(f32[256,2]{0,1:T(2,128)} %param.52) | copy-start | bytes 6148
  324.7 6.7 %copy-start.15 = (f32[256,4]{0,1:T(4,128)S(1)}, f32[256,4]{0,1:T(4,128)}, u32[]{:S(2)}) copy-start(f32[256,4]{0,1:T(4,128)} %param.53) | copy-start | bytes 12292
  324.7 6.7 %copy-start.19 = (f32[256,4]{0,1:T(4,128)S(1)}, f32[256,4]{0,1:T(4,128)}, u32[]{:S(2)}) copy-start(f32[256,4]{0,1:T(4,128)} %param.54) | copy-start | bytes 12292
  324.7 6.7 %copy-start.20 = (f32[256,4]{0,1:T(4,128)S(1)}, f32[256,4]{0,1:T(4,128)}, u32[]{:S(2)}) copy-start(f32[256,4]{0,1:T(4,128)} %param.55) | copy-start | bytes 12292

commit v6 on v5

--- a/solution.py
+++ b/solution.py
@@ -1054,7 +1054,6 @@
     close = (1 - apart) * lax.rem(at_z, 2) + apart * (1 - at_core)
     to_y.wait_recv()
     again.start()
-    outlets[0].forward(close, 0)
     slopes(1)
     again.wait_recv()
     slopes(3)
@@ -1163,6 +1162,7 @@
     start_turns("down")
     again.wait_recv()
     contexts(3)
+    outlets[0].forward(close, 0)
     outlets[0].forward(close, 1)
     outlets[0].forward(1 - close, 0)
     outlets[0].forward(1 - close, 1)

time: 342 us -> 320 us (0.936)
  Pallas kernels: 307 us -> 284 us
    pallas_call x1, Pallas kernels: 307 us -> 284 us  [run_layer(): pl.pallas_call(layer_kernel, out_shape=[shape(tokens.shape, low), shape(t...]
where the time goes in v6:
time: 320 us; the launch traced here: 316 us
  Pallas kernels  284 us (89%)
  other arithmetic  17.3 us (5%)
  local copies, waits for them, and re-layouts  11.7 us (4%)
    pallas_call x1, Pallas kernels, run_layer(): pl.pallas_call(layer_kernel, out_shape=[shape(tokens.shape, low), shape(t...  284 us
    sub x7, other arithmetic, adam_update(): return (weight - rate * (corrected + decay * weight), moment, square)  8.46 us
    convert_element_type x1, other arithmetic, on_grid(): results = [block_output, input_grad.astype(f32), grad_norm.reshape(1)]  6.76 us

profile of v6, /device:TPU:1, one launch (start us, length us, event | category | flops | bytes accessed | tf_op | source)
XLA Modules:
  0.0 316.2 jit_solution(15074053598403327198)
XLA Ops:
  0.7 0.7 maximum_bitcast_fusion
  1.4 0.1 dynamic_update_slice.26
  1.5 0.8 slice_bitcast_fusion.7
  2.3 0.2 dynamic_update_slice.30
  2.5 0.8 slice_bitcast_fusion.5
  3.3 0.2 dynamic_update_slice.31
  3.5 0.3 dynamic_update_slice.27
  3.9 0.3 dynamic_update_slice.28
  4.2 0.6 pad_maximum_fusion.tiles
  4.8 1.3 reshape.95.times
  6.1 0.7 convert_element_type.7
  6.8 0.6 reshape.92.ids
  7.4 284.3 %layer.1 = (bf16[2048,1024]{1,0:T(8,128)(2,1)}, bf16[2048,1024]{1,0:T(8,128)(2,1)}, f32[2,256,256]{2,1,0:T(8,128)}, f32[256,512]{1,0:T(8,128)}, f32[256,512]{1,0...) custom-call(f32[256,384]{1,0:T(8,128)} %in_full.1, f32[256,128]{1,0:T(8,128)} %out_full.1, ...), custom_call_target="tpu_custom_call" | custom-call | tf_op jit(solution)/shard_map/layer/pallas_call | solution.py:1423
  291.7 0.0 copy-start.3
  291.7 0.0 copy-start.2
  291.7 0.0 copy-start.11
  291.7 0.0 copy-start.12
  291.7 0.0 copy-start.14
  291.7 6.8 %convert_element_type.8 = f32[2048,1024]{1,0:T(8,128)} convert(bf16[2048,1024]{1,0:T(8,128)(2,1)} %get-tuple-element.36) | non-fusion elementwise | flops 2097152 | bytes 12582912 | tf_op jit(solution)/shard_map/convert_element_type | solution.py:1517
  298.5 0.0 copy-start.5
  298.5 0.0 copy-start.6
  298.5 0.0 copy-start.7
  298.5 0.0 copy-start.8
  298.5 0.0 copy-start.9
  298.5 0.0 copy-start.10
  298.6 1.3 slice.43
  300.6 0.0 copy-done.3
  300.7 0.0 copy-done.2
  300.7 0.0 copy-done.11
  300.7 0.0 copy-done.12
  300.7 1.3 multiply_subtract_fusion.2
  302.0 0.1 slice_bitcast_fusion.3
  302.2 0.0 copy-done.14
  302.2 0.0 copy-done.4
  302.2 0.0 copy-done.13
  302.2 0.0 copy-start.18
  302.2 0.0 copy-start.25
  302.2 0.0 copy-start.26
  302.2 0.0 copy-start.17
  302.2 0.0 copy-start.21
  302.2 0.0 copy-start.22
  302.3 0.0 copy-start.16
  302.3 0.0 copy-start.23
  302.3 0.0 copy-start.24
  302.3 0.0 copy-start.15
  302.3 0.0 copy-start.19
  302.3 0.0 copy-start.20
  302.3 0.9 multiply_subtract_fusion.3
  303.2 0.0 copy-done
  303.2 0.0 copy-done.1
  303.3 0.0 copy-done.5
  303.3 0.0 copy-done.6
  303.3 0.0 copy-done.7
  303.3 0.0 copy-done.8
  303.3 2.2 multiply_subtract_fusion
  305.5 0.8 fusion.20
  306.3 0.1 dynamic-slice_multiply_fusion.3
  306.4 0.0 copy-done.18
  306.4 0.6 multiply_subtract_fusion.7
  307.0 0.7 multiply_subtract_fusion.6
  307.7 1.3 multiply_subtract_fusion.5
  309.0 0.0 copy-done.19
  309.0 1.4 multiply_subtract_fusion.4
  310.4 4.6 %copy.63 = bf16[2048,1024]{1,0:T(8,128)(2,1)} copy(bf16[2048,1024]{1,0:T(8,128)(2,1)} %get-tuple-element.107) | data formatting | bytes 8388608
  (23 shorter events, 0.1 us)
Async XLA Ops:
  291.7 9.0 %copy-start.3 = (f32[2,256,256]{2,1,0:T(8,128)S(1)}, f32[2,256,256]{2,1,0:T(8,128)}, u32[]{:S(2)}) copy-start(f32[2,256,256]{2,1,0:T(8,128)} %get-tuple-element.38) | copy-start | bytes 1572868
  291.7 9.0 %copy-start.2 = (f32[256,384]{1,0:T(8,128)S(1)}, f32[256,384]{1,0:T(8,128)}, u32[]{:S(2)}) copy-start(f32[256,384]{1,0:T(8,128)} %in_full.1) | copy-start | bytes 1179652
  291.7 9.0 %copy-start.11 = (f32[256,384]{1,0:T(8,128)S(1)}, f32[256,384]{1,0:T(8,128)}, u32[]{:S(2)}) copy-start(f32[256,384]{1,0:T(8,128)} %param.33) | copy-start | bytes 1179652
  291.7 9.0 %copy-start.12 = (f32[256,384]{1,0:T(8,128)S(1)}, f32[256,384]{1,0:T(8,128)}, u32[]{:S(2)}) copy-start(f32[256,384]{1,0:T(8,128)} %param.34) | copy-start | bytes 1179652
  291.7 10.4 %copy-start.14 = (f32[256,128]{1,0:T(8,128)S(1)}, f32[256,128]{1,0:T(8,128)}, u32[]{:S(2)}) copy-start(f32[256,128]{1,0:T(8,128)} %param.37) | copy-start | bytes 393220
  298.5 3.7 %copy-start.4 = (f32[256,128]{1,0:T(8,128)S(1)}, f32[256,128]{1,0:T(8,128)}, u32[]{:S(2)}) copy-start(f32[256,128]{1,0:T(8,128)} %out_full.1) | copy-start | bytes 393220
  298.5 3.7 %copy-start.13 = (f32[256,128]{1,0:T(8,128)S(1)}, f32[256,128]{1,0:T(8,128)}, u32[]{:S(2)}) copy-start(f32[256,128]{1,0:T(8,128)} %param.36) | copy-start | bytes 393220
  298.5 4.8 %copy-start = (f32[256,512]{1,0:T(8,128)S(1)}, f32[256,512]{1,0:T(8,128)}, u32[]{:S(2)}) copy-start(f32[256,512]{1,0:T(8,128)} %up_full.1) | copy-start | bytes 1572868
  298.5 4.8 %copy-start.1 = (f32[256,512]{1,0:T(8,128)S(1)}, f32[256,512]{1,0:T(8,128)}, u32[]{:S(2)}) copy-start(f32[256,512]{1,0:T(8,128)} %down_full.1) | copy-start | bytes 1572868
  298.5 4.8 %copy-start.5 = (f32[256,512]{1,0:T(8,128)S(1)}, f32[256,512]{1,0:T(8,128)}, u32[]{:S(2)}) copy-start(f32[256,512]{1,0:T(8,128)} %param.42) | copy-start | bytes 1572868
  298.5 4.8 %copy-start.6 = (f32[256,512]{1,0:T(8,128)S(1)}, f32[256,512]{1,0:T(8,128)}, u32[]{:S(2)}) copy-start(f32[256,512]{1,0:T(8,128)} %param.43) | copy-start | bytes 1572868
  298.5 4.8 %copy-start.7 = (f32[256,512]{1,0:T(8,128)S(1)}, f32[256,512]{1,0:T(8,128)}, u32[]{:S(2)}) copy-start(f32[256,512]{1,0:T(8,128)} %param.40) | copy-start | bytes 1572868
  298.5 4.8 %copy-start.8 = (f32[256,512]{1,0:T(8,128)S(1)}, f32[256,512]{1,0:T(8,128)}, u32[]{:S(2)}) copy-start(f32[256,512]{1,0:T(8,128)} %param.39) | copy-start | bytes 1572868
  298.5 4.8 %copy-start.9 = (f32[256,512]{1,0:T(8,128)S(1)}, f32[256,512]{1,0:T(8,128)}, u32[]{:S(2)}) copy-start(f32[256,512]{1,0:T(8,128)} %get-tuple-element.39) | copy-start | bytes 1572868
  298.5 4.8 %copy-start.10 = (f32[256,512]{1,0:T(8,128)S(1)}, f32[256,512]{1,0:T(8,128)}, u32[]{:S(2)}) copy-start(f32[256,512]{1,0:T(8,128)} %get-tuple-element.40) | copy-start | bytes 1572868
  302.2 4.2 %copy-start.18 = (f32[32,2]{0,1:T(2,128)S(1)}, f32[32,2]{0,1:T(2,128)}, u32[]{:S(2)}) copy-start(f32[32,2]{0,1:T(2,128)} %param.44) | copy-start | bytes 772
  302.2 4.2 %copy-start.25 = (f32[32,2]{0,1:T(2,128)S(1)}, f32[32,2]{0,1:T(2,128)}, u32[]{:S(2)}) copy-start(f32[32,2]{0,1:T(2,128)} %param.45) | copy-start | bytes 772
  302.2 4.2 %copy-start.26 = (f32[32,2]{0,1:T(2,128)S(1)}, f32[32,2]{0,1:T(2,128)}, u32[]{:S(2)}) copy-start(f32[32,2]{0,1:T(2,128)} %param.46) | copy-start | bytes 772
  302.2 4.8 %copy-start.17 = (f32[32,4]{0,1:T(4,128)S(1)}, f32[32,4]{0,1:T(4,128)}, u32[]{:S(2)}) copy-start(f32[32,4]{0,1:T(4,128)} %param.47) | copy-start | bytes 1540
  302.2 4.8 %copy-start.21 = (f32[32,4]{0,1:T(4,128)S(1)}, f32[32,4]{0,1:T(4,128)}, u32[]{:S(2)}) copy-start(f32[32,4]{0,1:T(4,128)} %param.48) | copy-start | bytes 1540
  302.2 4.8 %copy-start.22 = (f32[32,4]{0,1:T(4,128)S(1)}, f32[32,4]{0,1:T(4,128)}, u32[]{:S(2)}) copy-start(f32[32,4]{0,1:T(4,128)} %param.49) | copy-start | bytes 1540
  302.3 5.5 %copy-start.16 = (f32[256,2]{0,1:T(2,128)S(1)}, f32[256,2]{0,1:T(2,128)}, u32[]{:S(2)}) copy-start(f32[256,2]{0,1:T(2,128)} %param.50) | copy-start | bytes 6148
  302.3 5.4 %copy-start.23 = (f32[256,2]{0,1:T(2,128)S(1)}, f32[256,2]{0,1:T(2,128)}, u32[]{:S(2)}) copy-start(f32[256,2]{0,1:T(2,128)} %param.51) | copy-start | bytes 6148
  302.3 5.4 %copy-start.24 = (f32[256,2]{0,1:T(2,128)S(1)}, f32[256,2]{0,1:T(2,128)}, u32[]{:S(2)}) copy-start(f32[256,2]{0,1:T(2,128)} %param.52) | copy-start | bytes 6148
  302.3 6.7 %copy-start.15 = (f32[256,4]{0,1:T(4,128)S(1)}, f32[256,4]{0,1:T(4,128)}, u32[]{:S(2)}) copy-start(f32[256,4]{0,1:T(4,128)} %param.53) | copy-start | bytes 12292
  302.3 6.7 %copy-start.19 = (f32[256,4]{0,1:T(4,128)S(1)}, f32[256,4]{0,1:T(4,128)}, u32[]{:S(2)}) copy-start(f32[256,4]{0,1:T(4,128)} %param.54) | copy-start | bytes 12292
  302.3 6.7 %copy-start.20 = (f32[256,4]{0,1:T(4,128)S(1)}, f32[256,4]{0,1:T(4,128)}, u32[]{:S(2)}) copy-start(f32[256,4]{0,1:T(4,128)} %param.55) | copy-start | bytes 12292
